TPU v7x, 32 devices: a whole 2x2x4 slice. The times are simulated.
32 devices in a mesh: row: 16 (over z, y, x), col: 2 (over core).
Axes of the slice: x: 2, y: 2, z: 4, core: 2. Of those that a mesh axis runs over, the one named last changes fastest.
Arguments:
- acts: bfloat16 [2048, 8192], P('row'), may hold values from -22 to 22
- out_grads: bfloat16 [2048, 4096], P('row', 'col'), may hold values from -0.198873782 to 0.198873782
- weight: float32 [8192, 4096], P('row', 'col'), may hold values from -30 to 30
- row_state: float32 [8192], P('row'), may hold values from 0.002 to 2
- col_state: float32 [4096], P('col'), may hold values from 0.01 to 0.3
Outputs:
- new_weight: float32 [8192, 4096], P('row', 'col')
- update: float32 [8192, 4096], P('row', 'col')
- row_moment: float32 [8192], P('row')
- col_moment: float32 [4096], P('col')
All inputs are finite; a program needn't handle non-finite values.
Results may differ from a plain program's by a relative error of at most 0.0003.
Values may be sent and summed in bfloat16 or wider, within the bound.
No kernel may reach another device: no remote copies, remote signals or barrier semaphores. Data moves between devices by JAX's collectives and lax.ppermute only.
A program may use at most 64 MiB of HBM per device.

v0:
```python
import jax
import jax.numpy as jnp
from jax import lax
from jax.sharding import PartitionSpec as P

decay_rate = 0.85
floor_eps = 1e-30
relative_rate = 0.05


def per_device(acts, out_grads, weight, row_state, col_state):
    n_col = lax.axis_size("col")
    width = acts.shape[1]
    cols_here = out_grads.shape[1]
    cols_all = cols_here * n_col
    columns = lax.all_to_all(acts, "row", split_axis=1, concat_axis=0, tiled=True)
    gradient = lax.dot_general(
        columns,
        lax.all_gather(out_grads, "row", axis=0, tiled=True),
        (((0,), (0,)), ((), ())),
        preferred_element_type=jnp.float32,
    )
    squares = gradient * gradient + floor_eps
    row_squares = jnp.sum(squares, axis=1)
    col_squares = jnp.sum(squares, axis=0)
    weight_part = jnp.sum(weight * weight)
    row_total = lax.psum(row_squares, "col")
    col_total = lax.psum(col_squares, "row")
    weight_total = lax.psum(weight_part, ("row", "col"))
    row_moment = decay_rate * row_state + (1.0 - decay_rate) * (row_total / cols_all)
    col_moment = decay_rate * col_state + (1.0 - decay_rate) * (col_total / width)
    unclipped = gradient * lax.rsqrt(row_moment[:, None] * col_moment[None, :])
    update_total = lax.psum(jnp.sum(unclipped * unclipped), ("row", "col"))
    count_all = width * cols_all
    clip_factor = jnp.maximum(1.0, jnp.sqrt(update_total / count_all))
    update = unclipped / clip_factor
    step_size = relative_rate * jnp.sqrt(weight_total / count_all + 1e-06)
    new_weight = weight - step_size * update
    return (new_weight, update, row_moment, col_moment)


def solution(mesh):
    return jax.shard_map(
        per_device,
        mesh=mesh,
        in_specs=(P("row", None), P("row", "col"), P("row", "col"), P("row"), P("col")),
        out_specs=(P("row", "col"), P("row", "col"), P("row"), P("col")),
        check_vma=False,
    )
```

profile of v0, /device:TPU:12, one launch (start us, length us, event | category | flops | bytes accessed | tf_op | source)
XLA Modules:
  0.0 269.7 jit_solution(2994545322753481755)
XLA Ops:
  7.2 0.0 all-gather.2.cloned.1.call-start
  7.2 0.7 all-gather.2.cloned.1.call-update
  7.9 4.1 %copy.9 = bf16[128,8192]{0,1:T(8,128)(2,1)} copy(bf16[128,8192]{1,0:T(8,128)(2,1)} %param.5) | data formatting | bytes 4194304 | tf_op args[0]
  12.0 7.2 %all-to-all-start = ((bf16[128,16,512]{0,2,1:T(8,128)(2,1)}), bf16[128,16,512]{0,2,1:T(8,128)(2,1)S(1)}, u32[]{:S(2)}, u32[]{:S(2)}) async-start(bf16[128,16,512]{0,2,1:T(8,128)(2,1)} %bitcast.6), calls=%async_computation | async-start | bytes 4194304 | tf_op jit(solution)/shard_map/all_to_all | solution.py:16
  19.1 4.1 %multiply_reduce_fusion.1 = f32[]{:T(128)} fusion(f32[512,2048]{1,0:T(8,128)} %param.7), kind=kLoop, calls=%fused_computation.4 | loop fusion | flops 2097151 | bytes 4194308 | tf_op jit(solution)/shard_map/reduce_sum | solution.py:26
  23.3 77.5 %all-to-all-done = bf16[128,16,512]{0,2,1:T(8,128)(2,1)S(1)} async-done(((bf16[128,16,512]{0,2,1:T(8,128)(2,1)}), bf16[128,16,512]{0,2,1:T(8,128)(2,1)S(1)}, u32[]{:S(2)}, u32[]{:S(2)}) %all-to-all-start) | async-done | bytes 2097184 | tf_op jit(solution)/shard_map/all_to_all | solution.py:16
  100.7 2.6 copy.10
  103.3 52.0 %all-gather.2.cloned.1.call-done = bf16[2048,2048]{1,0:T(8,128)(2,1)} async-done(((bf16[128,2048]{1,0:T(8,128)(2,1)}), bf16[2048,2048]{1,0:T(8,128)(2,1)}) %all-gather.2.cloned.1.call-update) | async-done | bytes 8388624 | tf_op jit(solution)/shard_map/all_gather | solution.py:19
  155.4 0.0 copy-start.2
  155.4 0.0 copy-start.3
  155.4 10.9 %fusion.1 = (f32[512]{0:T(512)S(1)}, f32[2048]{0:T(1024)S(1)}, f32[512,2048]{1,0:T(8,128)}) fusion(bf16[2048,512]{1,0:T(8,128)(2,1)} %bitcast.7, bf16[2048,2048]{1,0:T(8,128)(2,1)} %all-gather.2.cloned.1.call-done), kind=kOutput, calls=%fused_computation.6 | convolution fusion | flops 4299159040 | bytes 14690304 | tf_op jit(solution)/shard_map/dot_general | solution.py:17
  166.3 30.4 %psum.30 = f32[2048]{0:T(1024)S(1)} all-reduce(f32[2048]{0:T(1024)S(1)} %get-tuple-element.5), channel_id=1, replica_groups=mesh['row'=16,'col'=2] {'row'}, use_global_device_ids=true, to_apply=%region_5.0 | all-reduce | flops 2048 | bytes 16384 | tf_op jit(solution)/shard_map/psum | solution.py:28
  196.7 2.5 psum.29
  199.2 0.0 copy-done.2
  199.2 0.0 copy-done.3
  199.2 0.0 copy-start
  199.2 0.0 copy-start.1
  199.2 4.1 %multiply_reduce_fusion = f32[]{:T(128)} fusion(f32[512,2048]{1,0:T(8,128)} %get-tuple-element.10, f32[2048]{0:T(1024)S(1)} %multiply_add_fusion.1, f32[512]{0:T(512)S(1)} %multiply_add_fusion.2), kind=kLoop, calls=%fused_computation.1 | loop fusion | flops 4194303 | bytes 4204548 | tf_op jit(solution)/shard_map/reduce_sum | solution.py:33
  203.3 49.3 %all-reduce = (f32[]{:T(128)}, f32[]{:T(128)}) all-reduce(f32[]{:T(128)} %multiply_reduce_fusion, f32[]{:T(128)} %multiply_reduce_fusion.1), channel_id=1, replica_groups=mesh['row'=16,'col'=2] {'row','col'}, use_global_device_ids=true, to_apply=%region_7.0 | all-reduce | flops 2 | bytes 16 | tf_op jit(solution)/shard_map/psum | solution.py:33
  253.9 8.9 %multiply_subtract_fusion = (f32[512,2048]{1,0:T(8,128)}, f32[512,2048]{1,0:T(8,128)}) fusion(f32[512,2048]{1,0:T(8,128)} %param.7, f32[]{:T(128)S(6)} %mul_shard_map.3, f32[]{:T(128)S(6)} %max_shard_map.3, f32[512,2048]{1,0:T(8,128)} %get-tuple-element.10, f32[2048]{0:T(1024)S(1)} %multiply_add_fusion.1, f32[512]{0:T(512)S(1)} %multiply_add_fusion.2), kind=kLoop, calls=%fused_computation | loop fusion | flops 5242880 | bytes 16787464 | tf_op jit(solution)/shard_map/sub | solution.py:38
  262.9 0.0 copy-done
  262.9 0.0 copy-done.1
  (2 shorter events, 0.0 us)
Async XLA Ops:
  7.2 148.2 %all-gather.2.cloned.1.call-start = ((), (), s32[]{:S(2)}) async-start(), calls=%async_computation.1 | async-start | bytes 8912896 | tf_op jit(solution)/shard_map/all_gather | solution.py:19
  12.0 88.8 %all-to-all-start = ((bf16[128,16,512]{0,2,1:T(8,128)(2,1)}), bf16[128,16,512]{0,2,1:T(8,128)(2,1)S(1)}, u32[]{:S(2)}, u32[]{:S(2)}) async-start(bf16[128,16,512]{0,2,1:T(8,128)(2,1)} %bitcast.6), calls=%async_computation | async-start | bytes 4194304 | tf_op jit(solution)/shard_map/all_to_all | solution.py:16
  155.4 43.8 %copy-start.2 = (f32[2048]{0:T(1024)S(1)}, f32[2048]{0:T(1024)}, u32[]{:S(2)}) copy-start(f32[2048]{0:T(1024)} %param.9) | copy-start | bytes 24580
  155.4 43.8 %copy-start.3 = (f32[512]{0:T(512)S(1)}, f32[512]{0:T(512)}, u32[]{:S(2)}) copy-start(f32[512]{0:T(512)} %param.8) | copy-start | bytes 6148
  199.2 63.7 %copy-start = (f32[2048]{0:T(1024)}, f32[2048]{0:T(1024)S(1)}, u32[]{:S(2)}) copy-start(f32[2048]{0:T(1024)S(1)} %multiply_add_fusion.1) | copy-start | bytes 24580
  199.2 63.6 %copy-start.1 = (f32[512]{0:T(512)}, f32[512]{0:T(512)S(1)}, u32[]{:S(2)}) copy-start(f32[512]{0:T(512)S(1)} %multiply_add_fusion.2) | copy-start | bytes 6148
Sparse Core Ops, SparseCore 0:
  10.7 144.5 all-gather.1
where the time goes:
time: 270 us
  waiting for transfers between devices  130 us (48%)
  blocking collectives  82.2 us (30%)
  other arithmetic  17.1 us (6%)
  between operations  15.4 us (6%)
  matrix products  10.9 us (4%)
  starting transfers between devices  7.21 us (3%)
  local copies, waits for them, and re-layouts  6.67 us (2%)
    all_to_all x1, waiting for transfers between devices, per_device(): lax.all_to_all(acts, 'row', split_axis=1, concat_axis=0, tiled=True)  77.5 us
    all_gather x1, waiting for transfers between devices, per_device(): lax.all_gather(out_grads, 'row', axis=0, tiled=True)  52 us
    psum x1, blocking collectives, per_device(): update_total = lax.psum(jnp.sum(unclipped * unclipped), ('row', 'col'))  49.3 us
    psum x1, blocking collectives, per_device(): col_total = lax.psum(col_squares, 'row')  30.4 us
    dot_general x1, matrix products, per_device(): lax.dot_general(columns, lax.all_gather(out_grads, 'row', axis=0, tiled=T...  10.9 us
    sub x1, other arithmetic, per_device(): new_weight = weight - step_size * update  8.93 us
    all_to_all x1, starting transfers between devices, per_device(): lax.all_to_all(acts, 'row', split_axis=1, concat_axis=0, tiled=True)  7.17 us
  transfers between devices with their start and end apart: 2, of which 2 were waited for; matrix products, arithmetic and copies ran while one was open for 4% of the time, Pallas kernels for 0%

commit v1 on v0

v1 whole, which is shorter than its diff:
```python
import functools

import jax
import jax.numpy as jnp
from jax import lax
from jax.experimental import pallas as pl
from jax.experimental.pallas import tpu as pltpu
from jax.sharding import PartitionSpec as P

decay_rate = 0.85
floor_eps = 1e-30
relative_rate = 0.05
LANES = 128


def spans(offsets):
    out = [0]
    for offset in offsets:
        out = out + [offset ^ s for s in out]
    return out


def butterfly(value, axis, offsets):
    n = lax.axis_size(axis)
    terms = [value] + [lax.ppermute(value, axis, [(i, i ^ s) for i in range(n)]) for s in spans(offsets)[1:]]
    while len(terms) > 1:
        terms = [a + b for a, b in zip(terms[::2], terms[1::2])]
    return terms[0]


def powers(first, end):
    out = []
    while first < end:
        out.append(first)
        first *= 2
    return out


def placed(space, arrays):
    return [pltpu.with_memory_space_constraint(a, space) for a in arrays]


def in_vmem(*arrays):
    return placed(pltpu.VMEM, arrays)


WHOLE = pl.BlockSpec(memory_space=pltpu.VMEM)
SCALARS = pl.BlockSpec(memory_space=pltpu.SMEM)


def pack_kernel(side_ref, acts_ref, out_ref):
    _, _, width = out_ref.shape
    low = side_ref[0] == 0
    for d in range(out_ref.shape[0]):
        at = 2 * d * width
        a, b = acts_ref[:, at : at + width], acts_ref[:, at + width : at + 2 * width]
        out_ref[d] = jnp.where(low, a, b)


def pack(side, acts, n_row):
    tokens, width = acts.shape
    return pl.pallas_call(
        pack_kernel,
        out_shape=jax.ShapeDtypeStruct((n_row, tokens, width // (2 * n_row)), acts.dtype),
        in_specs=[SCALARS, WHOLE],
        out_specs=WHOLE,
        compiler_params=pltpu.CompilerParams(vmem_limit_bytes=12 << 20),
        cost_estimate=pl.CostEstimate(flops=0, bytes_accessed=3 * acts.size, transcendentals=0),
        name="pack",
    )(side, acts)


def arrange_kernel(index_ref, blocks_ref, out_ref):
    n_row, tokens, _ = blocks_ref.shape
    for s in range(n_row):
        out_ref[:, s * tokens : (s + 1) * tokens] = blocks_ref[index_ref[s]].T


def arrange(index, blocks):
    n_row, tokens, rows = blocks.shape
    return pl.pallas_call(
        arrange_kernel,
        out_shape=pltpu.VMEM((rows, n_row * tokens), blocks.dtype),
        in_specs=[SCALARS, WHOLE],
        out_specs=WHOLE,
        compiler_params=pltpu.CompilerParams(vmem_limit_bytes=12 << 20),
        cost_estimate=pl.CostEstimate(flops=0, bytes_accessed=8 * blocks.size, transcendentals=0),
        name="arrange",
    )(index, *in_vmem(blocks))


def fill(slab, pieces, lanes):
    at = 0
    for piece in pieces:
        slab[at : at + piece.shape[0], :] = piece[:, lanes]
        at += piece.shape[0]


def gemm_kernel(side_ref, mine_ref, other_ref, *refs):
    *pieces, out_ref, slab = refs
    depth = slab.shape[0]
    height = mine_ref.shape[0]
    fill(slab, pieces, slice(None))
    for at, columns_ref in ((side_ref[0], mine_ref), (1 - side_ref[0], other_ref)):
        rows = pl.ds(pl.multiple_of(at * height, height), height)
        out_ref[rows, :] = jnp.dot(columns_ref[:, :depth], slab[...], preferred_element_type=jnp.float32)


def gemm(side, mine, other, pieces):
    rows = 2 * mine.shape[0]
    depth = sum(p.shape[0] for p in pieces)
    cols = pieces[0].shape[1]
    width = min(512, cols)
    return pl.pallas_call(
        gemm_kernel,
        grid=(cols // width,),
        out_shape=jax.ShapeDtypeStruct((rows, cols), jnp.float32),
        in_specs=[SCALARS, WHOLE, WHOLE] + [pl.BlockSpec((p.shape[0], width), lambda j: (0, j)) for p in pieces],
        out_specs=pl.BlockSpec((rows, width), lambda j: (0, j)),
        scratch_shapes=[pltpu.VMEM((depth, width), jnp.bfloat16)],
        compiler_params=pltpu.CompilerParams(vmem_limit_bytes=24 << 20),
        cost_estimate=pl.CostEstimate(flops=2 * rows * depth * cols, bytes_accessed=2 * depth * cols, transcendentals=0),
        name="gemm",
    )(side, *in_vmem(mine, other), *placed(pltpu.HBM, pieces))


def last_kernel(side_ref, mine_ref, other_ref, before_ref, *refs):
    *pieces, out_ref, rows_ref, slab, sums = refs
    depth, width = slab.shape
    height = mine_ref.shape[0]
    first = mine_ref.shape[1] - depth
    cols = out_ref.shape[1]
    side = side_ref[0]
    for t in range(0, cols, width):
        lanes = slice(t, t + width)
        fill(slab, pieces, lanes)
        for at, columns_ref in ((side, mine_ref), (1 - side, other_ref)):
            rows = pl.ds(pl.multiple_of(at * height, height), height)
            total = before_ref[rows, lanes] + jnp.dot(
                columns_ref[:, first:], slab[...], preferred_element_type=jnp.float32
            )
            out_ref[rows, lanes] = total
            squares = total * total + floor_eps
            part = squares[:, :LANES]
            for u in range(LANES, width, LANES):
                part = part + squares[:, u : u + LANES]
            sums[rows, :] = part if t == 0 else sums[rows, :] + part
    rows_ref[...] = jnp.sum(sums[...].T, axis=0, keepdims=True)


def last_gemm(side, mine, other, before, pieces):
    rows, cols = before.shape
    depth = sum(p.shape[0] for p in pieces)
    return pl.pallas_call(
        last_kernel,
        out_shape=[pltpu.VMEM((rows, cols), jnp.float32), pltpu.VMEM((1, rows), jnp.float32)],
        in_specs=[SCALARS] + [WHOLE] * (3 + len(pieces)),
        out_specs=[WHOLE, WHOLE],
        scratch_shapes=[pltpu.VMEM((depth, min(512, cols)), jnp.bfloat16), pltpu.VMEM((rows, LANES), jnp.float32)],
        compiler_params=pltpu.CompilerParams(vmem_limit_bytes=24 << 20),
        cost_estimate=pl.CostEstimate(flops=2 * rows * depth * cols, bytes_accessed=2 * depth * cols, transcendentals=0),
        name="last_gemm",
    )(side, *in_vmem(mine, other, before), *pieces)


def moments_kernel(height, totals_ref, state_ref, col_ref, sums_ref):
    col = decay_rate * state_ref[...] + (1.0 - decay_rate) * (totals_ref[0:1, :] / height)
    col_ref[...] = col
    clip = jnp.sum(totals_ref[1:2, :] / col)
    weight = jnp.sum(totals_ref[2:3, :])
    row = lax.broadcasted_iota(jnp.int32, sums_ref.shape, 0)
    sums_ref[...] = jnp.where(row == 0, clip, weight)


def moments(height, totals, col_state):
    cols = col_state.shape[0]
    whole = pl.BlockSpec(memory_space=pltpu.VMEM)
    return pl.pallas_call(
        functools.partial(moments_kernel, height),
        out_shape=[pltpu.VMEM((1, cols), jnp.float32), pltpu.VMEM((8, LANES), jnp.float32)],
        in_specs=[whole, whole],
        out_specs=[whole, whole],
        compiler_params=pltpu.CompilerParams(vmem_limit_bytes=8 << 20),
        name="moments",
    )(totals, col_state[None, :])


def finish_kernel(count_all, sums_ref, row_ref, col_ref, gradient_ref, weight_ref, new_hbm, update_hbm, new, update, rows, cols, sems):
    clip = jnp.maximum(1.0, jnp.sqrt(sums_ref[0:1, :] / count_all))
    step_size = relative_rate * jnp.sqrt(sums_ref[1:2, :] / count_all + 1e-06)
    root = lax.rsqrt(row_ref[...])
    rows[...] = jnp.broadcast_to(root, (LANES, root.shape[1])).T
    for t in range(0, cols.shape[1], LANES):
        cols[:, t : t + LANES] = lax.rsqrt(col_ref[:, t : t + LANES]) / clip
    height = min(64, rows.shape[0])
    copies = []
    for i in range(rows.shape[0] // height):
        here = slice(i * height, (i + 1) * height)
        scale = rows[here, :]
        for t in range(0, cols.shape[1], LANES):
            lanes = slice(t, t + LANES)
            value = gradient_ref[here, lanes] * scale * cols[:, lanes]
            update[here, lanes] = value
            new[here, lanes] = weight_ref[here, lanes] - step_size * value
        for j, (source, target) in enumerate(((update, update_hbm), (new, new_hbm))):
            copies.append(pltpu.make_async_copy(source.at[here], target.at[here], sems.at[2 * i + j]))
            copies[-1].start()
    for copy in copies:
        copy.wait()


def finish(count_all, sums, row_moment, col_moment, gradient, weight):
    rows, cols = gradient.shape
    out = pltpu.HBM((rows, cols), jnp.float32)
    there = pl.BlockSpec(memory_space=pl.ANY)
    return pl.pallas_call(
        functools.partial(finish_kernel, count_all),
        out_shape=[out, out],
        in_specs=[WHOLE] * 5,
        out_specs=[there, there],
        scratch_shapes=[
            pltpu.VMEM((rows, cols), jnp.float32),
            pltpu.VMEM((rows, cols), jnp.float32),
            pltpu.VMEM((rows, LANES), jnp.float32),
            pltpu.VMEM((1, cols), jnp.float32),
            pltpu.SemaphoreType.DMA((2 * pl.cdiv(rows, min(64, rows)),)),
        ],
        compiler_params=pltpu.CompilerParams(vmem_limit_bytes=20 << 20),
        cost_estimate=pl.CostEstimate(flops=4 * rows * cols, bytes_accessed=16 * rows * cols, transcendentals=0),
        name="finish",
    )(*in_vmem(sums, row_moment[None, :], col_moment, gradient, weight))


def per_device(acts, out_grads, weight, row_state, col_state):
    n_row = lax.axis_size("row")
    n_col = lax.axis_size("col")
    depth = n_row // 4
    width = acts.shape[1]
    tokens = acts.shape[0]
    half, quarter = tokens // 2, tokens // 4
    cols_all = out_grads.shape[1] * n_col
    count_all = width * cols_all
    me = lax.axis_index("row")
    side = lax.axis_index("col") % 2

    def swap(v, bit):
        return lax.ppermute(v, "row", [(i, i ^ bit) for i in range(n_row)])

    def along_z(by, v):
        return lax.ppermute(v, "row", [(i, (i + 4 * by) % n_row) for i in range(n_row)])

    own, pieces = {0: out_grads}, {}
    by_x, by_y = swap(out_grads, 1), swap(out_grads, 2)
    top = swap(by_x[:half], 2)
    pieces[0] = [own[0], by_x, by_y, top, swap(by_y[half:], 1)]
    for k in planes_of(depth):
        by = 1 if 2 * k <= depth else -1
        before = (k - by) % depth
        own[k] = along_z(by, own[before])
        by_x, by_y = swap(own[k], 1), swap(own[k], 2)
        if before == 0:
            far, cut = [along_z(by, top)], half + quarter
            q1, q2 = by_x[half:cut], by_y[cut:]
        else:
            far, q1, q2 = [], by_x[:half], by_y[half:]
        pieces[k] = [own[k], by_x, by_y] + far + [swap(q1, 2), swap(q2, 1)]

    side = side[None]
    blocks = pack(side, acts, n_row)
    blocks = lax.all_to_all(blocks, "row", 0, 0, tiled=True)
    *sooner, last = planes = [0] + planes_of(depth)
    early = [(k, 0) for k in planes] + [(k, j) for k in sooner for j in (1, 2)] + [(0, 3), (last, 1), (last, 2)]
    late = [(k, 3) for k in planes[1:]]
    below = jnp.array([(-k % depth) * 4 for k, _ in early + late], jnp.int32)
    place = jnp.array([j for _, j in early + late], jnp.int32)
    mine = arrange((me - me % 4 + below) % n_row + ((me % 4) ^ place), blocks)
    other = lax.ppermute(mine, "col", [(i, i ^ 1) for i in range(n_col)])
    of = lambda shards: [p for k, j in shards for p in (pieces[k][3:] if j == 3 else [pieces[k][j]])]
    near, far = of(early), of(late)
    gradient, row_squares = last_gemm(side, mine, other, gemm(side, mine, other, near), far)

    row_total = butterfly(row_squares[0], "col", powers(1, n_col))
    row_moment = decay_rate * row_state + (1.0 - decay_rate) * (row_total / cols_all)
    squares = gradient * gradient
    parts = jnp.stack(
        [
            jnp.sum(squares + floor_eps, axis=0),
            jnp.sum(squares * (1.0 / row_moment)[:, None], axis=0),
            jnp.sum(weight * weight, axis=0),
        ]
    )
    totals = parts
    for bit in powers(1, n_row):
        totals = butterfly(totals, "row", [bit])
    col_moment, sums = moments(width, totals, col_state)
    sums = butterfly(sums, "col", powers(1, n_col))
    new_weight, update = finish(count_all, sums, row_moment, col_moment, gradient, weight)
    return (new_weight, update, row_moment, col_moment[0])


def planes_of(depth):
    return [k for i in range(1, depth // 2) for k in (i, depth - i)] + [depth // 2]


def solution(mesh):
    return jax.shard_map(
        per_device,
        mesh=mesh,
        in_specs=(P("row", None), P("row", "col"), P("row", "col"), P("row"), P("col")),
        out_specs=(P("row", "col"), P("row", "col"), P("row"), P("col")),
        check_vma=False,
    )
```

time: 270 us -> 147 us (0.54)
  blocking collectives: 82.2 us -> 0 us
  waiting for transfers between devices: 130 us -> 94.2 us
  starting transfers between devices: 7.21 us -> 30.7 us
  other arithmetic: 17.1 us -> 1.22 us
  between operations: 15.4 us -> 1.03 us
  Pallas kernels: 0 us -> 14 us
  matrix products: 10.9 us -> 0 us
  local copies, waits for them, and re-layouts: 6.67 us -> 3.65 us
    ppermute x0 -> x28, waiting for transfers between devices: none -> 94.2 us  [the longest x5 49 us: along_z(): lax.ppermute(v, 'row', [(i, (i + 4 * by) % n_row) for i in range(n_row)])]
    psum x3 -> x0, blocking collectives: 82.2 us -> none  [the longest x1 49.3 us: per_device(): update_total = lax.psum(jnp.sum(unclipped * unclipped), ('row', 'col'))]
    all_to_all x1, waiting for transfers between devices: 77.5 us -> 0.01 us  [per_device(): blocks = lax.all_to_all(blocks, 'row', 0, 0, tiled=True)]
    all_gather x1 -> x0, waiting for transfers between devices: 52 us -> none  [per_device(): lax.all_gather(out_grads, 'row', axis=0, tiled=True)]
    ppermute x0 -> x28, starting transfers between devices: none -> 23.6 us  [the longest x16 16.5 us: swap(): return lax.ppermute(v, 'row', [(i, i ^ bit) for i in range(n_row)])]
    pallas_call x0 -> x6, Pallas kernels: none -> 14 us  [the longest x1 6.69 us: gemm(): pl.pallas_call(gemm_kernel, grid=(cols // width,), out_shape=jax.ShapeDty...]
    dot_general x1 -> x0, matrix products: 10.9 us -> none  [per_device(): lax.dot_general(columns, lax.all_gather(out_grads, 'row', axis=0, tiled=T...]
    sub x1 -> x0, other arithmetic: 8.93 us -> none  [per_device(): new_weight = weight - step_size * update]
  transfers between devices with their start and end apart: 2 -> 29, of which waited for: 2 -> 14; matrix products, arithmetic and copies ran while one was open for 4% -> 1% of each run, Pallas kernels for 0% -> 5%
where the time goes in v1:
time: 147 us; the launch traced here: 145 us
  waiting for transfers between devices  94.2 us (64%)
  starting transfers between devices  30.7 us (21%)
  Pallas kernels  14 us (10%)
  local copies, waits for them, and re-layouts  3.65 us (2%)
    ppermute x5, waiting for transfers between devices, along_z(): lax.ppermute(v, 'row', [(i, (i + 4 * by) % n_row) for i in range(n_row)])  49 us
    ppermute x16, waiting for transfers between devices, swap(): return lax.ppermute(v, 'row', [(i, i ^ bit) for i in range(n_row)])  29.5 us
    ppermute x16, starting transfers between devices, swap(): return lax.ppermute(v, 'row', [(i, i ^ bit) for i in range(n_row)])  16.5 us
    ppermute x6, waiting for transfers between devices, butterfly(): lax.ppermute(value, axis, [(i, i ^ s) for i in range(n)])  15.8 us
    all_to_all x1, starting transfers between devices, per_device(): blocks = lax.all_to_all(blocks, 'row', 0, 0, tiled=True)  7.17 us
    pallas_call x1, Pallas kernels, gemm(): pl.pallas_call(gemm_kernel, grid=(cols // width,), out_shape=jax.ShapeDty...  6.69 us
    ppermute x5, starting transfers between devices, along_z(): lax.ppermute(v, 'row', [(i, (i + 4 * by) % n_row) for i in range(n_row)])  4.98 us
    pallas_call x1, Pallas kernels, finish(): pl.pallas_call(functools.partial(finish_kernel, count_all), out_shape=[ou...  3.69 us
  transfers between devices with their start and end apart: 29, of which 14 were waited for; matrix products, arithmetic and copies ran while one was open for 1% of the time, Pallas kernels for 5%

profile of v1, /device:TPU:12, one launch (start us, length us, event | category | flops | bytes accessed | tf_op | source)
XLA Modules:
  0.0 144.9 jit_solution(12460873008990224097)
XLA Ops:
  0.7 1.6 %copy-done.1 = bf16[128,8192]{1,0:T(8,128)(2,1)S(1)} copy-done((bf16[128,8192]{1,0:T(8,128)(2,1)S(1)}, bf16[128,8192]{1,0:T(8,128)(2,1)}, u32[]{:S(2)}) %copy-start.1) | copy-done | bytes 2097176
  2.3 1.1 pack.1
  3.3 7.2 %all-to-all-start = ((bf16[16,128,256]{2,1,0:T(8,128)(2,1)}), bf16[16,128,256]{2,1,0:T(8,128)(2,1)S(1)}, u32[]{:S(2)}, u32[]{:S(2)}) async-start(bf16[16,128,256]{2,1,0:T(8,128)(2,1)} %pack.1), calls=%async_computation | async-start | bytes 2097152 | tf_op jit(solution)/shard_map/all_to_all | solution.py:270
  10.5 1.5 %collective-permute-start.1 = (bf16[128,2048]{1,0:T(8,128)(2,1)}, bf16[128,2048]{1,0:T(8,128)(2,1)}, u32[]{:S(2)}, u32[]{:S(2)}) collective-permute-start(bf16[128,2048]{1,0:T(8,128)(2,1)} %refs_0_.1), channel_id=1, source_target_pairs={{0,8},{2,10},{4,12},{6,14},{8,16},{10,18},{12,20},{14,22},{16,24},... | collective-permute-start | bytes 1572872 | tf_op jit(solution)/shard_map/ppermute | solution.py:250
  12.0 1.5 %collective-permute-start.4 = (bf16[128,2048]{1,0:T(8,128)(2,1)}, bf16[128,2048]{1,0:T(8,128)(2,1)S(1)}, u32[]{:S(2)}, u32[]{:S(2)}) collective-permute-start(bf16[128,2048]{1,0:T(8,128)(2,1)} %refs_0_.1), channel_id=1, source_target_pairs={{0,2},{2,0},{4,6},{6,4},{8,10},{10,8},{12,14},{14,12},{16,18},{18,... | collective-permute-start | bytes 1572872 | tf_op jit(solution)/shard_map/ppermute | solution.py:247
  13.4 0.6 collective-permute-start.2
  14.0 0.6 collective-permute-start.5
  14.6 40.9 %collective-permute-done.1.refs_1_ = bf16[128,2048]{1,0:T(8,128)(2,1)} collective-permute-done((bf16[128,2048]{1,0:T(8,128)(2,1)}, bf16[128,2048]{1,0:T(8,128)(2,1)}, u32[]{:S(2)}, u32[]{:S(2)}) %collective-permute-start.1) | collective-permute-done | bytes 524320 | tf_op jit(solution)/shard_map/ppermute | solution.py:250
  55.5 2.5 %collective-permute-start.3 = (bf16[128,2048]{1,0:T(8,128)(2,1)}, bf16[128,2048]{1,0:T(8,128)(2,1)}, u32[]{:S(2)}, u32[]{:S(2)}) collective-permute-start(bf16[128,2048]{1,0:T(8,128)(2,1)} %collective-permute-done.1.refs_1_), channel_id=1, source_target_pairs={{0,8},{2,10},{4,12},{6,14},{8,16},{10,18},{12,20},{14,22},{16,24},... | collective-permute-start | bytes 1572872 | tf_op jit(solution)/shard_map/ppermute | solution.py:250
  57.9 1.5 %collective-permute-start.6 = (bf16[128,2048]{1,0:T(8,128)(2,1)}, bf16[128,2048]{1,0:T(8,128)(2,1)S(1)}, u32[]{:S(2)}, u32[]{:S(2)}) collective-permute-start(bf16[128,2048]{1,0:T(8,128)(2,1)} %collective-permute-done.1.refs_1_), channel_id=1, source_target_pairs={{0,2},{2,0},{4,6},{6,4},{8,10},{10,8},{12,14},{14,12},{16,18},{18,... | collective-permute-start | bytes 1572872 | tf_op jit(solution)/shard_map/ppermute | solution.py:247
  59.4 0.8 slice.32
  60.2 0.5 collective-permute-start.10
  60.7 8.1 %collective-permute-done.2.refs_2_ = bf16[128,2048]{1,0:T(8,128)(2,1)} collective-permute-done((bf16[128,2048]{1,0:T(8,128)(2,1)}, bf16[128,2048]{1,0:T(8,128)(2,1)}, u32[]{:S(2)}, u32[]{:S(2)}) %collective-permute-start.2) | collective-permute-done | bytes 524320 | tf_op jit(solution)/shard_map/ppermute | solution.py:250
  68.7 0.4 collective-permute-start.7
  69.2 0.9 arrange.1.mine_ref
  70.2 1.5 %collective-permute-start.8 = (bf16[128,2048]{1,0:T(8,128)(2,1)}, bf16[128,2048]{1,0:T(8,128)(2,1)S(1)}, u32[]{:S(2)}, u32[]{:S(2)}) collective-permute-start(bf16[128,2048]{1,0:T(8,128)(2,1)} %collective-permute-done.2.refs_2_), channel_id=1, source_target_pairs={{0,2},{2,0},{4,6},{6,4},{8,10},{10,8},{12,14},{14,12},{16,18},{18,... | collective-permute-start | bytes 1572872 | tf_op jit(solution)/shard_map/ppermute | solution.py:247
  71.8 1.6 %collective-permute-start.9 = (bf16[128,2048]{1,0:T(8,128)(2,1)}, bf16[128,2048]{1,0:T(8,128)(2,1)S(1)}, u32[]{:S(2)}, u32[]{:S(2)}) collective-permute-start(bf16[128,2048]{1,0:T(8,128)(2,1)} %collective-permute-done.2.refs_2_), channel_id=1, source_target_pairs={{0,4},{2,6},{4,0},{6,2},{8,12},{10,14},{12,8},{14,10},{16,20},{18,... | collective-permute-start | bytes 1572872 | tf_op jit(solution)/shard_map/ppermute | solution.py:247
  73.4 0.6 collective-permute-start.12
  73.9 9.8 %collective-permute-done.7.refs_7_ = bf16[128,2048]{1,0:T(8,128)(2,1)S(1)} collective-permute-done((bf16[128,2048]{1,0:T(8,128)(2,1)}, bf16[128,2048]{1,0:T(8,128)(2,1)S(1)}, u32[]{:S(2)}, u32[]{:S(2)}) %collective-permute-start.7) | collective-permute-done | bytes 524320 | tf_op jit(solution)/shard_map/ppermute | solution.py:247
  83.8 0.4 collective-permute-start.13
  84.2 1.1 collective-permute-done.8.refs_8_
  85.3 1.5 %collective-permute-start.11 = (bf16[64,2048]{1,0:T(8,128)(2,1)S(1)}, bf16[64,2048]{1,0:T(8,128)(2,1)S(1)}, u32[]{:S(2)}, u32[]{:S(2)}) collective-permute-start(bf16[64,2048]{1,0:T(8,128)(2,1)S(1)} %slice.33), channel_id=1, source_target_pairs={{0,2},{2,0},{4,6},{6,4},{8,10},{10,8},{12,14},{14,12},{16,18},{18,... | collective-permute-start | bytes 786440 | tf_op jit(solution)/shard_map/ppermute | solution.py:247
  86.8 8.2 %collective-permute-done.9.refs_9_ = bf16[128,2048]{1,0:T(8,128)(2,1)S(1)} collective-permute-done((bf16[128,2048]{1,0:T(8,128)(2,1)}, bf16[128,2048]{1,0:T(8,128)(2,1)S(1)}, u32[]{:S(2)}, u32[]{:S(2)}) %collective-permute-start.9) | collective-permute-done | bytes 524320 | tf_op jit(solution)/shard_map/ppermute | solution.py:247
  95.0 1.6 %collective-permute-done.12.refs_12_ = bf16[128,2048]{1,0:T(8,128)(2,1)S(1)} collective-permute-done((bf16[128,2048]{1,0:T(8,128)(2,1)}, bf16[128,2048]{1,0:T(8,128)(2,1)S(1)}, u32[]{:S(2)}, u32[]{:S(2)}) %collective-permute-start.12) | collective-permute-done | bytes 524320 | tf_op jit(solution)/shard_map/ppermute | solution.py:247
  96.5 0.5 collective-permute-start.17
  97.0 7.3 %collective-permute-done.13.refs_13_ = bf16[128,2048]{1,0:T(8,128)(2,1)S(1)} collective-permute-done((bf16[128,2048]{1,0:T(8,128)(2,1)}, bf16[128,2048]{1,0:T(8,128)(2,1)S(1)}, u32[]{:S(2)}, u32[]{:S(2)}) %collective-permute-start.13) | collective-permute-done | bytes 524320 | tf_op jit(solution)/shard_map/ppermute | solution.py:247
  104.4 0.4 collective-permute-start.15
  104.9 1.5 %collective-permute-start.16 = (bf16[32,2048]{1,0:T(8,128)(2,1)S(1)}, bf16[32,2048]{1,0:T(8,128)(2,1)S(1)}, u32[]{:S(2)}, u32[]{:S(2)}) collective-permute-start(bf16[32,2048]{1,0:T(8,128)(2,1)S(1)} %slice.35), channel_id=1, source_target_pairs={{0,2},{2,0},{4,6},{6,4},{8,10},{10,8},{12,14},{14,12},{16,18},{18,... | collective-permute-start | bytes 393224 | tf_op jit(solution)/shard_map/ppermute | solution.py:247
  106.5 1.6 %collective-permute-start.18 = (bf16[32,2048]{1,0:T(8,128)(2,1)S(1)}, bf16[32,2048]{1,0:T(8,128)(2,1)S(1)}, u32[]{:S(2)}, u32[]{:S(2)}) collective-permute-start(bf16[32,2048]{1,0:T(8,128)(2,1)S(1)} %slice.36), channel_id=1, source_target_pairs={{0,4},{2,6},{4,0},{6,2},{8,12},{10,14},{12,8},{14,10},{16,20},{18,... | collective-permute-start | bytes 393224 | tf_op jit(solution)/shard_map/ppermute | solution.py:247
  108.1 0.6 collective-permute-start.19
  108.6 1.5 %collective-permute-done.15.refs_1_ = bf16[32,2048]{1,0:T(8,128)(2,1)S(1)} collective-permute-done((bf16[32,2048]{1,0:T(8,128)(2,1)S(1)}, bf16[32,2048]{1,0:T(8,128)(2,1)S(1)}, u32[]{:S(2)}, u32[]{:S(2)}) %collective-permute-start.15) | collective-permute-done | bytes 131104 | tf_op jit(solution)/shard_map/ppermute | solution.py:247
  110.1 1.1 collective-permute-start.20
  111.2 1.3 collective-permute-start.21
  112.6 6.7 %gemm.1.before_ref = f32[512,2048]{1,0:T(8,128)S(1)} custom-call(s32[1]{0:T(128)} %bitcast.side_ref, bf16[256,2048]{1,0:T(8,128)(2,1)S(1)} %arrange.1.mine_ref, bf16[256,2048]{1,0:T(8,128)(2,1)S(1)} %collective-permute-done.other_ref, bf16[128,2048]{1,0:T(8,128)(2,1)} %refs_0_.1, bf16[128,2048]{1,0:T(8,128)(2,1)} %collective-permute-done.1.refs_1_, ...), custom_call_target="tpu_custom_call" | custom-call | flops 3489660928 | bytes 6815744 | tf_op jit(solution)/shard_map/gemm/pallas_call | solution.py:114
  119.3 1.5 %last_gemm.1 = (f32[512,2048]{1,0:T(8,128)S(1)}, f32[1,512]{1,0:T(1,128)S(1)}) custom-call(s32[1]{0:T(128)} %bitcast.side_ref, bf16[256,2048]{1,0:T(8,128)(2,1)S(1)} %arrange.1.mine_ref, bf16[256,2048]{1,0:T(8,128)(2,1)S(1)} %collective-permute-done.other_ref, f32[512,2048]{1,0:T(8,128)S(1)} %gemm.1.before_ref, ...), custom_call_target="tpu_custom_call" | custom-call | flops 805306368 | bytes 1572864 | tf_op jit(solution)/shard_map/last_gemm/pallas_call | solution.py:154
  120.9 0.5 copy-done
  121.5 0.4 multiply_reduce_fusion
  121.8 0.2 collective-permute-done.22
  122.1 0.7 add_reduce_fusion
  122.9 0.8 collective-permute-start.23
  123.6 3.2 %collective-permute-done.23 = f32[3,2048]{1,0:T(4,128)S(1)} collective-permute-done((f32[3,2048]{1,0:T(4,128)S(1)}, f32[3,2048]{1,0:T(4,128)S(1)}, u32[]{:S(2)}, u32[]{:S(2)}) %collective-permute-start.23) | collective-permute-done | bytes 24608 | tf_op jit(solution)/shard_map/ppermute | solution.py:25
  126.9 0.9 collective-permute-start.24
  127.8 3.1 %collective-permute-done.24 = f32[3,2048]{1,0:T(4,128)S(1)} collective-permute-done((f32[3,2048]{1,0:T(4,128)S(1)}, f32[3,2048]{1,0:T(4,128)S(1)}, u32[]{:S(2)}, u32[]{:S(2)}) %collective-permute-start.24) | collective-permute-done | bytes 24608 | tf_op jit(solution)/shard_map/ppermute | solution.py:25
  131.0 3.9 %collective-permute-done.25 = f32[3,2048]{1,0:T(4,128)S(1)} collective-permute-done((f32[3,2048]{1,0:T(4,128)S(1)}, f32[3,2048]{1,0:T(4,128)S(1)}, u32[]{:S(2)}, u32[]{:S(2)}) %collective-permute-start.25) | collective-permute-done | bytes 24608 | tf_op jit(solution)/shard_map/ppermute | solution.py:25
  135.0 4.8 %collective-permute-done.26 = f32[3,2048]{1,0:T(4,128)S(1)} collective-permute-done((f32[3,2048]{1,0:T(4,128)S(1)}, f32[3,2048]{1,0:T(4,128)S(1)}, u32[]{:S(2)}, u32[]{:S(2)}) %collective-permute-start.26) | collective-permute-done | bytes 24608 | tf_op jit(solution)/shard_map/ppermute | solution.py:25
  140.0 0.6 copy.11
  140.6 0.6 collective-permute-done.27
  141.2 3.7 %finish.1 = (f32[512,2048]{1,0:T(8,128)}, f32[512,2048]{1,0:T(8,128)}) custom-call(f32[8,128]{1,0:T(8,128)S(1)} %add.64.sums_ref, f32[1,512]{1,0:T(1,128)S(1)} %bitcast.9, f32[1,2048]{1,0:T(1,128)S(1)} %get-tuple-element.13.col_ref, f32[512,2048]{1,0:T(8,128)S(1)} %get-tuple-element.10.gradient_ref, f32[512,2048]{1,0:T(8,128)S(1)} %copy-done), custom_call_target="tpu_custom_call" | custom-call | flops 4194304 | bytes 16777216 | tf_op jit(solution)/shard_map/finish/pallas_call | solution.py:216
  (69 shorter events, 0.9 us)
Async XLA Ops:
  0.6 68.6 %copy-start.15 = (s32[16]{0:T(128)S(1)}, s32[16]{0:T(128)}, u32[]{:S(2)}) copy-start(s32[16]{0:T(128)} %constant.64.clone) | copy-start | bytes 196
  0.6 68.5 %copy-start.16 = (s32[16]{0:T(128)S(1)}, s32[16]{0:T(128)}, u32[]{:S(2)}) copy-start(s32[16]{0:T(128)} %constant.65.clone) | copy-start | bytes 196
  0.7 1.6 %copy-start.1 = (bf16[128,8192]{1,0:T(8,128)(2,1)S(1)}, bf16[128,8192]{1,0:T(8,128)(2,1)}, u32[]{:S(2)}) copy-start(bf16[128,8192]{1,0:T(8,128)(2,1)} %acts_ref.1) | copy-start | bytes 6291460
  3.3 65.9 %all-to-all-start = ((bf16[16,128,256]{2,1,0:T(8,128)(2,1)}), bf16[16,128,256]{2,1,0:T(8,128)(2,1)S(1)}, u32[]{:S(2)}, u32[]{:S(2)}) async-start(bf16[16,128,256]{2,1,0:T(8,128)(2,1)} %pack.1), calls=%async_computation | async-start | bytes 2097152 | tf_op jit(solution)/shard_map/all_to_all | solution.py:270
  10.5 45.0 %collective-permute-start.1 = (bf16[128,2048]{1,0:T(8,128)(2,1)}, bf16[128,2048]{1,0:T(8,128)(2,1)}, u32[]{:S(2)}, u32[]{:S(2)}) collective-permute-start(bf16[128,2048]{1,0:T(8,128)(2,1)} %refs_0_.1), channel_id=1, source_target_pairs={{0,8},{2,10},{4,12},{6,14},{8,16},{10,18},{12,20},{14,22},{16,24},... | collective-permute-start | bytes 1572872 | tf_op jit(solution)/shard_map/ppermute | solution.py:250
  12.0 47.4 %collective-permute-start.4 = (bf16[128,2048]{1,0:T(8,128)(2,1)}, bf16[128,2048]{1,0:T(8,128)(2,1)S(1)}, u32[]{:S(2)}, u32[]{:S(2)}) collective-permute-start(bf16[128,2048]{1,0:T(8,128)(2,1)} %refs_0_.1), channel_id=1, source_target_pairs={{0,2},{2,0},{4,6},{6,4},{8,10},{10,8},{12,14},{14,12},{16,18},{18,... | collective-permute-start | bytes 1572872 | tf_op jit(solution)/shard_map/ppermute | solution.py:247
  13.4 55.3 %collective-permute-start.2 = (bf16[128,2048]{1,0:T(8,128)(2,1)}, bf16[128,2048]{1,0:T(8,128)(2,1)}, u32[]{:S(2)}, u32[]{:S(2)}) collective-permute-start(bf16[128,2048]{1,0:T(8,128)(2,1)} %refs_0_.1), channel_id=1, source_target_pairs={{0,24},{2,26},{4,28},{6,30},{8,0},{10,2},{12,4},{14,6},{16,8},{18,... | collective-permute-start | bytes 1572872 | tf_op jit(solution)/shard_map/ppermute | solution.py:250
  14.0 56.1 %collective-permute-start.5 = (bf16[128,2048]{1,0:T(8,128)(2,1)}, bf16[128,2048]{1,0:T(8,128)(2,1)S(1)}, u32[]{:S(2)}, u32[]{:S(2)}) collective-permute-start(bf16[128,2048]{1,0:T(8,128)(2,1)} %refs_0_.1), channel_id=1, source_target_pairs={{0,4},{2,6},{4,0},{6,2},{8,12},{10,14},{12,8},{14,10},{16,20},{18,... | collective-permute-start | bytes 1572872 | tf_op jit(solution)/shard_map/ppermute | solution.py:247
  55.5 16.3 %collective-permute-start.3 = (bf16[128,2048]{1,0:T(8,128)(2,1)}, bf16[128,2048]{1,0:T(8,128)(2,1)}, u32[]{:S(2)}, u32[]{:S(2)}) collective-permute-start(bf16[128,2048]{1,0:T(8,128)(2,1)} %collective-permute-done.1.refs_1_), channel_id=1, source_target_pairs={{0,8},{2,10},{4,12},{6,14},{8,16},{10,18},{12,20},{14,22},{16,24},... | collective-permute-start | bytes 1572872 | tf_op jit(solution)/shard_map/ppermute | solution.py:250
  57.9 15.4 %collective-permute-start.6 = (bf16[128,2048]{1,0:T(8,128)(2,1)}, bf16[128,2048]{1,0:T(8,128)(2,1)S(1)}, u32[]{:S(2)}, u32[]{:S(2)}) collective-permute-start(bf16[128,2048]{1,0:T(8,128)(2,1)} %collective-permute-done.1.refs_1_), channel_id=1, source_target_pairs={{0,2},{2,0},{4,6},{6,4},{8,10},{10,8},{12,14},{14,12},{16,18},{18,... | collective-permute-start | bytes 1572872 | tf_op jit(solution)/shard_map/ppermute | solution.py:247
  59.4 53.1 %copy-start.4 = (bf16[128,2048]{1,0:T(8,128)(2,1)}, bf16[128,2048]{1,0:T(8,128)(2,1)S(1)}, u32[]{:S(2)}) copy-start(bf16[128,2048]{1,0:T(8,128)(2,1)S(1)} %collective-permute-done.4.refs_4_) | copy-start | bytes 1572868
  60.2 10.0 %collective-permute-start.10 = (bf16[64,2048]{1,0:T(8,128)(2,1)}, bf16[64,2048]{1,0:T(8,128)(2,1)S(1)}, u32[]{:S(2)}, u32[]{:S(2)}) collective-permute-start(bf16[64,2048]{1,0:T(8,128)(2,1)} %slice.32), channel_id=1, source_target_pairs={{0,4},{2,6},{4,0},{6,2},{8,12},{10,14},{12,8},{14,10},{16,20},{18,... | collective-permute-start | bytes 786440 | tf_op jit(solution)/shard_map/ppermute | solution.py:247
  68.7 15.0 %collective-permute-start.7 = (bf16[128,2048]{1,0:T(8,128)(2,1)}, bf16[128,2048]{1,0:T(8,128)(2,1)S(1)}, u32[]{:S(2)}, u32[]{:S(2)}) collective-permute-start(bf16[128,2048]{1,0:T(8,128)(2,1)} %collective-permute-done.1.refs_1_), channel_id=1, source_target_pairs={{0,4},{2,6},{4,0},{6,2},{8,12},{10,14},{12,8},{14,10},{16,20},{18,... | collective-permute-start | bytes 1572872 | tf_op jit(solution)/shard_map/ppermute | solution.py:247
  70.1 42.4 %copy-start.5 = (bf16[128,2048]{1,0:T(8,128)(2,1)}, bf16[128,2048]{1,0:T(8,128)(2,1)S(1)}, u32[]{:S(2)}) copy-start(bf16[128,2048]{1,0:T(8,128)(2,1)S(1)} %collective-permute-done.5.refs_5_) | copy-start | bytes 1572868
  70.1 41.0 %collective-permute-start = (bf16[256,2048]{1,0:T(8,128)(2,1)S(1)}, bf16[256,2048]{1,0:T(8,128)(2,1)S(1)}, u32[]{:S(2)}, u32[]{:S(2)}) collective-permute-start(bf16[256,2048]{1,0:T(8,128)(2,1)S(1)} %arrange.1.mine_ref), channel_id=1, source_target_pairs={{0,1},{1,0},{2,3},{3,2},{4,5},{5,4},{6,7},{7,6},{8,9},{9,8},{10,11... | collective-permute-start | bytes 3145736 | tf_op jit(solution)/shard_map/ppermute | solution.py:277
  70.2 42.3 %copy-start.12 = (bf16[64,2048]{1,0:T(8,128)(2,1)}, bf16[64,2048]{1,0:T(8,128)(2,1)S(1)}, u32[]{:S(2)}) copy-start(bf16[64,2048]{1,0:T(8,128)(2,1)S(1)} %collective-permute-done.10.refs_10_) | copy-start | bytes 786436
  70.2 15.1 %collective-permute-start.8 = (bf16[128,2048]{1,0:T(8,128)(2,1)}, bf16[128,2048]{1,0:T(8,128)(2,1)S(1)}, u32[]{:S(2)}, u32[]{:S(2)}) collective-permute-start(bf16[128,2048]{1,0:T(8,128)(2,1)} %collective-permute-done.2.refs_2_), channel_id=1, source_target_pairs={{0,2},{2,0},{4,6},{6,4},{8,10},{10,8},{12,14},{14,12},{16,18},{18,... | collective-permute-start | bytes 1572872 | tf_op jit(solution)/shard_map/ppermute | solution.py:247
  71.8 23.2 %collective-permute-start.9 = (bf16[128,2048]{1,0:T(8,128)(2,1)}, bf16[128,2048]{1,0:T(8,128)(2,1)S(1)}, u32[]{:S(2)}, u32[]{:S(2)}) collective-permute-start(bf16[128,2048]{1,0:T(8,128)(2,1)} %collective-permute-done.2.refs_2_), channel_id=1, source_target_pairs={{0,4},{2,6},{4,0},{6,2},{8,12},{10,14},{12,8},{14,10},{16,20},{18,... | collective-permute-start | bytes 1572872 | tf_op jit(solution)/shard_map/ppermute | solution.py:247
  73.4 39.1 %copy-start.8 = (bf16[128,2048]{1,0:T(8,128)(2,1)}, bf16[128,2048]{1,0:T(8,128)(2,1)S(1)}, u32[]{:S(2)}) copy-start(bf16[128,2048]{1,0:T(8,128)(2,1)S(1)} %collective-permute-done.6.refs_6_) | copy-start | bytes 1572868
  73.4 23.2 %collective-permute-start.12 = (bf16[128,2048]{1,0:T(8,128)(2,1)}, bf16[128,2048]{1,0:T(8,128)(2,1)S(1)}, u32[]{:S(2)}, u32[]{:S(2)}) collective-permute-start(bf16[128,2048]{1,0:T(8,128)(2,1)} %collective-permute-done.3.refs_3_), channel_id=1, source_target_pairs={{0,2},{2,0},{4,6},{6,4},{8,10},{10,8},{12,14},{14,12},{16,18},{18,... | collective-permute-start | bytes 1572872 | tf_op jit(solution)/shard_map/ppermute | solution.py:247
  83.8 28.8 %copy-start.9 = (bf16[128,2048]{1,0:T(8,128)(2,1)}, bf16[128,2048]{1,0:T(8,128)(2,1)S(1)}, u32[]{:S(2)}) copy-start(bf16[128,2048]{1,0:T(8,128)(2,1)S(1)} %collective-permute-done.7.refs_7_) | copy-start | bytes 1572868
  83.8 20.6 %collective-permute-start.13 = (bf16[128,2048]{1,0:T(8,128)(2,1)}, bf16[128,2048]{1,0:T(8,128)(2,1)S(1)}, u32[]{:S(2)}, u32[]{:S(2)}) collective-permute-start(bf16[128,2048]{1,0:T(8,128)(2,1)} %collective-permute-done.3.refs_3_), channel_id=1, source_target_pairs={{0,4},{2,6},{4,0},{6,2},{8,12},{10,14},{12,8},{14,10},{16,20},{18,... | collective-permute-start | bytes 1572872 | tf_op jit(solution)/shard_map/ppermute | solution.py:247
  85.3 27.2 %copy-start.10 = (bf16[128,2048]{1,0:T(8,128)(2,1)}, bf16[128,2048]{1,0:T(8,128)(2,1)S(1)}, u32[]{:S(2)}) copy-start(bf16[128,2048]{1,0:T(8,128)(2,1)S(1)} %collective-permute-done.8.refs_8_) | copy-start | bytes 1572868
  85.3 19.6 %collective-permute-start.11 = (bf16[64,2048]{1,0:T(8,128)(2,1)S(1)}, bf16[64,2048]{1,0:T(8,128)(2,1)S(1)}, u32[]{:S(2)}, u32[]{:S(2)}) collective-permute-start(bf16[64,2048]{1,0:T(8,128)(2,1)S(1)} %slice.33), channel_id=1, source_target_pairs={{0,2},{2,0},{4,6},{6,4},{8,10},{10,8},{12,14},{14,12},{16,18},{18,... | collective-permute-start | bytes 786440 | tf_op jit(solution)/shard_map/ppermute | solution.py:247
  95.0 17.5 %copy-start.11 = (bf16[128,2048]{1,0:T(8,128)(2,1)}, bf16[128,2048]{1,0:T(8,128)(2,1)S(1)}, u32[]{:S(2)}) copy-start(bf16[128,2048]{1,0:T(8,128)(2,1)S(1)} %collective-permute-done.9.refs_9_) | copy-start | bytes 1572868
  95.0 11.5 %collective-permute-start.14 = (bf16[64,2048]{1,0:T(8,128)(2,1)S(1)}, bf16[64,2048]{1,0:T(8,128)(2,1)S(1)}, u32[]{:S(2)}, u32[]{:S(2)}) collective-permute-start(bf16[64,2048]{1,0:T(8,128)(2,1)S(1)} %collective-permute-done.10.refs_10_), channel_id=1, source_target_pairs={{0,8},{2,10},{4,12},{6,14},{8,16},{10,18},{12,20},{14,22},{16,24},... | collective-permute-start | bytes 786440 | tf_op jit(solution)/shard_map/ppermute | solution.py:250
  96.5 16.0 %copy-start.6 = (bf16[128,2048]{1,0:T(8,128)(2,1)}, bf16[128,2048]{1,0:T(8,128)(2,1)S(1)}, u32[]{:S(2)}) copy-start(bf16[128,2048]{1,0:T(8,128)(2,1)S(1)} %collective-permute-done.12.refs_12_) | copy-start | bytes 1572868
  96.5 11.5 %collective-permute-start.17 = (bf16[64,2048]{1,0:T(8,128)(2,1)S(1)}, bf16[64,2048]{1,0:T(8,128)(2,1)S(1)}, u32[]{:S(2)}, u32[]{:S(2)}) collective-permute-start(bf16[64,2048]{1,0:T(8,128)(2,1)S(1)} %collective-permute-done.10.refs_10_), channel_id=1, source_target_pairs={{0,24},{2,26},{4,28},{6,30},{8,0},{10,2},{12,4},{14,6},{16,8},{18,... | collective-permute-start | bytes 786440 | tf_op jit(solution)/shard_map/ppermute | solution.py:250
  104.4 8.2 %copy-start.7 = (bf16[128,2048]{1,0:T(8,128)(2,1)}, bf16[128,2048]{1,0:T(8,128)(2,1)S(1)}, u32[]{:S(2)}) copy-start(bf16[128,2048]{1,0:T(8,128)(2,1)S(1)} %collective-permute-done.13.refs_13_) | copy-start | bytes 1572868
  104.4 5.7 %collective-permute-start.15 = (bf16[32,2048]{1,0:T(8,128)(2,1)S(1)}, bf16[32,2048]{1,0:T(8,128)(2,1)S(1)}, u32[]{:S(2)}, u32[]{:S(2)}) collective-permute-start(bf16[32,2048]{1,0:T(8,128)(2,1)S(1)} %slice.34), channel_id=1, source_target_pairs={{0,4},{2,6},{4,0},{6,2},{8,12},{10,14},{12,8},{14,10},{16,20},{18,... | collective-permute-start | bytes 393224 | tf_op jit(solution)/shard_map/ppermute | solution.py:247
  104.9 7.6 %copy-start.13 = (bf16[64,2048]{1,0:T(8,128)(2,1)}, bf16[64,2048]{1,0:T(8,128)(2,1)S(1)}, u32[]{:S(2)}) copy-start(bf16[64,2048]{1,0:T(8,128)(2,1)S(1)} %collective-permute-done.11.refs_11_) | copy-start | bytes 786436
  104.9 14.4 %collective-permute-start.16 = (bf16[32,2048]{1,0:T(8,128)(2,1)S(1)}, bf16[32,2048]{1,0:T(8,128)(2,1)S(1)}, u32[]{:S(2)}, u32[]{:S(2)}) collective-permute-start(bf16[32,2048]{1,0:T(8,128)(2,1)S(1)} %slice.35), channel_id=1, source_target_pairs={{0,2},{2,0},{4,6},{6,4},{8,10},{10,8},{12,14},{14,12},{16,18},{18,... | collective-permute-start | bytes 393224 | tf_op jit(solution)/shard_map/ppermute | solution.py:247
  106.5 12.8 %collective-permute-start.18 = (bf16[32,2048]{1,0:T(8,128)(2,1)S(1)}, bf16[32,2048]{1,0:T(8,128)(2,1)S(1)}, u32[]{:S(2)}, u32[]{:S(2)}) collective-permute-start(bf16[32,2048]{1,0:T(8,128)(2,1)S(1)} %slice.36), channel_id=1, source_target_pairs={{0,4},{2,6},{4,0},{6,2},{8,12},{10,14},{12,8},{14,10},{16,20},{18,... | collective-permute-start | bytes 393224 | tf_op jit(solution)/shard_map/ppermute | solution.py:247
  108.1 11.3 %collective-permute-start.19 = (bf16[32,2048]{1,0:T(8,128)(2,1)S(1)}, bf16[32,2048]{1,0:T(8,128)(2,1)S(1)}, u32[]{:S(2)}, u32[]{:S(2)}) collective-permute-start(bf16[32,2048]{1,0:T(8,128)(2,1)S(1)} %slice.37), channel_id=1, source_target_pairs={{0,2},{2,0},{4,6},{6,4},{8,10},{10,8},{12,14},{14,12},{16,18},{18,... | collective-permute-start | bytes 393224 | tf_op jit(solution)/shard_map/ppermute | solution.py:247
  110.1 9.2 %collective-permute-start.20 = (bf16[64,2048]{1,0:T(8,128)(2,1)S(1)}, bf16[64,2048]{1,0:T(8,128)(2,1)S(1)}, u32[]{:S(2)}, u32[]{:S(2)}) collective-permute-start(bf16[64,2048]{1,0:T(8,128)(2,1)S(1)} %slice.38), channel_id=1, source_target_pairs={{0,4},{2,6},{4,0},{6,2},{8,12},{10,14},{12,8},{14,10},{16,20},{18,... | collective-permute-start | bytes 786440 | tf_op jit(solution)/shard_map/ppermute | solution.py:247
  111.2 8.2 %collective-permute-start.21 = (bf16[64,2048]{1,0:T(8,128)(2,1)S(1)}, bf16[64,2048]{1,0:T(8,128)(2,1)S(1)}, u32[]{:S(2)}, u32[]{:S(2)}) collective-permute-start(bf16[64,2048]{1,0:T(8,128)(2,1)S(1)} %slice.39), channel_id=1, source_target_pairs={{0,2},{2,0},{4,6},{6,4},{8,10},{10,8},{12,14},{14,12},{16,18},{18,... | collective-permute-start | bytes 786440 | tf_op jit(solution)/shard_map/ppermute | solution.py:247
  119.3 2.2 %copy-start = (f32[512,2048]{1,0:T(8,128)S(1)}, f32[512,2048]{1,0:T(8,128)}, u32[]{:S(2)}) copy-start(f32[512,2048]{1,0:T(8,128)} %weight_ref.1) | copy-start | bytes 12582916
  119.3 2.8 %copy-start.14 = (f32[512]{0:T(512)S(1)}, f32[512]{0:T(512)}, u32[]{:S(2)}) copy-start(f32[512]{0:T(512)} %param.10) | copy-start | bytes 6148
  120.8 18.9 %copy-start.3 = (f32[2048]{0:T(1024)S(1)}, f32[2048]{0:T(1024)}, u32[]{:S(2)}) copy-start(f32[2048]{0:T(1024)} %param.11) | copy-start | bytes 24580
  120.8 1.2 collective-permute-start.22
  122.1 22.8 %copy-start.2 = (f32[512]{0:T(512)}, f32[512]{0:T(512)S(1)}, u32[]{:S(2)}) copy-start(f32[512]{0:T(512)S(1)} %get-tuple-element.22) | copy-start | bytes 6148
  122.9 4.0 %collective-permute-start.23 = (f32[3,2048]{1,0:T(4,128)S(1)}, f32[3,2048]{1,0:T(4,128)S(1)}, u32[]{:S(2)}, u32[]{:S(2)}) collective-permute-start(f32[3,2048]{1,0:T(4,128)S(1)} %pad_maximum_fusion), channel_id=1, source_target_pairs={{0,2},{2,0},{4,6},{6,4},{8,10},{10,8},{12,14},{14,12},{16,18},{18,... | collective-permute-start | bytes 73736 | tf_op jit(solution)/shard_map/ppermute | solution.py:25
  126.9 4.0 %collective-permute-start.24 = (f32[3,2048]{1,0:T(4,128)S(1)}, f32[3,2048]{1,0:T(4,128)S(1)}, u32[]{:S(2)}, u32[]{:S(2)}) collective-permute-start(f32[3,2048]{1,0:T(4,128)S(1)} %fusion.2), channel_id=1, source_target_pairs={{0,4},{2,6},{4,0},{6,2},{8,12},{10,14},{12,8},{14,10},{16,20},{18,... | collective-permute-start | bytes 73736 | tf_op jit(solution)/shard_map/ppermute | solution.py:25
  130.9 4.0 %collective-permute-start.25 = (f32[3,2048]{1,0:T(4,128)S(1)}, f32[3,2048]{1,0:T(4,128)S(1)}, u32[]{:S(2)}, u32[]{:S(2)}) collective-permute-start(f32[3,2048]{1,0:T(4,128)S(1)} %fusion.3), channel_id=1, source_target_pairs={{0,8},{2,10},{4,12},{6,14},{8,0},{10,2},{12,4},{14,6},{16,24},{18,... | collective-permute-start | bytes 73736 | tf_op jit(solution)/shard_map/ppermute | solution.py:25
  134.9 4.9 %collective-permute-start.26 = (f32[3,2048]{1,0:T(4,128)S(1)}, f32[3,2048]{1,0:T(4,128)S(1)}, u32[]{:S(2)}, u32[]{:S(2)}) collective-permute-start(f32[3,2048]{1,0:T(4,128)S(1)} %add.62), channel_id=1, source_target_pairs={{0,16},{2,18},{4,20},{6,22},{8,24},{10,26},{12,28},{14,30},{16,0},... | collective-permute-start | bytes 73736 | tf_op jit(solution)/shard_map/ppermute | solution.py:25
  139.9 1.2 collective-permute-start.27

commit v2 on v1

--- a/solution.py
+++ b/solution.py
@@ -160,14 +160,15 @@
         compiler_params=pltpu.CompilerParams(vmem_limit_bytes=24 << 20),
         cost_estimate=pl.CostEstimate(flops=2 * rows * depth * cols, bytes_accessed=2 * depth * cols, transcendentals=0),
         name="last_gemm",
-    )(side, *in_vmem(mine, other, before), *pieces)
+    )(side, *in_vmem(mine, other, before, *pieces[:2]), *pieces[2:])
 
 
 def moments_kernel(height, totals_ref, state_ref, col_ref, sums_ref):
-    col = decay_rate * state_ref[...] + (1.0 - decay_rate) * (totals_ref[0:1, :] / height)
+    cols = state_ref.shape[1]
+    col = decay_rate * state_ref[...] + (1.0 - decay_rate) * (totals_ref[0:1, :cols] / height)
     col_ref[...] = col
-    clip = jnp.sum(totals_ref[1:2, :] / col)
-    weight = jnp.sum(totals_ref[2:3, :])
+    clip = jnp.sum(totals_ref[1:2, :cols] / col)
+    weight = jnp.sum(totals_ref[0:1, cols:])
     row = lax.broadcasted_iota(jnp.int32, sums_ref.shape, 0)
     sums_ref[...] = jnp.where(row == 0, clip, weight)
 
@@ -269,8 +270,8 @@
     blocks = pack(side, acts, n_row)
     blocks = lax.all_to_all(blocks, "row", 0, 0, tiled=True)
     *sooner, last = planes = [0] + planes_of(depth)
-    early = [(k, 0) for k in planes] + [(k, j) for k in sooner for j in (1, 2)] + [(0, 3), (last, 1), (last, 2)]
-    late = [(k, 3) for k in planes[1:]]
+    early = [(k, 0) for k in planes] + [(k, j) for k in sooner for j in (1, 2)] + [(0, 3)]
+    late = [(last, 1), (last, 2)] + [(k, 3) for k in planes[1:]]
     below = jnp.array([(-k % depth) * 4 for k, _ in early + late], jnp.int32)
     place = jnp.array([j for _, j in early + late], jnp.int32)
     mine = arrange((me - me % 4 + below) % n_row + ((me % 4) ^ place), blocks)
@@ -282,15 +283,16 @@
     row_total = butterfly(row_squares[0], "col", powers(1, n_col))
     row_moment = decay_rate * row_state + (1.0 - decay_rate) * (row_total / cols_all)
     squares = gradient * gradient
-    parts = jnp.stack(
+    spare = jnp.sum(weight * weight, axis=0)
+    spare = jnp.sum(spare.reshape(-1, LANES), axis=0)
+    totals = jnp.stack(
         [
-            jnp.sum(squares + floor_eps, axis=0),
-            jnp.sum(squares * (1.0 / row_moment)[:, None], axis=0),
-            jnp.sum(weight * weight, axis=0),
+            jnp.concatenate([jnp.sum(squares + floor_eps, axis=0), spare]),
+            jnp.concatenate([jnp.sum(squares * (1.0 / row_moment)[:, None], axis=0), jnp.zeros_like(spare)]),
         ]
     )
-    totals = parts
-    for bit in powers(1, n_row):
+    totals = butterfly(totals, "row", [1, 2])
+    for bit in powers(4, n_row):
         totals = butterfly(totals, "row", [bit])
     col_moment, sums = moments(width, totals, col_state)
     sums = butterfly(sums, "col", powers(1, n_col))

time: 147 us -> 146 us (level)
  waiting for transfers between devices: 94.2 us -> 91.1 us
  other arithmetic: 1.22 us -> 3.38 us
    ppermute x6 -> x7, waiting for transfers between devices: 15.8 us -> 11.9 us  [butterfly(): lax.ppermute(value, axis, [(i, i ^ s) for i in range(n)])]
    ppermute x6 -> x7, starting transfers between devices: 1.97 us -> 5.46 us  [butterfly(): lax.ppermute(value, axis, [(i, i ^ s) for i in range(n)])]
    ppermute x16, starting transfers between devices: 16.5 us -> 13.8 us  [swap(): return lax.ppermute(v, 'row', [(i, i ^ bit) for i in range(n_row)])]
    reduce_sum x1 -> x2, other arithmetic: 0.38 us -> 2.57 us  [the longest x1 2.55 us: per_device(): spare = jnp.sum(weight * weight, axis=0)]
  transfers between devices with their start and end apart: 29 -> 30, of which waited for: 14 -> 14; matrix products, arithmetic and copies ran while one was open for 1% -> 3% of each run, Pallas kernels for 5% -> 5%
where the time goes in v2:
time: 146 us; the launch traced here: 144 us
  waiting for transfers between devices  91.1 us (62%)
  starting transfers between devices  31.3 us (21%)
  Pallas kernels  13.9 us (10%)
  other arithmetic  3.38 us (2%)
  local copies, waits for them, and re-layouts  3.08 us (2%)
    ppermute x5, waiting for transfers between devices, along_z(): lax.ppermute(v, 'row', [(i, (i + 4 * by) % n_row) for i in range(n_row)])  50 us
    ppermute x16, waiting for transfers between devices, swap(): return lax.ppermute(v, 'row', [(i, i ^ bit) for i in range(n_row)])  29.2 us
    ppermute x16, starting transfers between devices, swap(): return lax.ppermute(v, 'row', [(i, i ^ bit) for i in range(n_row)])  13.8 us
    ppermute x7, waiting for transfers between devices, butterfly(): lax.ppermute(value, axis, [(i, i ^ s) for i in range(n)])  11.9 us
    all_to_all x1, starting transfers between devices, per_device(): blocks = lax.all_to_all(blocks, 'row', 0, 0, tiled=True)  7.17 us
    pallas_call x1, Pallas kernels, gemm(): pl.pallas_call(gemm_kernel, grid=(cols // width,), out_shape=jax.ShapeDty...  6.07 us
    ppermute x7, starting transfers between devices, butterfly(): lax.ppermute(value, axis, [(i, i ^ s) for i in range(n)])  5.46 us
    ppermute x5, starting transfers between devices, along_z(): lax.ppermute(v, 'row', [(i, (i + 4 * by) % n_row) for i in range(n_row)])  4.79 us
  transfers between devices with their start and end apart: 30, of which 14 were waited for; matrix products, arithmetic and copies ran while one was open for 3% of the time, Pallas kernels for 5%

profile of v2, /device:TPU:12, one launch (start us, length us, event | category | flops | bytes accessed | tf_op | source)
XLA Modules:
  0.0 143.8 jit_solution(8279595655745807177)
XLA Ops:
  0.7 1.6 %copy-done.1 = bf16[128,8192]{1,0:T(8,128)(2,1)S(1)} copy-done((bf16[128,8192]{1,0:T(8,128)(2,1)S(1)}, bf16[128,8192]{1,0:T(8,128)(2,1)}, u32[]{:S(2)}) %copy-start.1) | copy-done | bytes 2097176
  2.3 1.1 pack.1
  3.3 7.2 %all-to-all-start = ((bf16[16,128,256]{2,1,0:T(8,128)(2,1)}), bf16[16,128,256]{2,1,0:T(8,128)(2,1)S(1)}, u32[]{:S(2)}, u32[]{:S(2)}) async-start(bf16[16,128,256]{2,1,0:T(8,128)(2,1)} %pack.1), calls=%async_computation | async-start | bytes 2097152 | tf_op jit(solution)/shard_map/all_to_all | solution.py:271
  10.5 1.5 %collective-permute-start.1 = (bf16[128,2048]{1,0:T(8,128)(2,1)}, bf16[128,2048]{1,0:T(8,128)(2,1)}, u32[]{:S(2)}, u32[]{:S(2)}) collective-permute-start(bf16[128,2048]{1,0:T(8,128)(2,1)} %refs_0_.1), channel_id=1, source_target_pairs={{0,8},{2,10},{4,12},{6,14},{8,16},{10,18},{12,20},{14,22},{16,24},... | collective-permute-start | bytes 1572872 | tf_op jit(solution)/shard_map/ppermute | solution.py:251
  12.0 1.5 %collective-permute-start.4 = (bf16[128,2048]{1,0:T(8,128)(2,1)}, bf16[128,2048]{1,0:T(8,128)(2,1)S(1)}, u32[]{:S(2)}, u32[]{:S(2)}) collective-permute-start(bf16[128,2048]{1,0:T(8,128)(2,1)} %refs_0_.1), channel_id=1, source_target_pairs={{0,2},{2,0},{4,6},{6,4},{8,10},{10,8},{12,14},{14,12},{16,18},{18,... | collective-permute-start | bytes 1572872 | tf_op jit(solution)/shard_map/ppermute | solution.py:248
  13.4 0.6 collective-permute-start.2
  14.0 0.6 collective-permute-start.5
  14.6 40.9 %collective-permute-done.1.refs_1_ = bf16[128,2048]{1,0:T(8,128)(2,1)} collective-permute-done((bf16[128,2048]{1,0:T(8,128)(2,1)}, bf16[128,2048]{1,0:T(8,128)(2,1)}, u32[]{:S(2)}, u32[]{:S(2)}) %collective-permute-start.1) | collective-permute-done | bytes 524320 | tf_op jit(solution)/shard_map/ppermute | solution.py:251
  55.5 2.5 %collective-permute-start.3 = (bf16[128,2048]{1,0:T(8,128)(2,1)}, bf16[128,2048]{1,0:T(8,128)(2,1)}, u32[]{:S(2)}, u32[]{:S(2)}) collective-permute-start(bf16[128,2048]{1,0:T(8,128)(2,1)} %collective-permute-done.1.refs_1_), channel_id=1, source_target_pairs={{0,8},{2,10},{4,12},{6,14},{8,16},{10,18},{12,20},{14,22},{16,24},... | collective-permute-start | bytes 1572872 | tf_op jit(solution)/shard_map/ppermute | solution.py:251
  57.9 1.5 %collective-permute-start.6 = (bf16[128,2048]{1,0:T(8,128)(2,1)}, bf16[128,2048]{1,0:T(8,128)(2,1)S(1)}, u32[]{:S(2)}, u32[]{:S(2)}) collective-permute-start(bf16[128,2048]{1,0:T(8,128)(2,1)} %collective-permute-done.1.refs_1_), channel_id=1, source_target_pairs={{0,2},{2,0},{4,6},{6,4},{8,10},{10,8},{12,14},{14,12},{16,18},{18,... | collective-permute-start | bytes 1572872 | tf_op jit(solution)/shard_map/ppermute | solution.py:248
  59.4 0.5 collective-permute-start.7
  59.9 0.7 slice.32
  60.6 8.1 %collective-permute-done.2.refs_2_ = bf16[128,2048]{1,0:T(8,128)(2,1)} collective-permute-done((bf16[128,2048]{1,0:T(8,128)(2,1)}, bf16[128,2048]{1,0:T(8,128)(2,1)}, u32[]{:S(2)}, u32[]{:S(2)}) %collective-permute-start.2) | collective-permute-done | bytes 524320 | tf_op jit(solution)/shard_map/ppermute | solution.py:251
  68.7 0.4 collective-permute-start.10
  69.2 0.9 arrange.1.mine_ref
  70.2 7.6 %collective-permute-done.10.refs_10_ = bf16[64,2048]{1,0:T(8,128)(2,1)S(1)} collective-permute-done((bf16[64,2048]{1,0:T(8,128)(2,1)}, bf16[64,2048]{1,0:T(8,128)(2,1)S(1)}, u32[]{:S(2)}, u32[]{:S(2)}) %collective-permute-start.10) | collective-permute-done | bytes 262176 | tf_op jit(solution)/shard_map/ppermute | solution.py:248
  77.8 0.6 collective-permute-start.8
  78.4 0.3 collective-permute-start.9
  78.7 1.5 %collective-permute-start.12 = (bf16[128,2048]{1,0:T(8,128)(2,1)}, bf16[128,2048]{1,0:T(8,128)(2,1)S(1)}, u32[]{:S(2)}, u32[]{:S(2)}) collective-permute-start(bf16[128,2048]{1,0:T(8,128)(2,1)} %collective-permute-done.3.refs_3_), channel_id=1, source_target_pairs={{0,2},{2,0},{4,6},{6,4},{8,10},{10,8},{12,14},{14,12},{16,18},{18,... | collective-permute-start | bytes 1572872 | tf_op jit(solution)/shard_map/ppermute | solution.py:248
  80.2 1.7 %collective-permute-start.13 = (bf16[128,2048]{1,0:T(8,128)(2,1)}, bf16[128,2048]{1,0:T(8,128)(2,1)S(1)}, u32[]{:S(2)}, u32[]{:S(2)}) collective-permute-start(bf16[128,2048]{1,0:T(8,128)(2,1)} %collective-permute-done.3.refs_3_), channel_id=1, source_target_pairs={{0,4},{2,6},{4,0},{6,2},{8,12},{10,14},{12,8},{14,10},{16,20},{18,... | collective-permute-start | bytes 1572872 | tf_op jit(solution)/shard_map/ppermute | solution.py:248
  81.9 10.9 %collective-permute-done.8.refs_8_ = bf16[128,2048]{1,0:T(8,128)(2,1)S(1)} collective-permute-done((bf16[128,2048]{1,0:T(8,128)(2,1)}, bf16[128,2048]{1,0:T(8,128)(2,1)S(1)}, u32[]{:S(2)}, u32[]{:S(2)}) %collective-permute-start.8) | collective-permute-done | bytes 524320 | tf_op jit(solution)/shard_map/ppermute | solution.py:248
  92.8 0.6 collective-permute-start.11
  93.4 0.3 collective-permute-start.14
  93.7 10.4 %collective-permute-done.12.refs_0_ = bf16[128,2048]{1,0:T(8,128)(2,1)S(1)} collective-permute-done((bf16[128,2048]{1,0:T(8,128)(2,1)}, bf16[128,2048]{1,0:T(8,128)(2,1)S(1)}, u32[]{:S(2)}, u32[]{:S(2)}) %collective-permute-start.12) | collective-permute-done | bytes 524320 | tf_op jit(solution)/shard_map/ppermute | solution.py:248
  104.1 0.3 collective-permute-start.15
  104.4 2.6 %multiply_reduce_fusion.1 = f32[2048]{0:T(1024)S(1)} fusion(f32[512,2048]{1,0:T(8,128)} %weight_ref.1), kind=kLoop, calls=%fused_computation.1 | loop fusion | flops 2095104 | bytes 4202496 | tf_op jit(solution)/shard_map/reduce_sum | solution.py:286
  107.3 0.9 collective-permute-start.16
  108.2 1.2 collective-permute-start.18
  109.4 1.0 collective-permute-done.17.refs_5_
  110.4 0.6 collective-permute-start.19
  111.0 0.3 collective-permute-start.20
  111.4 1.4 collective-permute-start.21
  112.8 6.1 %gemm.1.before_ref = f32[512,2048]{1,0:T(8,128)S(1)} custom-call(s32[1]{0:T(128)} %bitcast.side_ref, bf16[256,2048]{1,0:T(8,128)(2,1)S(1)} %arrange.1.mine_ref, bf16[256,2048]{1,0:T(8,128)(2,1)S(1)} %collective-permute-done.other_ref, bf16[128,2048]{1,0:T(8,128)(2,1)} %refs_0_.1, bf16[128,2048]{1,0:T(8,128)(2,1)} %collective-permute-done.1.refs_1_, ...), custom_call_target="tpu_custom_call" | custom-call | flops 2952790016 | bytes 5767168 | tf_op jit(solution)/shard_map/gemm/pallas_call | solution.py:114
  119.0 2.0 %last_gemm.1 = (f32[512,2048]{1,0:T(8,128)S(1)}, f32[1,512]{1,0:T(1,128)S(1)}) custom-call(s32[1]{0:T(128)} %bitcast.side_ref, bf16[256,2048]{1,0:T(8,128)(2,1)S(1)} %arrange.1.mine_ref, bf16[256,2048]{1,0:T(8,128)(2,1)S(1)} %collective-permute-done.other_ref, f32[512,2048]{1,0:T(8,128)S(1)} %gemm.1.before_ref, ...), custom_call_target="tpu_custom_call" | custom-call | flops 1342177280 | bytes 2621440 | tf_op jit(solution)/shard_map/last_gemm/pallas_call | solution.py:154
  121.1 1.1 collective-permute-done.22
  122.3 0.7 add_reduce_fusion
  123.1 1.3 collective-permute-start.23
  124.4 1.1 collective-permute-start.24
  125.4 1.2 collective-permute-start.25
  126.7 0.3 collective-permute-done.23
  126.9 1.2 collective-permute-done.24
  128.1 2.0 %collective-permute-done.25 = f32[2,2176]{1,0:T(2,128)S(1)} collective-permute-done((f32[2,2176]{1,0:T(2,128)S(1)}, f32[2,2176]{1,0:T(2,128)S(1)}, u32[]{:S(2)}, u32[]{:S(2)}) %collective-permute-start.25) | collective-permute-done | bytes 17440 | tf_op jit(solution)/shard_map/ppermute | solution.py:25
  130.2 3.7 %collective-permute-done.26 = f32[2,2176]{1,0:T(2,128)S(1)} collective-permute-done((f32[2,2176]{1,0:T(2,128)S(1)}, f32[2,2176]{1,0:T(2,128)S(1)}, u32[]{:S(2)}, u32[]{:S(2)}) %collective-permute-start.26) | collective-permute-done | bytes 17440 | tf_op jit(solution)/shard_map/ppermute | solution.py:25
  134.0 1.7 %collective-permute-start.27 = (f32[2,2176]{1,0:T(2,128)S(1)}, f32[2,2176]{1,0:T(2,128)S(1)}, u32[]{:S(2)}, u32[]{:S(2)}) collective-permute-start(f32[2,2176]{1,0:T(2,128)S(1)} %add.68), channel_id=1, source_target_pairs={{0,16},{2,18},{4,20},{6,22},{8,24},{10,26},{12,28},{14,30},{16,0},... | collective-permute-start | bytes 52232 | tf_op jit(solution)/shard_map/ppermute | solution.py:25
  135.6 3.0 %collective-permute-done.27 = f32[2,2176]{1,0:T(2,128)S(1)} collective-permute-done((f32[2,2176]{1,0:T(2,128)S(1)}, f32[2,2176]{1,0:T(2,128)S(1)}, u32[]{:S(2)}, u32[]{:S(2)}) %collective-permute-start.27) | collective-permute-done | bytes 17440 | tf_op jit(solution)/shard_map/ppermute | solution.py:25
  138.9 0.6 copy.11
  139.5 0.6 collective-permute-done.28
  140.1 3.7 %finish.1 = (f32[512,2048]{1,0:T(8,128)}, f32[512,2048]{1,0:T(8,128)}) custom-call(f32[8,128]{1,0:T(8,128)S(1)} %add.70.sums_ref, f32[1,512]{1,0:T(1,128)S(1)} %bitcast.8, f32[1,2048]{1,0:T(1,128)S(1)} %get-tuple-element.13.col_ref, f32[512,2048]{1,0:T(8,128)S(1)} %get-tuple-element.10.gradient_ref, f32[512,2048]{1,0:T(8,128)S(1)} %copy-done), custom_call_target="tpu_custom_call" | custom-call | flops 4194304 | bytes 16777216 | tf_op jit(solution)/shard_map/finish/pallas_call | solution.py:217
  (71 shorter events, 1.0 us)
Async XLA Ops:
  0.6 68.6 %copy-start.13 = (s32[16]{0:T(128)S(1)}, s32[16]{0:T(128)}, u32[]{:S(2)}) copy-start(s32[16]{0:T(128)} %constant.65.clone) | copy-start | bytes 196
  0.6 68.5 %copy-start.14 = (s32[16]{0:T(128)S(1)}, s32[16]{0:T(128)}, u32[]{:S(2)}) copy-start(s32[16]{0:T(128)} %constant.66.clone) | copy-start | bytes 196
  0.7 1.6 %copy-start.1 = (bf16[128,8192]{1,0:T(8,128)(2,1)S(1)}, bf16[128,8192]{1,0:T(8,128)(2,1)}, u32[]{:S(2)}) copy-start(bf16[128,8192]{1,0:T(8,128)(2,1)} %acts_ref.1) | copy-start | bytes 6291460
  3.3 65.9 %all-to-all-start = ((bf16[16,128,256]{2,1,0:T(8,128)(2,1)}), bf16[16,128,256]{2,1,0:T(8,128)(2,1)S(1)}, u32[]{:S(2)}, u32[]{:S(2)}) async-start(bf16[16,128,256]{2,1,0:T(8,128)(2,1)} %pack.1), calls=%async_computation | async-start | bytes 2097152 | tf_op jit(solution)/shard_map/all_to_all | solution.py:271
  10.5 45.0 %collective-permute-start.1 = (bf16[128,2048]{1,0:T(8,128)(2,1)}, bf16[128,2048]{1,0:T(8,128)(2,1)}, u32[]{:S(2)}, u32[]{:S(2)}) collective-permute-start(bf16[128,2048]{1,0:T(8,128)(2,1)} %refs_0_.1), channel_id=1, source_target_pairs={{0,8},{2,10},{4,12},{6,14},{8,16},{10,18},{12,20},{14,22},{16,24},... | collective-permute-start | bytes 1572872 | tf_op jit(solution)/shard_map/ppermute | solution.py:251
  12.0 47.4 %collective-permute-start.4 = (bf16[128,2048]{1,0:T(8,128)(2,1)}, bf16[128,2048]{1,0:T(8,128)(2,1)S(1)}, u32[]{:S(2)}, u32[]{:S(2)}) collective-permute-start(bf16[128,2048]{1,0:T(8,128)(2,1)} %refs_0_.1), channel_id=1, source_target_pairs={{0,2},{2,0},{4,6},{6,4},{8,10},{10,8},{12,14},{14,12},{16,18},{18,... | collective-permute-start | bytes 1572872 | tf_op jit(solution)/shard_map/ppermute | solution.py:248
  13.4 55.3 %collective-permute-start.2 = (bf16[128,2048]{1,0:T(8,128)(2,1)}, bf16[128,2048]{1,0:T(8,128)(2,1)}, u32[]{:S(2)}, u32[]{:S(2)}) collective-permute-start(bf16[128,2048]{1,0:T(8,128)(2,1)} %refs_0_.1), channel_id=1, source_target_pairs={{0,24},{2,26},{4,28},{6,30},{8,0},{10,2},{12,4},{14,6},{16,8},{18,... | collective-permute-start | bytes 1572872 | tf_op jit(solution)/shard_map/ppermute | solution.py:251
  14.0 56.1 %collective-permute-start.5 = (bf16[128,2048]{1,0:T(8,128)(2,1)}, bf16[128,2048]{1,0:T(8,128)(2,1)S(1)}, u32[]{:S(2)}, u32[]{:S(2)}) collective-permute-start(bf16[128,2048]{1,0:T(8,128)(2,1)} %refs_0_.1), channel_id=1, source_target_pairs={{0,4},{2,6},{4,0},{6,2},{8,12},{10,14},{12,8},{14,10},{16,20},{18,... | collective-permute-start | bytes 1572872 | tf_op jit(solution)/shard_map/ppermute | solution.py:248
  55.5 22.9 %collective-permute-start.3 = (bf16[128,2048]{1,0:T(8,128)(2,1)}, bf16[128,2048]{1,0:T(8,128)(2,1)}, u32[]{:S(2)}, u32[]{:S(2)}) collective-permute-start(bf16[128,2048]{1,0:T(8,128)(2,1)} %collective-permute-done.1.refs_1_), channel_id=1, source_target_pairs={{0,8},{2,10},{4,12},{6,14},{8,16},{10,18},{12,20},{14,22},{16,24},... | collective-permute-start | bytes 1572872 | tf_op jit(solution)/shard_map/ppermute | solution.py:251
  57.9 20.8 %collective-permute-start.6 = (bf16[128,2048]{1,0:T(8,128)(2,1)}, bf16[128,2048]{1,0:T(8,128)(2,1)S(1)}, u32[]{:S(2)}, u32[]{:S(2)}) collective-permute-start(bf16[128,2048]{1,0:T(8,128)(2,1)} %collective-permute-done.1.refs_1_), channel_id=1, source_target_pairs={{0,2},{2,0},{4,6},{6,4},{8,10},{10,8},{12,14},{14,12},{16,18},{18,... | collective-permute-start | bytes 1572872 | tf_op jit(solution)/shard_map/ppermute | solution.py:248
  59.4 47.6 %copy-start.4 = (bf16[128,2048]{1,0:T(8,128)(2,1)}, bf16[128,2048]{1,0:T(8,128)(2,1)S(1)}, u32[]{:S(2)}) copy-start(bf16[128,2048]{1,0:T(8,128)(2,1)S(1)} %collective-permute-done.4.refs_4_) | copy-start | bytes 1572868
  59.4 20.8 %collective-permute-start.7 = (bf16[128,2048]{1,0:T(8,128)(2,1)}, bf16[128,2048]{1,0:T(8,128)(2,1)S(1)}, u32[]{:S(2)}, u32[]{:S(2)}) collective-permute-start(bf16[128,2048]{1,0:T(8,128)(2,1)} %collective-permute-done.1.refs_1_), channel_id=1, source_target_pairs={{0,4},{2,6},{4,0},{6,2},{8,12},{10,14},{12,8},{14,10},{16,20},{18,... | collective-permute-start | bytes 1572872 | tf_op jit(solution)/shard_map/ppermute | solution.py:248
  68.7 9.1 %collective-permute-start.10 = (bf16[64,2048]{1,0:T(8,128)(2,1)}, bf16[64,2048]{1,0:T(8,128)(2,1)S(1)}, u32[]{:S(2)}, u32[]{:S(2)}) collective-permute-start(bf16[64,2048]{1,0:T(8,128)(2,1)} %slice.32), channel_id=1, source_target_pairs={{0,4},{2,6},{4,0},{6,2},{8,12},{10,14},{12,8},{14,10},{16,20},{18,... | collective-permute-start | bytes 786440 | tf_op jit(solution)/shard_map/ppermute | solution.py:248
  70.1 42.7 %copy-start.5 = (bf16[128,2048]{1,0:T(8,128)(2,1)}, bf16[128,2048]{1,0:T(8,128)(2,1)S(1)}, u32[]{:S(2)}) copy-start(bf16[128,2048]{1,0:T(8,128)(2,1)S(1)} %collective-permute-done.5.refs_5_) | copy-start | bytes 1572868
  70.1 41.2 %collective-permute-start = (bf16[256,2048]{1,0:T(8,128)(2,1)S(1)}, bf16[256,2048]{1,0:T(8,128)(2,1)S(1)}, u32[]{:S(2)}, u32[]{:S(2)}) collective-permute-start(bf16[256,2048]{1,0:T(8,128)(2,1)S(1)} %arrange.1.mine_ref), channel_id=1, source_target_pairs={{0,1},{1,0},{2,3},{3,2},{4,5},{5,4},{6,7},{7,6},{8,9},{9,8},{10,11... | collective-permute-start | bytes 3145736 | tf_op jit(solution)/shard_map/ppermute | solution.py:278
  77.8 35.0 %copy-start.10 = (bf16[64,2048]{1,0:T(8,128)(2,1)}, bf16[64,2048]{1,0:T(8,128)(2,1)S(1)}, u32[]{:S(2)}) copy-start(bf16[64,2048]{1,0:T(8,128)(2,1)S(1)} %collective-permute-done.10.refs_10_) | copy-start | bytes 786436
  77.8 15.0 %collective-permute-start.8 = (bf16[128,2048]{1,0:T(8,128)(2,1)}, bf16[128,2048]{1,0:T(8,128)(2,1)S(1)}, u32[]{:S(2)}, u32[]{:S(2)}) collective-permute-start(bf16[128,2048]{1,0:T(8,128)(2,1)} %collective-permute-done.2.refs_2_), channel_id=1, source_target_pairs={{0,2},{2,0},{4,6},{6,4},{8,10},{10,8},{12,14},{14,12},{16,18},{18,... | collective-permute-start | bytes 1572872 | tf_op jit(solution)/shard_map/ppermute | solution.py:248
  78.4 15.0 %collective-permute-start.9 = (bf16[128,2048]{1,0:T(8,128)(2,1)}, bf16[128,2048]{1,0:T(8,128)(2,1)S(1)}, u32[]{:S(2)}, u32[]{:S(2)}) collective-permute-start(bf16[128,2048]{1,0:T(8,128)(2,1)} %collective-permute-done.2.refs_2_), channel_id=1, source_target_pairs={{0,4},{2,6},{4,0},{6,2},{8,12},{10,14},{12,8},{14,10},{16,20},{18,... | collective-permute-start | bytes 1572872 | tf_op jit(solution)/shard_map/ppermute | solution.py:248
  78.7 34.1 %copy-start.6 = (bf16[128,2048]{1,0:T(8,128)(2,1)}, bf16[128,2048]{1,0:T(8,128)(2,1)S(1)}, u32[]{:S(2)}) copy-start(bf16[128,2048]{1,0:T(8,128)(2,1)S(1)} %collective-permute-done.6.refs_6_) | copy-start | bytes 1572868
  78.7 25.4 %collective-permute-start.12 = (bf16[128,2048]{1,0:T(8,128)(2,1)}, bf16[128,2048]{1,0:T(8,128)(2,1)S(1)}, u32[]{:S(2)}, u32[]{:S(2)}) collective-permute-start(bf16[128,2048]{1,0:T(8,128)(2,1)} %collective-permute-done.3.refs_3_), channel_id=1, source_target_pairs={{0,2},{2,0},{4,6},{6,4},{8,10},{10,8},{12,14},{14,12},{16,18},{18,... | collective-permute-start | bytes 1572872 | tf_op jit(solution)/shard_map/ppermute | solution.py:248
  80.2 32.6 %copy-start.7 = (bf16[128,2048]{1,0:T(8,128)(2,1)}, bf16[128,2048]{1,0:T(8,128)(2,1)S(1)}, u32[]{:S(2)}) copy-start(bf16[128,2048]{1,0:T(8,128)(2,1)S(1)} %collective-permute-done.7.refs_7_) | copy-start | bytes 1572868
  80.2 23.9 %collective-permute-start.13 = (bf16[128,2048]{1,0:T(8,128)(2,1)}, bf16[128,2048]{1,0:T(8,128)(2,1)S(1)}, u32[]{:S(2)}, u32[]{:S(2)}) collective-permute-start(bf16[128,2048]{1,0:T(8,128)(2,1)} %collective-permute-done.3.refs_3_), channel_id=1, source_target_pairs={{0,4},{2,6},{4,0},{6,2},{8,12},{10,14},{12,8},{14,10},{16,20},{18,... | collective-permute-start | bytes 1572872 | tf_op jit(solution)/shard_map/ppermute | solution.py:248
  92.8 20.0 %copy-start.8 = (bf16[128,2048]{1,0:T(8,128)(2,1)}, bf16[128,2048]{1,0:T(8,128)(2,1)S(1)}, u32[]{:S(2)}) copy-start(bf16[128,2048]{1,0:T(8,128)(2,1)S(1)} %collective-permute-done.8.refs_8_) | copy-start | bytes 1572868
  92.8 14.5 %collective-permute-start.11 = (bf16[64,2048]{1,0:T(8,128)(2,1)S(1)}, bf16[64,2048]{1,0:T(8,128)(2,1)S(1)}, u32[]{:S(2)}, u32[]{:S(2)}) collective-permute-start(bf16[64,2048]{1,0:T(8,128)(2,1)S(1)} %slice.33), channel_id=1, source_target_pairs={{0,2},{2,0},{4,6},{6,4},{8,10},{10,8},{12,14},{14,12},{16,18},{18,... | collective-permute-start | bytes 786440 | tf_op jit(solution)/shard_map/ppermute | solution.py:248
  93.4 19.4 %copy-start.9 = (bf16[128,2048]{1,0:T(8,128)(2,1)}, bf16[128,2048]{1,0:T(8,128)(2,1)S(1)}, u32[]{:S(2)}) copy-start(bf16[128,2048]{1,0:T(8,128)(2,1)S(1)} %collective-permute-done.9.refs_9_) | copy-start | bytes 1572868
  93.4 14.8 %collective-permute-start.14 = (bf16[64,2048]{1,0:T(8,128)(2,1)S(1)}, bf16[64,2048]{1,0:T(8,128)(2,1)S(1)}, u32[]{:S(2)}, u32[]{:S(2)}) collective-permute-start(bf16[64,2048]{1,0:T(8,128)(2,1)S(1)} %collective-permute-done.10.refs_10_), channel_id=1, source_target_pairs={{0,8},{2,10},{4,12},{6,14},{8,16},{10,18},{12,20},{14,22},{16,24},... | collective-permute-start | bytes 786440 | tf_op jit(solution)/shard_map/ppermute | solution.py:251
  104.1 6.4 %collective-permute-start.17 = (bf16[64,2048]{1,0:T(8,128)(2,1)S(1)}, bf16[64,2048]{1,0:T(8,128)(2,1)S(1)}, u32[]{:S(2)}, u32[]{:S(2)}) collective-permute-start(bf16[64,2048]{1,0:T(8,128)(2,1)S(1)} %collective-permute-done.10.refs_10_), channel_id=1, source_target_pairs={{0,24},{2,26},{4,28},{6,30},{8,0},{10,2},{12,4},{14,6},{16,8},{18,... | collective-permute-start | bytes 786440 | tf_op jit(solution)/shard_map/ppermute | solution.py:251
  104.1 6.9 %collective-permute-start.15 = (bf16[32,2048]{1,0:T(8,128)(2,1)S(1)}, bf16[32,2048]{1,0:T(8,128)(2,1)S(1)}, u32[]{:S(2)}, u32[]{:S(2)}) collective-permute-start(bf16[32,2048]{1,0:T(8,128)(2,1)S(1)} %slice.34), channel_id=1, source_target_pairs={{0,4},{2,6},{4,0},{6,2},{8,12},{10,14},{12,8},{14,10},{16,20},{18,... | collective-permute-start | bytes 393224 | tf_op jit(solution)/shard_map/ppermute | solution.py:248
  107.3 5.5 %copy-start.11 = (bf16[64,2048]{1,0:T(8,128)(2,1)}, bf16[64,2048]{1,0:T(8,128)(2,1)S(1)}, u32[]{:S(2)}) copy-start(bf16[64,2048]{1,0:T(8,128)(2,1)S(1)} %collective-permute-done.11.refs_11_) | copy-start | bytes 786436
  107.3 11.6 %collective-permute-start.16 = (bf16[32,2048]{1,0:T(8,128)(2,1)S(1)}, bf16[32,2048]{1,0:T(8,128)(2,1)S(1)}, u32[]{:S(2)}, u32[]{:S(2)}) collective-permute-start(bf16[32,2048]{1,0:T(8,128)(2,1)S(1)} %slice.35), channel_id=1, source_target_pairs={{0,2},{2,0},{4,6},{6,4},{8,10},{10,8},{12,14},{14,12},{16,18},{18,... | collective-permute-start | bytes 393224 | tf_op jit(solution)/shard_map/ppermute | solution.py:248
  108.2 10.7 %collective-permute-start.18 = (bf16[32,2048]{1,0:T(8,128)(2,1)S(1)}, bf16[32,2048]{1,0:T(8,128)(2,1)S(1)}, u32[]{:S(2)}, u32[]{:S(2)}) collective-permute-start(bf16[32,2048]{1,0:T(8,128)(2,1)S(1)} %slice.36), channel_id=1, source_target_pairs={{0,4},{2,6},{4,0},{6,2},{8,12},{10,14},{12,8},{14,10},{16,20},{18,... | collective-permute-start | bytes 393224 | tf_op jit(solution)/shard_map/ppermute | solution.py:248
  110.4 8.5 %collective-permute-start.19 = (bf16[32,2048]{1,0:T(8,128)(2,1)S(1)}, bf16[32,2048]{1,0:T(8,128)(2,1)S(1)}, u32[]{:S(2)}, u32[]{:S(2)}) collective-permute-start(bf16[32,2048]{1,0:T(8,128)(2,1)S(1)} %slice.37), channel_id=1, source_target_pairs={{0,2},{2,0},{4,6},{6,4},{8,10},{10,8},{12,14},{14,12},{16,18},{18,... | collective-permute-start | bytes 393224 | tf_op jit(solution)/shard_map/ppermute | solution.py:248
  111.0 7.9 %collective-permute-start.20 = (bf16[64,2048]{1,0:T(8,128)(2,1)S(1)}, bf16[64,2048]{1,0:T(8,128)(2,1)S(1)}, u32[]{:S(2)}, u32[]{:S(2)}) collective-permute-start(bf16[64,2048]{1,0:T(8,128)(2,1)S(1)} %slice.38), channel_id=1, source_target_pairs={{0,4},{2,6},{4,0},{6,2},{8,12},{10,14},{12,8},{14,10},{16,20},{18,... | collective-permute-start | bytes 786440 | tf_op jit(solution)/shard_map/ppermute | solution.py:248
  111.4 7.6 %collective-permute-start.21 = (bf16[64,2048]{1,0:T(8,128)(2,1)S(1)}, bf16[64,2048]{1,0:T(8,128)(2,1)S(1)}, u32[]{:S(2)}, u32[]{:S(2)}) collective-permute-start(bf16[64,2048]{1,0:T(8,128)(2,1)S(1)} %slice.39), channel_id=1, source_target_pairs={{0,2},{2,0},{4,6},{6,4},{8,10},{10,8},{12,14},{14,12},{16,18},{18,... | collective-permute-start | bytes 786440 | tf_op jit(solution)/shard_map/ppermute | solution.py:248
  118.9 3.4 %copy-start.12 = (f32[512]{0:T(512)S(1)}, f32[512]{0:T(512)}, u32[]{:S(2)}) copy-start(f32[512]{0:T(512)} %param.10) | copy-start | bytes 6148
  121.0 17.7 %copy-start.3 = (f32[2048]{0:T(1024)S(1)}, f32[2048]{0:T(1024)}, u32[]{:S(2)}) copy-start(f32[2048]{0:T(1024)} %param.11) | copy-start | bytes 24580
  121.0 19.1 %copy-start = (f32[512,2048]{1,0:T(8,128)S(1)}, f32[512,2048]{1,0:T(8,128)}, u32[]{:S(2)}) copy-start(f32[512,2048]{1,0:T(8,128)} %weight_ref.1) | copy-start | bytes 12582916
  121.0 1.2 collective-permute-start.22
  122.3 21.5 %copy-start.2 = (f32[512]{0:T(512)}, f32[512]{0:T(512)S(1)}, u32[]{:S(2)}) copy-start(f32[512]{0:T(512)S(1)} %get-tuple-element.22) | copy-start | bytes 6148
  123.1 3.8 %collective-permute-start.23 = (f32[2,2176]{1,0:T(2,128)S(1)}, f32[2,2176]{1,0:T(2,128)S(1)}, u32[]{:S(2)}, u32[]{:S(2)}) collective-permute-start(f32[2,2176]{1,0:T(2,128)S(1)} %pad_maximum_fusion), channel_id=1, source_target_pairs={{0,2},{2,0},{4,6},{6,4},{8,10},{10,8},{12,14},{14,12},{16,18},{18,... | collective-permute-start | bytes 52232 | tf_op jit(solution)/shard_map/ppermute | solution.py:25
  124.4 3.8 %collective-permute-start.24 = (f32[2,2176]{1,0:T(2,128)S(1)}, f32[2,2176]{1,0:T(2,128)S(1)}, u32[]{:S(2)}, u32[]{:S(2)}) collective-permute-start(f32[2,2176]{1,0:T(2,128)S(1)} %pad_maximum_fusion), channel_id=1, source_target_pairs={{0,4},{2,6},{4,0},{6,2},{8,12},{10,14},{12,8},{14,10},{16,20},{18,... | collective-permute-start | bytes 52232 | tf_op jit(solution)/shard_map/ppermute | solution.py:25
  125.4 4.6 %collective-permute-start.25 = (f32[2,2176]{1,0:T(2,128)S(1)}, f32[2,2176]{1,0:T(2,128)S(1)}, u32[]{:S(2)}, u32[]{:S(2)}) collective-permute-start(f32[2,2176]{1,0:T(2,128)S(1)} %pad_maximum_fusion), channel_id=1, source_target_pairs={{0,6},{2,4},{4,2},{6,0},{8,14},{10,12},{12,10},{14,8},{16,22},{18,... | collective-permute-start | bytes 52232 | tf_op jit(solution)/shard_map/ppermute | solution.py:25
  130.1 3.8 %collective-permute-start.26 = (f32[2,2176]{1,0:T(2,128)S(1)}, f32[2,2176]{1,0:T(2,128)S(1)}, u32[]{:S(2)}, u32[]{:S(2)}) collective-permute-start(f32[2,2176]{1,0:T(2,128)S(1)} %add_add_fusion), channel_id=1, source_target_pairs={{0,8},{2,10},{4,12},{6,14},{8,0},{10,2},{12,4},{14,6},{16,24},{18,... | collective-permute-start | bytes 52232 | tf_op jit(solution)/shard_map/ppermute | solution.py:25
  134.0 4.7 %collective-permute-start.27 = (f32[2,2176]{1,0:T(2,128)S(1)}, f32[2,2176]{1,0:T(2,128)S(1)}, u32[]{:S(2)}, u32[]{:S(2)}) collective-permute-start(f32[2,2176]{1,0:T(2,128)S(1)} %add.68), channel_id=1, source_target_pairs={{0,16},{2,18},{4,20},{6,22},{8,24},{10,26},{12,28},{14,30},{16,0},... | collective-permute-start | bytes 52232 | tf_op jit(solution)/shard_map/ppermute | solution.py:25
  138.8 1.2 collective-permute-start.28

commit v3 on v2

--- a/solution.py
+++ b/solution.py
@@ -22,7 +22,9 @@
 
 def butterfly(value, axis, offsets):
     n = lax.axis_size(axis)
-    terms = [value] + [lax.ppermute(value, axis, [(i, i ^ s) for i in range(n)]) for s in spans(offsets)[1:]]
+    terms = [value]
+    for s in spans(offsets)[1:]:
+        terms.append(lax.ppermute(value, axis, [(i, i ^ s) for i in range(n)]))
     while len(terms) > 1:
         terms = [a + b for a, b in zip(terms[::2], terms[1::2])]
     return terms[0]
@@ -291,9 +293,7 @@
             jnp.concatenate([jnp.sum(squares * (1.0 / row_moment)[:, None], axis=0), jnp.zeros_like(spare)]),
         ]
     )
-    totals = butterfly(totals, "row", [1, 2])
-    for bit in powers(4, n_row):
-        totals = butterfly(totals, "row", [bit])
+    totals = butterfly(butterfly(totals, "row", [1, 2]), "row", powers(4, n_row))
     col_moment, sums = moments(width, totals, col_state)
     sums = butterfly(sums, "col", powers(1, n_col))
     new_weight, update = finish(count_all, sums, row_moment, col_moment, gradient, weight)

time: 146 us -> 145 us (level)
  the two profiles are of different devices: /device:TPU:12 before, /device:TPU:0 now
where the time goes in v3:
time: 145 us
  waiting for transfers between devices  68.8 us (47%)
  starting transfers between devices  55 us (38%)
  Pallas kernels  13.9 us (10%)
  other arithmetic  3.38 us (2%)
  local copies, waits for them, and re-layouts  3.1 us (2%)
    ppermute x16, waiting for transfers between devices, swap(): return lax.ppermute(v, 'row', [(i, i ^ bit) for i in range(n_row)])  33.1 us
    ppermute x5, waiting for transfers between devices, along_z(): lax.ppermute(v, 'row', [(i, (i + 4 * by) % n_row) for i in range(n_row)])  28.1 us
    ppermute x5, starting transfers between devices, along_z(): lax.ppermute(v, 'row', [(i, (i + 4 * by) % n_row) for i in range(n_row)])  19.9 us
    ppermute x16, starting transfers between devices, swap(): return lax.ppermute(v, 'row', [(i, i ^ bit) for i in range(n_row)])  17.7 us
    ppermute x8, starting transfers between devices, butterfly(): terms.append(lax.ppermute(value, axis, [(i, i ^ s) for i in range(n)]))  8.85 us
    all_to_all x1, starting transfers between devices, per_device(): blocks = lax.all_to_all(blocks, 'row', 0, 0, tiled=True)  8.34 us
    ppermute x8, waiting for transfers between devices, butterfly(): terms.append(lax.ppermute(value, axis, [(i, i ^ s) for i in range(n)]))  7.63 us
    pallas_call x1, Pallas kernels, gemm(): pl.pallas_call(gemm_kernel, grid=(cols // width,), out_shape=jax.ShapeDty...  6.07 us
  transfers between devices with their start and end apart: 31, of which 12 were waited for; matrix products, arithmetic and copies ran while one was open for 3% of the time, Pallas kernels for 5%

profile of v3, /device:TPU:0, one launch (start us, length us, event | category | flops | bytes accessed | tf_op | source)
XLA Modules:
  0.0 145.2 jit_solution(16802222752552337399)
XLA Ops:
  0.7 1.6 %copy-done.1 = bf16[128,8192]{1,0:T(8,128)(2,1)S(1)} copy-done((bf16[128,8192]{1,0:T(8,128)(2,1)S(1)}, bf16[128,8192]{1,0:T(8,128)(2,1)}, u32[]{:S(2)}) %copy-start.1) | copy-done | bytes 2097176
  2.3 1.1 pack.1
  3.3 8.3 %all-to-all-start = ((bf16[16,128,256]{2,1,0:T(8,128)(2,1)}), bf16[16,128,256]{2,1,0:T(8,128)(2,1)S(1)}, u32[]{:S(2)}, u32[]{:S(2)}) async-start(bf16[16,128,256]{2,1,0:T(8,128)(2,1)} %pack.1), calls=%async_computation | async-start | bytes 2097152 | tf_op jit(solution)/shard_map/all_to_all | solution.py:273
  11.7 1.9 %collective-permute-start.1 = (bf16[128,2048]{1,0:T(8,128)(2,1)}, bf16[128,2048]{1,0:T(8,128)(2,1)}, u32[]{:S(2)}, u32[]{:S(2)}) collective-permute-start(bf16[128,2048]{1,0:T(8,128)(2,1)} %refs_0_.1), channel_id=1, source_target_pairs={{0,8},{2,10},{4,12},{6,14},{8,16},{10,18},{12,20},{14,22},{16,24},... | collective-permute-start | bytes 1572872 | tf_op jit(solution)/shard_map/ppermute | solution.py:253
  13.6 1.5 %collective-permute-start.4 = (bf16[128,2048]{1,0:T(8,128)(2,1)}, bf16[128,2048]{1,0:T(8,128)(2,1)S(1)}, u32[]{:S(2)}, u32[]{:S(2)}) collective-permute-start(bf16[128,2048]{1,0:T(8,128)(2,1)} %refs_0_.1), channel_id=1, source_target_pairs={{0,2},{2,0},{4,6},{6,4},{8,10},{10,8},{12,14},{14,12},{16,18},{18,... | collective-permute-start | bytes 1572872 | tf_op jit(solution)/shard_map/ppermute | solution.py:250
  15.1 2.4 %collective-permute-start.2 = (bf16[128,2048]{1,0:T(8,128)(2,1)}, bf16[128,2048]{1,0:T(8,128)(2,1)}, u32[]{:S(2)}, u32[]{:S(2)}) collective-permute-start(bf16[128,2048]{1,0:T(8,128)(2,1)} %refs_0_.1), channel_id=1, source_target_pairs={{0,24},{2,26},{4,28},{6,30},{8,0},{10,2},{12,4},{14,6},{16,8},{18,... | collective-permute-start | bytes 1572872 | tf_op jit(solution)/shard_map/ppermute | solution.py:253
  17.4 1.5 %collective-permute-start.5 = (bf16[128,2048]{1,0:T(8,128)(2,1)}, bf16[128,2048]{1,0:T(8,128)(2,1)S(1)}, u32[]{:S(2)}, u32[]{:S(2)}) collective-permute-start(bf16[128,2048]{1,0:T(8,128)(2,1)} %refs_0_.1), channel_id=1, source_target_pairs={{0,4},{2,6},{4,0},{6,2},{8,12},{10,14},{12,8},{14,10},{16,20},{18,... | collective-permute-start | bytes 1572872 | tf_op jit(solution)/shard_map/ppermute | solution.py:250
  18.9 26.4 %collective-permute-done.1.refs_1_ = bf16[128,2048]{1,0:T(8,128)(2,1)} collective-permute-done((bf16[128,2048]{1,0:T(8,128)(2,1)}, bf16[128,2048]{1,0:T(8,128)(2,1)}, u32[]{:S(2)}, u32[]{:S(2)}) %collective-permute-start.1) | collective-permute-done | bytes 524320 | tf_op jit(solution)/shard_map/ppermute | solution.py:253
  45.3 13.2 %collective-permute-start.3 = (bf16[128,2048]{1,0:T(8,128)(2,1)}, bf16[128,2048]{1,0:T(8,128)(2,1)}, u32[]{:S(2)}, u32[]{:S(2)}) collective-permute-start(bf16[128,2048]{1,0:T(8,128)(2,1)} %collective-permute-done.1.refs_1_), channel_id=1, source_target_pairs={{0,8},{2,10},{4,12},{6,14},{8,16},{10,18},{12,20},{14,22},{16,24},... | collective-permute-start | bytes 1572872 | tf_op jit(solution)/shard_map/ppermute | solution.py:253
  58.5 1.5 %collective-permute-start.6 = (bf16[128,2048]{1,0:T(8,128)(2,1)}, bf16[128,2048]{1,0:T(8,128)(2,1)S(1)}, u32[]{:S(2)}, u32[]{:S(2)}) collective-permute-start(bf16[128,2048]{1,0:T(8,128)(2,1)} %collective-permute-done.1.refs_1_), channel_id=1, source_target_pairs={{0,2},{2,0},{4,6},{6,4},{8,10},{10,8},{12,14},{14,12},{16,18},{18,... | collective-permute-start | bytes 1572872 | tf_op jit(solution)/shard_map/ppermute | solution.py:250
  60.0 1.5 %collective-permute-start.7 = (bf16[128,2048]{1,0:T(8,128)(2,1)}, bf16[128,2048]{1,0:T(8,128)(2,1)S(1)}, u32[]{:S(2)}, u32[]{:S(2)}) collective-permute-start(bf16[128,2048]{1,0:T(8,128)(2,1)} %collective-permute-done.1.refs_1_), channel_id=1, source_target_pairs={{0,4},{2,6},{4,0},{6,2},{8,12},{10,14},{12,8},{14,10},{16,20},{18,... | collective-permute-start | bytes 1572872 | tf_op jit(solution)/shard_map/ppermute | solution.py:250
  61.5 0.7 slice.32
  62.2 0.5 collective-permute-start.10
  62.8 0.9 arrange.1.mine_ref
  63.8 14.4 %collective-permute-done.10.refs_10_ = bf16[64,2048]{1,0:T(8,128)(2,1)S(1)} collective-permute-done((bf16[64,2048]{1,0:T(8,128)(2,1)}, bf16[64,2048]{1,0:T(8,128)(2,1)S(1)}, u32[]{:S(2)}, u32[]{:S(2)}) %collective-permute-start.10) | collective-permute-done | bytes 262176 | tf_op jit(solution)/shard_map/ppermute | solution.py:250
  78.2 0.6 collective-permute-start.8
  78.8 1.7 %collective-permute-start.9 = (bf16[128,2048]{1,0:T(8,128)(2,1)}, bf16[128,2048]{1,0:T(8,128)(2,1)S(1)}, u32[]{:S(2)}, u32[]{:S(2)}) collective-permute-start(bf16[128,2048]{1,0:T(8,128)(2,1)} %collective-permute-done.2.refs_2_), channel_id=1, source_target_pairs={{0,4},{2,6},{4,0},{6,2},{8,12},{10,14},{12,8},{14,10},{16,20},{18,... | collective-permute-start | bytes 1572872 | tf_op jit(solution)/shard_map/ppermute | solution.py:250
  80.5 1.5 %collective-permute-start.12 = (bf16[128,2048]{1,0:T(8,128)(2,1)}, bf16[128,2048]{1,0:T(8,128)(2,1)S(1)}, u32[]{:S(2)}, u32[]{:S(2)}) collective-permute-start(bf16[128,2048]{1,0:T(8,128)(2,1)} %collective-permute-done.3.refs_3_), channel_id=1, source_target_pairs={{0,2},{2,0},{4,6},{6,4},{8,10},{10,8},{12,14},{14,12},{16,18},{18,... | collective-permute-start | bytes 1572872 | tf_op jit(solution)/shard_map/ppermute | solution.py:250
  82.0 0.3 collective-permute-start.13
  82.3 10.9 %collective-permute-done.8.refs_8_ = bf16[128,2048]{1,0:T(8,128)(2,1)S(1)} collective-permute-done((bf16[128,2048]{1,0:T(8,128)(2,1)}, bf16[128,2048]{1,0:T(8,128)(2,1)S(1)}, u32[]{:S(2)}, u32[]{:S(2)}) %collective-permute-start.8) | collective-permute-done | bytes 524320 | tf_op jit(solution)/shard_map/ppermute | solution.py:250
  93.2 0.6 collective-permute-start.11
  93.8 2.5 %collective-permute-start.14 = (bf16[64,2048]{1,0:T(8,128)(2,1)S(1)}, bf16[64,2048]{1,0:T(8,128)(2,1)S(1)}, u32[]{:S(2)}, u32[]{:S(2)}) collective-permute-start(bf16[64,2048]{1,0:T(8,128)(2,1)S(1)} %collective-permute-done.10.refs_10_), channel_id=1, source_target_pairs={{0,8},{2,10},{4,12},{6,14},{8,16},{10,18},{12,20},{14,22},{16,24},... | collective-permute-start | bytes 786440 | tf_op jit(solution)/shard_map/ppermute | solution.py:253
  96.3 7.7 %collective-permute-done.12.refs_0_ = bf16[128,2048]{1,0:T(8,128)(2,1)S(1)} collective-permute-done((bf16[128,2048]{1,0:T(8,128)(2,1)}, bf16[128,2048]{1,0:T(8,128)(2,1)S(1)}, u32[]{:S(2)}, u32[]{:S(2)}) %collective-permute-start.12) | collective-permute-done | bytes 524320 | tf_op jit(solution)/shard_map/ppermute | solution.py:250
  104.0 1.9 %collective-permute-start.15 = (bf16[32,2048]{1,0:T(8,128)(2,1)S(1)}, bf16[32,2048]{1,0:T(8,128)(2,1)S(1)}, u32[]{:S(2)}, u32[]{:S(2)}) collective-permute-start(bf16[32,2048]{1,0:T(8,128)(2,1)S(1)} %slice.34), channel_id=1, source_target_pairs={{0,4},{2,6},{4,0},{6,2},{8,12},{10,14},{12,8},{14,10},{16,20},{18,... | collective-permute-start | bytes 393224 | tf_op jit(solution)/shard_map/ppermute | solution.py:250
  105.9 2.6 %multiply_reduce_fusion.1 = f32[2048]{0:T(1024)S(1)} fusion(f32[512,2048]{1,0:T(8,128)} %weight_ref.1), kind=kLoop, calls=%fused_computation.1 | loop fusion | flops 2095104 | bytes 4202496 | tf_op jit(solution)/shard_map/reduce_sum | solution.py:288
  108.6 0.6 collective-permute-start.16
  109.2 0.4 collective-permute-start.18
  109.6 1.6 %collective-permute-done.17.refs_5_ = bf16[64,2048]{1,0:T(8,128)(2,1)S(1)} collective-permute-done((bf16[64,2048]{1,0:T(8,128)(2,1)S(1)}, bf16[64,2048]{1,0:T(8,128)(2,1)S(1)}, u32[]{:S(2)}, u32[]{:S(2)}) %collective-permute-start.17) | collective-permute-done | bytes 262176 | tf_op jit(solution)/shard_map/ppermute | solution.py:253
  111.3 0.6 collective-permute-start.19
  111.8 1.7 %collective-permute-start.20 = (bf16[64,2048]{1,0:T(8,128)(2,1)S(1)}, bf16[64,2048]{1,0:T(8,128)(2,1)S(1)}, u32[]{:S(2)}, u32[]{:S(2)}) collective-permute-start(bf16[64,2048]{1,0:T(8,128)(2,1)S(1)} %slice.38), channel_id=1, source_target_pairs={{0,4},{2,6},{4,0},{6,2},{8,12},{10,14},{12,8},{14,10},{16,20},{18,... | collective-permute-start | bytes 786440 | tf_op jit(solution)/shard_map/ppermute | solution.py:250
  113.6 1.5 %collective-permute-start.21 = (bf16[64,2048]{1,0:T(8,128)(2,1)S(1)}, bf16[64,2048]{1,0:T(8,128)(2,1)S(1)}, u32[]{:S(2)}, u32[]{:S(2)}) collective-permute-start(bf16[64,2048]{1,0:T(8,128)(2,1)S(1)} %slice.39), channel_id=1, source_target_pairs={{0,2},{2,0},{4,6},{6,4},{8,10},{10,8},{12,14},{14,12},{16,18},{18,... | collective-permute-start | bytes 786440 | tf_op jit(solution)/shard_map/ppermute | solution.py:250
  115.1 6.1 %gemm.1.before_ref = f32[512,2048]{1,0:T(8,128)S(1)} custom-call(s32[1]{0:T(128)} %bitcast.side_ref, bf16[256,2048]{1,0:T(8,128)(2,1)S(1)} %arrange.1.mine_ref, bf16[256,2048]{1,0:T(8,128)(2,1)S(1)} %collective-permute-done.other_ref, bf16[128,2048]{1,0:T(8,128)(2,1)} %refs_0_.1, bf16[128,2048]{1,0:T(8,128)(2,1)} %collective-permute-done.1.refs_1_, ...), custom_call_target="tpu_custom_call" | custom-call | flops 2952790016 | bytes 5767168 | tf_op jit(solution)/shard_map/gemm/pallas_call | solution.py:116
  121.2 2.0 %last_gemm.1 = (f32[512,2048]{1,0:T(8,128)S(1)}, f32[1,512]{1,0:T(1,128)S(1)}) custom-call(s32[1]{0:T(128)} %bitcast.side_ref, bf16[256,2048]{1,0:T(8,128)(2,1)S(1)} %arrange.1.mine_ref, bf16[256,2048]{1,0:T(8,128)(2,1)S(1)} %collective-permute-done.other_ref, f32[512,2048]{1,0:T(8,128)S(1)} %gemm.1.before_ref, ...), custom_call_target="tpu_custom_call" | custom-call | flops 1342177280 | bytes 2621440 | tf_op jit(solution)/shard_map/last_gemm/pallas_call | solution.py:156
  123.4 1.1 collective-permute-done.22
  124.5 0.7 add_reduce_fusion
  125.3 0.6 collective-permute-start.23
  126.0 0.3 collective-permute-start.24
  126.3 2.6 %collective-permute-start.25 = (f32[2,2176]{1,0:T(2,128)S(1)}, f32[2,2176]{1,0:T(2,128)S(1)}, u32[]{:S(2)}, u32[]{:S(2)}) collective-permute-start(f32[2,2176]{1,0:T(2,128)S(1)} %pad_maximum_fusion), channel_id=1, source_target_pairs={{0,6},{2,4},{4,2},{6,0},{8,14},{10,12},{12,10},{14,8},{16,22},{18,... | collective-permute-start | bytes 52232 | tf_op jit(solution)/shard_map/ppermute | solution.py:27
  129.2 0.6 collective-permute-done.24
  129.7 1.2 collective-permute-done.25
  131.0 2.7 %collective-permute-start.26 = (f32[2,2176]{1,0:T(2,128)S(1)}, f32[2,2176]{1,0:T(2,128)S(1)}, u32[]{:S(2)}, u32[]{:S(2)}) collective-permute-start(f32[2,2176]{1,0:T(2,128)S(1)} %add_add_fusion.1), channel_id=1, source_target_pairs={{0,8},{2,10},{4,12},{6,14},{8,0},{10,2},{12,4},{14,6},{16,24},{18,... | collective-permute-start | bytes 52232 | tf_op jit(solution)/shard_map/ppermute | solution.py:27
  133.7 0.8 collective-permute-start.27
  134.5 1.6 %collective-permute-start.28 = (f32[2,2176]{1,0:T(2,128)S(1)}, f32[2,2176]{1,0:T(2,128)S(1)}, u32[]{:S(2)}, u32[]{:S(2)}) collective-permute-start(f32[2,2176]{1,0:T(2,128)S(1)} %add_add_fusion.1), channel_id=1, source_target_pairs={{0,24},{2,26},{4,28},{6,30},{8,16},{10,18},{12,20},{14,22},{16,8},... | collective-permute-start | bytes 52232 | tf_op jit(solution)/shard_map/ppermute | solution.py:27
  136.1 2.2 %collective-permute-done.27 = f32[2,2176]{1,0:T(2,128)S(1)} collective-permute-done((f32[2,2176]{1,0:T(2,128)S(1)}, f32[2,2176]{1,0:T(2,128)S(1)}, u32[]{:S(2)}, u32[]{:S(2)}) %collective-permute-start.27) | collective-permute-done | bytes 17440 | tf_op jit(solution)/shard_map/ppermute | solution.py:27
  138.3 1.7 %collective-permute-done.28 = f32[2,2176]{1,0:T(2,128)S(1)} collective-permute-done((f32[2,2176]{1,0:T(2,128)S(1)}, f32[2,2176]{1,0:T(2,128)S(1)}, u32[]{:S(2)}, u32[]{:S(2)}) %collective-permute-start.28) | collective-permute-done | bytes 17440 | tf_op jit(solution)/shard_map/ppermute | solution.py:27
  140.3 0.6 copy.11
  140.9 0.6 collective-permute-done.29
  141.5 3.7 %finish.1 = (f32[512,2048]{1,0:T(8,128)}, f32[512,2048]{1,0:T(8,128)}) custom-call(f32[8,128]{1,0:T(8,128)S(1)} %add.74.sums_ref, f32[1,512]{1,0:T(1,128)S(1)} %bitcast.8, f32[1,2048]{1,0:T(1,128)S(1)} %get-tuple-element.13.col_ref, f32[512,2048]{1,0:T(8,128)S(1)} %get-tuple-element.10.gradient_ref, f32[512,2048]{1,0:T(8,128)S(1)} %copy-done), custom_call_target="tpu_custom_call" | custom-call | flops 4194304 | bytes 16777216 | tf_op jit(solution)/shard_map/finish/pallas_call | solution.py:219
  (72 shorter events, 1.0 us)
Async XLA Ops:
  0.6 62.1 %copy-start.13 = (s32[16]{0:T(128)S(1)}, s32[16]{0:T(128)}, u32[]{:S(2)}) copy-start(s32[16]{0:T(128)} %constant.65.clone) | copy-start | bytes 196
  0.6 62.1 %copy-start.14 = (s32[16]{0:T(128)S(1)}, s32[16]{0:T(128)}, u32[]{:S(2)}) copy-start(s32[16]{0:T(128)} %constant.66.clone) | copy-start | bytes 196
  0.7 1.6 %copy-start.1 = (bf16[128,8192]{1,0:T(8,128)(2,1)S(1)}, bf16[128,8192]{1,0:T(8,128)(2,1)}, u32[]{:S(2)}) copy-start(bf16[128,8192]{1,0:T(8,128)(2,1)} %acts_ref.1) | copy-start | bytes 6291460
  3.3 59.4 %all-to-all-start = ((bf16[16,128,256]{2,1,0:T(8,128)(2,1)}), bf16[16,128,256]{2,1,0:T(8,128)(2,1)S(1)}, u32[]{:S(2)}, u32[]{:S(2)}) async-start(bf16[16,128,256]{2,1,0:T(8,128)(2,1)} %pack.1), calls=%async_computation | async-start | bytes 2097152 | tf_op jit(solution)/shard_map/all_to_all | solution.py:273
  11.7 33.7 %collective-permute-start.1 = (bf16[128,2048]{1,0:T(8,128)(2,1)}, bf16[128,2048]{1,0:T(8,128)(2,1)}, u32[]{:S(2)}, u32[]{:S(2)}) collective-permute-start(bf16[128,2048]{1,0:T(8,128)(2,1)} %refs_0_.1), channel_id=1, source_target_pairs={{0,8},{2,10},{4,12},{6,14},{8,16},{10,18},{12,20},{14,22},{16,24},... | collective-permute-start | bytes 1572872 | tf_op jit(solution)/shard_map/ppermute | solution.py:253
  13.6 46.4 %collective-permute-start.4 = (bf16[128,2048]{1,0:T(8,128)(2,1)}, bf16[128,2048]{1,0:T(8,128)(2,1)S(1)}, u32[]{:S(2)}, u32[]{:S(2)}) collective-permute-start(bf16[128,2048]{1,0:T(8,128)(2,1)} %refs_0_.1), channel_id=1, source_target_pairs={{0,2},{2,0},{4,6},{6,4},{8,10},{10,8},{12,14},{14,12},{16,18},{18,... | collective-permute-start | bytes 1572872 | tf_op jit(solution)/shard_map/ppermute | solution.py:250
  15.1 47.2 %collective-permute-start.2 = (bf16[128,2048]{1,0:T(8,128)(2,1)}, bf16[128,2048]{1,0:T(8,128)(2,1)}, u32[]{:S(2)}, u32[]{:S(2)}) collective-permute-start(bf16[128,2048]{1,0:T(8,128)(2,1)} %refs_0_.1), channel_id=1, source_target_pairs={{0,24},{2,26},{4,28},{6,30},{8,0},{10,2},{12,4},{14,6},{16,8},{18,... | collective-permute-start | bytes 1572872 | tf_op jit(solution)/shard_map/ppermute | solution.py:253
  17.4 46.3 %collective-permute-start.5 = (bf16[128,2048]{1,0:T(8,128)(2,1)}, bf16[128,2048]{1,0:T(8,128)(2,1)S(1)}, u32[]{:S(2)}, u32[]{:S(2)}) collective-permute-start(bf16[128,2048]{1,0:T(8,128)(2,1)} %refs_0_.1), channel_id=1, source_target_pairs={{0,4},{2,6},{4,0},{6,2},{8,12},{10,14},{12,8},{14,10},{16,20},{18,... | collective-permute-start | bytes 1572872 | tf_op jit(solution)/shard_map/ppermute | solution.py:250
  45.3 33.4 %collective-permute-start.3 = (bf16[128,2048]{1,0:T(8,128)(2,1)}, bf16[128,2048]{1,0:T(8,128)(2,1)}, u32[]{:S(2)}, u32[]{:S(2)}) collective-permute-start(bf16[128,2048]{1,0:T(8,128)(2,1)} %collective-permute-done.1.refs_1_), channel_id=1, source_target_pairs={{0,8},{2,10},{4,12},{6,14},{8,16},{10,18},{12,20},{14,22},{16,24},... | collective-permute-start | bytes 1572872 | tf_op jit(solution)/shard_map/ppermute | solution.py:253
  58.5 22.0 %collective-permute-start.6 = (bf16[128,2048]{1,0:T(8,128)(2,1)}, bf16[128,2048]{1,0:T(8,128)(2,1)S(1)}, u32[]{:S(2)}, u32[]{:S(2)}) collective-permute-start(bf16[128,2048]{1,0:T(8,128)(2,1)} %collective-permute-done.1.refs_1_), channel_id=1, source_target_pairs={{0,2},{2,0},{4,6},{6,4},{8,10},{10,8},{12,14},{14,12},{16,18},{18,... | collective-permute-start | bytes 1572872 | tf_op jit(solution)/shard_map/ppermute | solution.py:250
  60.0 48.5 %copy-start.4 = (bf16[128,2048]{1,0:T(8,128)(2,1)}, bf16[128,2048]{1,0:T(8,128)(2,1)S(1)}, u32[]{:S(2)}) copy-start(bf16[128,2048]{1,0:T(8,128)(2,1)S(1)} %collective-permute-done.4.refs_4_) | copy-start | bytes 1572868
  60.0 22.0 %collective-permute-start.7 = (bf16[128,2048]{1,0:T(8,128)(2,1)}, bf16[128,2048]{1,0:T(8,128)(2,1)S(1)}, u32[]{:S(2)}, u32[]{:S(2)}) collective-permute-start(bf16[128,2048]{1,0:T(8,128)(2,1)} %collective-permute-done.1.refs_1_), channel_id=1, source_target_pairs={{0,4},{2,6},{4,0},{6,2},{8,12},{10,14},{12,8},{14,10},{16,20},{18,... | collective-permute-start | bytes 1572872 | tf_op jit(solution)/shard_map/ppermute | solution.py:250
  62.2 16.0 %collective-permute-start.10 = (bf16[64,2048]{1,0:T(8,128)(2,1)}, bf16[64,2048]{1,0:T(8,128)(2,1)S(1)}, u32[]{:S(2)}, u32[]{:S(2)}) collective-permute-start(bf16[64,2048]{1,0:T(8,128)(2,1)} %slice.32), channel_id=1, source_target_pairs={{0,4},{2,6},{4,0},{6,2},{8,12},{10,14},{12,8},{14,10},{16,20},{18,... | collective-permute-start | bytes 786440 | tf_op jit(solution)/shard_map/ppermute | solution.py:250
  63.7 51.3 %copy-start.5 = (bf16[128,2048]{1,0:T(8,128)(2,1)}, bf16[128,2048]{1,0:T(8,128)(2,1)S(1)}, u32[]{:S(2)}) copy-start(bf16[128,2048]{1,0:T(8,128)(2,1)S(1)} %collective-permute-done.5.refs_5_) | copy-start | bytes 1572868
  63.7 49.9 %collective-permute-start = (bf16[256,2048]{1,0:T(8,128)(2,1)S(1)}, bf16[256,2048]{1,0:T(8,128)(2,1)S(1)}, u32[]{:S(2)}, u32[]{:S(2)}) collective-permute-start(bf16[256,2048]{1,0:T(8,128)(2,1)S(1)} %arrange.1.mine_ref), channel_id=1, source_target_pairs={{0,1},{1,0},{2,3},{3,2},{4,5},{5,4},{6,7},{7,6},{8,9},{9,8},{10,11... | collective-permute-start | bytes 3145736 | tf_op jit(solution)/shard_map/ppermute | solution.py:280
  78.2 36.8 %copy-start.10 = (bf16[64,2048]{1,0:T(8,128)(2,1)}, bf16[64,2048]{1,0:T(8,128)(2,1)S(1)}, u32[]{:S(2)}) copy-start(bf16[64,2048]{1,0:T(8,128)(2,1)S(1)} %collective-permute-done.10.refs_10_) | copy-start | bytes 786436
  78.2 15.0 %collective-permute-start.8 = (bf16[128,2048]{1,0:T(8,128)(2,1)}, bf16[128,2048]{1,0:T(8,128)(2,1)S(1)}, u32[]{:S(2)}, u32[]{:S(2)}) collective-permute-start(bf16[128,2048]{1,0:T(8,128)(2,1)} %collective-permute-done.2.refs_2_), channel_id=1, source_target_pairs={{0,2},{2,0},{4,6},{6,4},{8,10},{10,8},{12,14},{14,12},{16,18},{18,... | collective-permute-start | bytes 1572872 | tf_op jit(solution)/shard_map/ppermute | solution.py:250
  78.8 15.0 %collective-permute-start.9 = (bf16[128,2048]{1,0:T(8,128)(2,1)}, bf16[128,2048]{1,0:T(8,128)(2,1)S(1)}, u32[]{:S(2)}, u32[]{:S(2)}) collective-permute-start(bf16[128,2048]{1,0:T(8,128)(2,1)} %collective-permute-done.2.refs_2_), channel_id=1, source_target_pairs={{0,4},{2,6},{4,0},{6,2},{8,12},{10,14},{12,8},{14,10},{16,20},{18,... | collective-permute-start | bytes 1572872 | tf_op jit(solution)/shard_map/ppermute | solution.py:250
  80.5 34.5 %copy-start.6 = (bf16[128,2048]{1,0:T(8,128)(2,1)}, bf16[128,2048]{1,0:T(8,128)(2,1)S(1)}, u32[]{:S(2)}) copy-start(bf16[128,2048]{1,0:T(8,128)(2,1)S(1)} %collective-permute-done.6.refs_6_) | copy-start | bytes 1572868
  80.5 23.5 %collective-permute-start.12 = (bf16[128,2048]{1,0:T(8,128)(2,1)}, bf16[128,2048]{1,0:T(8,128)(2,1)S(1)}, u32[]{:S(2)}, u32[]{:S(2)}) collective-permute-start(bf16[128,2048]{1,0:T(8,128)(2,1)} %collective-permute-done.3.refs_3_), channel_id=1, source_target_pairs={{0,2},{2,0},{4,6},{6,4},{8,10},{10,8},{12,14},{14,12},{16,18},{18,... | collective-permute-start | bytes 1572872 | tf_op jit(solution)/shard_map/ppermute | solution.py:250
  82.0 33.1 %copy-start.7 = (bf16[128,2048]{1,0:T(8,128)(2,1)}, bf16[128,2048]{1,0:T(8,128)(2,1)S(1)}, u32[]{:S(2)}) copy-start(bf16[128,2048]{1,0:T(8,128)(2,1)S(1)} %collective-permute-done.7.refs_7_) | copy-start | bytes 1572868
  82.0 22.0 %collective-permute-start.13 = (bf16[128,2048]{1,0:T(8,128)(2,1)}, bf16[128,2048]{1,0:T(8,128)(2,1)S(1)}, u32[]{:S(2)}, u32[]{:S(2)}) collective-permute-start(bf16[128,2048]{1,0:T(8,128)(2,1)} %collective-permute-done.3.refs_3_), channel_id=1, source_target_pairs={{0,4},{2,6},{4,0},{6,2},{8,12},{10,14},{12,8},{14,10},{16,20},{18,... | collective-permute-start | bytes 1572872 | tf_op jit(solution)/shard_map/ppermute | solution.py:250
  93.2 21.8 %copy-start.8 = (bf16[128,2048]{1,0:T(8,128)(2,1)}, bf16[128,2048]{1,0:T(8,128)(2,1)S(1)}, u32[]{:S(2)}) copy-start(bf16[128,2048]{1,0:T(8,128)(2,1)S(1)} %collective-permute-done.8.refs_8_) | copy-start | bytes 1572868
  93.2 15.4 %collective-permute-start.11 = (bf16[64,2048]{1,0:T(8,128)(2,1)S(1)}, bf16[64,2048]{1,0:T(8,128)(2,1)S(1)}, u32[]{:S(2)}, u32[]{:S(2)}) collective-permute-start(bf16[64,2048]{1,0:T(8,128)(2,1)S(1)} %slice.33), channel_id=1, source_target_pairs={{0,2},{2,0},{4,6},{6,4},{8,10},{10,8},{12,14},{14,12},{16,18},{18,... | collective-permute-start | bytes 786440 | tf_op jit(solution)/shard_map/ppermute | solution.py:250
  93.8 21.3 %copy-start.9 = (bf16[128,2048]{1,0:T(8,128)(2,1)}, bf16[128,2048]{1,0:T(8,128)(2,1)S(1)}, u32[]{:S(2)}) copy-start(bf16[128,2048]{1,0:T(8,128)(2,1)S(1)} %collective-permute-done.9.refs_9_) | copy-start | bytes 1572868
  93.8 15.4 %collective-permute-start.14 = (bf16[64,2048]{1,0:T(8,128)(2,1)S(1)}, bf16[64,2048]{1,0:T(8,128)(2,1)S(1)}, u32[]{:S(2)}, u32[]{:S(2)}) collective-permute-start(bf16[64,2048]{1,0:T(8,128)(2,1)S(1)} %collective-permute-done.10.refs_10_), channel_id=1, source_target_pairs={{0,8},{2,10},{4,12},{6,14},{8,16},{10,18},{12,20},{14,22},{16,24},... | collective-permute-start | bytes 786440 | tf_op jit(solution)/shard_map/ppermute | solution.py:253
  104.0 7.3 %collective-permute-start.17 = (bf16[64,2048]{1,0:T(8,128)(2,1)S(1)}, bf16[64,2048]{1,0:T(8,128)(2,1)S(1)}, u32[]{:S(2)}, u32[]{:S(2)}) collective-permute-start(bf16[64,2048]{1,0:T(8,128)(2,1)S(1)} %collective-permute-done.10.refs_10_), channel_id=1, source_target_pairs={{0,24},{2,26},{4,28},{6,30},{8,0},{10,2},{12,4},{14,6},{16,8},{18,... | collective-permute-start | bytes 786440 | tf_op jit(solution)/shard_map/ppermute | solution.py:253
  104.0 7.9 %collective-permute-start.15 = (bf16[32,2048]{1,0:T(8,128)(2,1)S(1)}, bf16[32,2048]{1,0:T(8,128)(2,1)S(1)}, u32[]{:S(2)}, u32[]{:S(2)}) collective-permute-start(bf16[32,2048]{1,0:T(8,128)(2,1)S(1)} %slice.34), channel_id=1, source_target_pairs={{0,4},{2,6},{4,0},{6,2},{8,12},{10,14},{12,8},{14,10},{16,20},{18,... | collective-permute-start | bytes 393224 | tf_op jit(solution)/shard_map/ppermute | solution.py:250
  108.6 6.5 %copy-start.11 = (bf16[64,2048]{1,0:T(8,128)(2,1)}, bf16[64,2048]{1,0:T(8,128)(2,1)S(1)}, u32[]{:S(2)}) copy-start(bf16[64,2048]{1,0:T(8,128)(2,1)S(1)} %collective-permute-done.11.refs_11_) | copy-start | bytes 786436
  108.6 12.6 %collective-permute-start.16 = (bf16[32,2048]{1,0:T(8,128)(2,1)S(1)}, bf16[32,2048]{1,0:T(8,128)(2,1)S(1)}, u32[]{:S(2)}, u32[]{:S(2)}) collective-permute-start(bf16[32,2048]{1,0:T(8,128)(2,1)S(1)} %slice.35), channel_id=1, source_target_pairs={{0,2},{2,0},{4,6},{6,4},{8,10},{10,8},{12,14},{14,12},{16,18},{18,... | collective-permute-start | bytes 393224 | tf_op jit(solution)/shard_map/ppermute | solution.py:250
  109.2 11.9 %collective-permute-start.18 = (bf16[32,2048]{1,0:T(8,128)(2,1)S(1)}, bf16[32,2048]{1,0:T(8,128)(2,1)S(1)}, u32[]{:S(2)}, u32[]{:S(2)}) collective-permute-start(bf16[32,2048]{1,0:T(8,128)(2,1)S(1)} %slice.36), channel_id=1, source_target_pairs={{0,4},{2,6},{4,0},{6,2},{8,12},{10,14},{12,8},{14,10},{16,20},{18,... | collective-permute-start | bytes 393224 | tf_op jit(solution)/shard_map/ppermute | solution.py:250
  111.3 9.9 %collective-permute-start.19 = (bf16[32,2048]{1,0:T(8,128)(2,1)S(1)}, bf16[32,2048]{1,0:T(8,128)(2,1)S(1)}, u32[]{:S(2)}, u32[]{:S(2)}) collective-permute-start(bf16[32,2048]{1,0:T(8,128)(2,1)S(1)} %slice.37), channel_id=1, source_target_pairs={{0,2},{2,0},{4,6},{6,4},{8,10},{10,8},{12,14},{14,12},{16,18},{18,... | collective-permute-start | bytes 393224 | tf_op jit(solution)/shard_map/ppermute | solution.py:250
  111.8 9.3 %collective-permute-start.20 = (bf16[64,2048]{1,0:T(8,128)(2,1)S(1)}, bf16[64,2048]{1,0:T(8,128)(2,1)S(1)}, u32[]{:S(2)}, u32[]{:S(2)}) collective-permute-start(bf16[64,2048]{1,0:T(8,128)(2,1)S(1)} %slice.38), channel_id=1, source_target_pairs={{0,4},{2,6},{4,0},{6,2},{8,12},{10,14},{12,8},{14,10},{16,20},{18,... | collective-permute-start | bytes 786440 | tf_op jit(solution)/shard_map/ppermute | solution.py:250
  113.6 7.6 %collective-permute-start.21 = (bf16[64,2048]{1,0:T(8,128)(2,1)S(1)}, bf16[64,2048]{1,0:T(8,128)(2,1)S(1)}, u32[]{:S(2)}, u32[]{:S(2)}) collective-permute-start(bf16[64,2048]{1,0:T(8,128)(2,1)S(1)} %slice.39), channel_id=1, source_target_pairs={{0,2},{2,0},{4,6},{6,4},{8,10},{10,8},{12,14},{14,12},{16,18},{18,... | collective-permute-start | bytes 786440 | tf_op jit(solution)/shard_map/ppermute | solution.py:250
  121.1 3.4 %copy-start.12 = (f32[512]{0:T(512)S(1)}, f32[512]{0:T(512)}, u32[]{:S(2)}) copy-start(f32[512]{0:T(512)} %param.10) | copy-start | bytes 6148
  123.3 16.8 %copy-start.3 = (f32[2048]{0:T(1024)S(1)}, f32[2048]{0:T(1024)}, u32[]{:S(2)}) copy-start(f32[2048]{0:T(1024)} %param.11) | copy-start | bytes 24580
  123.3 18.2 %copy-start = (f32[512,2048]{1,0:T(8,128)S(1)}, f32[512,2048]{1,0:T(8,128)}, u32[]{:S(2)}) copy-start(f32[512,2048]{1,0:T(8,128)} %weight_ref.1) | copy-start | bytes 12582916
  123.3 1.2 collective-permute-start.22
  124.5 20.6 %copy-start.2 = (f32[512]{0:T(512)}, f32[512]{0:T(512)S(1)}, u32[]{:S(2)}) copy-start(f32[512]{0:T(512)S(1)} %get-tuple-element.22) | copy-start | bytes 6148
  125.3 3.8 %collective-permute-start.23 = (f32[2,2176]{1,0:T(2,128)S(1)}, f32[2,2176]{1,0:T(2,128)S(1)}, u32[]{:S(2)}, u32[]{:S(2)}) collective-permute-start(f32[2,2176]{1,0:T(2,128)S(1)} %pad_maximum_fusion), channel_id=1, source_target_pairs={{0,2},{2,0},{4,6},{6,4},{8,10},{10,8},{12,14},{14,12},{16,18},{18,... | collective-permute-start | bytes 52232 | tf_op jit(solution)/shard_map/ppermute | solution.py:27
  126.0 3.8 %collective-permute-start.24 = (f32[2,2176]{1,0:T(2,128)S(1)}, f32[2,2176]{1,0:T(2,128)S(1)}, u32[]{:S(2)}, u32[]{:S(2)}) collective-permute-start(f32[2,2176]{1,0:T(2,128)S(1)} %pad_maximum_fusion), channel_id=1, source_target_pairs={{0,4},{2,6},{4,0},{6,2},{8,12},{10,14},{12,8},{14,10},{16,20},{18,... | collective-permute-start | bytes 52232 | tf_op jit(solution)/shard_map/ppermute | solution.py:27
  126.3 4.6 %collective-permute-start.25 = (f32[2,2176]{1,0:T(2,128)S(1)}, f32[2,2176]{1,0:T(2,128)S(1)}, u32[]{:S(2)}, u32[]{:S(2)}) collective-permute-start(f32[2,2176]{1,0:T(2,128)S(1)} %pad_maximum_fusion), channel_id=1, source_target_pairs={{0,6},{2,4},{4,2},{6,0},{8,14},{10,12},{12,10},{14,8},{16,22},{18,... | collective-permute-start | bytes 52232 | tf_op jit(solution)/shard_map/ppermute | solution.py:27
  131.0 5.2 %collective-permute-start.26 = (f32[2,2176]{1,0:T(2,128)S(1)}, f32[2,2176]{1,0:T(2,128)S(1)}, u32[]{:S(2)}, u32[]{:S(2)}) collective-permute-start(f32[2,2176]{1,0:T(2,128)S(1)} %add_add_fusion.1), channel_id=1, source_target_pairs={{0,8},{2,10},{4,12},{6,14},{8,0},{10,2},{12,4},{14,6},{16,24},{18,... | collective-permute-start | bytes 52232 | tf_op jit(solution)/shard_map/ppermute | solution.py:27
  133.7 4.6 %collective-permute-start.27 = (f32[2,2176]{1,0:T(2,128)S(1)}, f32[2,2176]{1,0:T(2,128)S(1)}, u32[]{:S(2)}, u32[]{:S(2)}) collective-permute-start(f32[2,2176]{1,0:T(2,128)S(1)} %add_add_fusion.1), channel_id=1, source_target_pairs={{0,16},{2,18},{4,20},{6,22},{8,24},{10,26},{12,28},{14,30},{16,0},... | collective-permute-start | bytes 52232 | tf_op jit(solution)/shard_map/ppermute | solution.py:27
  134.5 5.5 %collective-permute-start.28 = (f32[2,2176]{1,0:T(2,128)S(1)}, f32[2,2176]{1,0:T(2,128)S(1)}, u32[]{:S(2)}, u32[]{:S(2)}) collective-permute-start(f32[2,2176]{1,0:T(2,128)S(1)} %add_add_fusion.1), channel_id=1, source_target_pairs={{0,24},{2,26},{4,28},{6,30},{8,16},{10,18},{12,20},{14,22},{16,8},... | collective-permute-start | bytes 52232 | tf_op jit(solution)/shard_map/ppermute | solution.py:27
  140.2 1.2 collective-permute-start.29

commit v4 on v3

--- a/solution.py
+++ b/solution.py
@@ -99,31 +99,45 @@
 
 
 def gemm_kernel(side_ref, mine_ref, other_ref, *refs):
-    *pieces, out_ref, slab = refs
-    depth = slab.shape[0]
+    *pieces, out_ref, slab, sems = refs
+    depth, cols = slab.shape
     height = mine_ref.shape[0]
-    fill(slab, pieces, slice(None))
-    for at, columns_ref in ((side_ref[0], mine_ref), (1 - side_ref[0], other_ref)):
-        rows = pl.ds(pl.multiple_of(at * height, height), height)
-        out_ref[rows, :] = jnp.dot(columns_ref[:, :depth], slab[...], preferred_element_type=jnp.float32)
+    width = min(512, cols)
+    blocks = [slice(t, t + width) for t in range(0, cols, width)]
+    copies = []
+    for t, lanes in enumerate(blocks):
+        at = 0
+        for p, piece in enumerate(pieces):
+            here = slice(at, at + piece.shape[0])
+            sem = sems.at[t * len(pieces) + p]
+            copies.append(pltpu.make_async_copy(piece.at[:, lanes], slab.at[here, lanes], sem))
+            copies[-1].start()
+            at += piece.shape[0]
+    for t, lanes in enumerate(blocks):
+        for copy in copies[t * len(pieces) : (t + 1) * len(pieces)]:
+            copy.wait()
+        for at, columns_ref in ((side_ref[0], mine_ref), (1 - side_ref[0], other_ref)):
+            rows = pl.ds(pl.multiple_of(at * height, height), height)
+            out_ref[rows, lanes] = jnp.dot(columns_ref[:, :depth], slab[:, lanes], preferred_element_type=jnp.float32)
 
 
 def gemm(side, mine, other, pieces):
     rows = 2 * mine.shape[0]
     depth = sum(p.shape[0] for p in pieces)
     cols = pieces[0].shape[1]
-    width = min(512, cols)
     return pl.pallas_call(
         gemm_kernel,
-        grid=(cols // width,),
-        out_shape=jax.ShapeDtypeStruct((rows, cols), jnp.float32),
-        in_specs=[SCALARS, WHOLE, WHOLE] + [pl.BlockSpec((p.shape[0], width), lambda j: (0, j)) for p in pieces],
-        out_specs=pl.BlockSpec((rows, width), lambda j: (0, j)),
-        scratch_shapes=[pltpu.VMEM((depth, width), jnp.bfloat16)],
+        out_shape=pltpu.VMEM((rows, cols), jnp.float32),
+        in_specs=[SCALARS, WHOLE, WHOLE] + [pl.BlockSpec(memory_space=pl.ANY)] * (len(pieces) - 2) + [WHOLE] * 2,
+        out_specs=WHOLE,
+        scratch_shapes=[
+            pltpu.VMEM((depth, cols), jnp.bfloat16),
+            pltpu.SemaphoreType.DMA((len(pieces) * pl.cdiv(cols, 512),)),
+        ],
         compiler_params=pltpu.CompilerParams(vmem_limit_bytes=24 << 20),
         cost_estimate=pl.CostEstimate(flops=2 * rows * depth * cols, bytes_accessed=2 * depth * cols, transcendentals=0),
         name="gemm",
-    )(side, *in_vmem(mine, other), *placed(pltpu.HBM, pieces))
+    )(side, *in_vmem(mine, other), *placed(pltpu.HBM, pieces[:-2]), *in_vmem(*pieces[-2:]))
 
 
 def last_kernel(side_ref, mine_ref, other_ref, before_ref, *refs):
@@ -162,7 +176,7 @@
         compiler_params=pltpu.CompilerParams(vmem_limit_bytes=24 << 20),
         cost_estimate=pl.CostEstimate(flops=2 * rows * depth * cols, bytes_accessed=2 * depth * cols, transcendentals=0),
         name="last_gemm",
-    )(side, *in_vmem(mine, other, before, *pieces[:2]), *pieces[2:])
+    )(side, *in_vmem(mine, other, before), *pieces)
 
 
 def moments_kernel(height, totals_ref, state_ref, col_ref, sums_ref):
@@ -272,8 +286,8 @@
     blocks = pack(side, acts, n_row)
     blocks = lax.all_to_all(blocks, "row", 0, 0, tiled=True)
     *sooner, last = planes = [0] + planes_of(depth)
-    early = [(k, 0) for k in planes] + [(k, j) for k in sooner for j in (1, 2)] + [(0, 3)]
-    late = [(last, 1), (last, 2)] + [(k, 3) for k in planes[1:]]
+    early = [(k, 0) for k in planes] + [(k, j) for k in sooner for j in (1, 2)] + [(0, 3), (last, 1), (last, 2)]
+    late = [(k, 3) for k in planes[1:]]
     below = jnp.array([(-k % depth) * 4 for k, _ in early + late], jnp.int32)
     place = jnp.array([j for _, j in early + late], jnp.int32)
     mine = arrange((me - me % 4 + below) % n_row + ((me % 4) ^ place), blocks)

time: 145 us -> 145 us (level)
  no operation moved by 1% of the time
where the time goes in v4:
time: 145 us
  waiting for transfers between devices  69.1 us (48%)
  starting transfers between devices  54.7 us (38%)
  Pallas kernels  13.8 us (10%)
  other arithmetic  3.38 us (2%)
  local copies, waits for them, and re-layouts  3.1 us (2%)
    ppermute x16, waiting for transfers between devices, swap(): return lax.ppermute(v, 'row', [(i, i ^ bit) for i in range(n_row)])  33.1 us
    ppermute x5, waiting for transfers between devices, along_z(): lax.ppermute(v, 'row', [(i, (i + 4 * by) % n_row) for i in range(n_row)])  28.1 us
    ppermute x5, starting transfers between devices, along_z(): lax.ppermute(v, 'row', [(i, (i + 4 * by) % n_row) for i in range(n_row)])  19.9 us
    ppermute x16, starting transfers between devices, swap(): return lax.ppermute(v, 'row', [(i, i ^ bit) for i in range(n_row)])  17.7 us
    ppermute x8, starting transfers between devices, butterfly(): terms.append(lax.ppermute(value, axis, [(i, i ^ s) for i in range(n)]))  8.59 us
    all_to_all x1, starting transfers between devices, per_device(): blocks = lax.all_to_all(blocks, 'row', 0, 0, tiled=True)  8.34 us
    ppermute x8, waiting for transfers between devices, butterfly(): terms.append(lax.ppermute(value, axis, [(i, i ^ s) for i in range(n)]))  7.9 us
    pallas_call x1, Pallas kernels, gemm(): pl.pallas_call(gemm_kernel, out_shape=pltpu.VMEM((rows, cols), jnp.float3...  6.48 us
  transfers between devices with their start and end apart: 31, of which 12 were waited for; matrix products, arithmetic and copies ran while one was open for 3% of the time, Pallas kernels for 5%

profile of v4, /device:TPU:0, one launch (start us, length us, event | category | flops | bytes accessed | tf_op | source)
XLA Modules:
  0.0 145.0 jit_solution(6293895572791969131)
XLA Ops:
  0.7 1.6 %copy-done.1 = bf16[128,8192]{1,0:T(8,128)(2,1)S(1)} copy-done((bf16[128,8192]{1,0:T(8,128)(2,1)S(1)}, bf16[128,8192]{1,0:T(8,128)(2,1)}, u32[]{:S(2)}) %copy-start.1) | copy-done | bytes 2097176
  2.3 1.1 pack.1
  3.3 8.3 %all-to-all-start = ((bf16[16,128,256]{2,1,0:T(8,128)(2,1)}), bf16[16,128,256]{2,1,0:T(8,128)(2,1)S(1)}, u32[]{:S(2)}, u32[]{:S(2)}) async-start(bf16[16,128,256]{2,1,0:T(8,128)(2,1)} %pack.1), calls=%async_computation | async-start | bytes 2097152 | tf_op jit(solution)/shard_map/all_to_all | solution.py:287
  11.7 1.9 %collective-permute-start.1 = (bf16[128,2048]{1,0:T(8,128)(2,1)}, bf16[128,2048]{1,0:T(8,128)(2,1)}, u32[]{:S(2)}, u32[]{:S(2)}) collective-permute-start(bf16[128,2048]{1,0:T(8,128)(2,1)} %refs_0_.1), channel_id=1, source_target_pairs={{0,8},{2,10},{4,12},{6,14},{8,16},{10,18},{12,20},{14,22},{16,24},... | collective-permute-start | bytes 1572872 | tf_op jit(solution)/shard_map/ppermute | solution.py:267
  13.6 1.5 %collective-permute-start.4 = (bf16[128,2048]{1,0:T(8,128)(2,1)}, bf16[128,2048]{1,0:T(8,128)(2,1)S(1)}, u32[]{:S(2)}, u32[]{:S(2)}) collective-permute-start(bf16[128,2048]{1,0:T(8,128)(2,1)} %refs_0_.1), channel_id=1, source_target_pairs={{0,2},{2,0},{4,6},{6,4},{8,10},{10,8},{12,14},{14,12},{16,18},{18,... | collective-permute-start | bytes 1572872 | tf_op jit(solution)/shard_map/ppermute | solution.py:264
  15.1 2.4 %collective-permute-start.2 = (bf16[128,2048]{1,0:T(8,128)(2,1)}, bf16[128,2048]{1,0:T(8,128)(2,1)}, u32[]{:S(2)}, u32[]{:S(2)}) collective-permute-start(bf16[128,2048]{1,0:T(8,128)(2,1)} %refs_0_.1), channel_id=1, source_target_pairs={{0,24},{2,26},{4,28},{6,30},{8,0},{10,2},{12,4},{14,6},{16,8},{18,... | collective-permute-start | bytes 1572872 | tf_op jit(solution)/shard_map/ppermute | solution.py:267
  17.4 1.5 %collective-permute-start.5 = (bf16[128,2048]{1,0:T(8,128)(2,1)}, bf16[128,2048]{1,0:T(8,128)(2,1)S(1)}, u32[]{:S(2)}, u32[]{:S(2)}) collective-permute-start(bf16[128,2048]{1,0:T(8,128)(2,1)} %refs_0_.1), channel_id=1, source_target_pairs={{0,4},{2,6},{4,0},{6,2},{8,12},{10,14},{12,8},{14,10},{16,20},{18,... | collective-permute-start | bytes 1572872 | tf_op jit(solution)/shard_map/ppermute | solution.py:264
  18.9 26.4 %collective-permute-done.1.refs_1_ = bf16[128,2048]{1,0:T(8,128)(2,1)} collective-permute-done((bf16[128,2048]{1,0:T(8,128)(2,1)}, bf16[128,2048]{1,0:T(8,128)(2,1)}, u32[]{:S(2)}, u32[]{:S(2)}) %collective-permute-start.1) | collective-permute-done | bytes 524320 | tf_op jit(solution)/shard_map/ppermute | solution.py:267
  45.3 13.2 %collective-permute-start.3 = (bf16[128,2048]{1,0:T(8,128)(2,1)}, bf16[128,2048]{1,0:T(8,128)(2,1)}, u32[]{:S(2)}, u32[]{:S(2)}) collective-permute-start(bf16[128,2048]{1,0:T(8,128)(2,1)} %collective-permute-done.1.refs_1_), channel_id=1, source_target_pairs={{0,8},{2,10},{4,12},{6,14},{8,16},{10,18},{12,20},{14,22},{16,24},... | collective-permute-start | bytes 1572872 | tf_op jit(solution)/shard_map/ppermute | solution.py:267
  58.5 1.5 %collective-permute-start.6 = (bf16[128,2048]{1,0:T(8,128)(2,1)}, bf16[128,2048]{1,0:T(8,128)(2,1)S(1)}, u32[]{:S(2)}, u32[]{:S(2)}) collective-permute-start(bf16[128,2048]{1,0:T(8,128)(2,1)} %collective-permute-done.1.refs_1_), channel_id=1, source_target_pairs={{0,2},{2,0},{4,6},{6,4},{8,10},{10,8},{12,14},{14,12},{16,18},{18,... | collective-permute-start | bytes 1572872 | tf_op jit(solution)/shard_map/ppermute | solution.py:264
  60.0 1.5 %collective-permute-start.7 = (bf16[128,2048]{1,0:T(8,128)(2,1)}, bf16[128,2048]{1,0:T(8,128)(2,1)S(1)}, u32[]{:S(2)}, u32[]{:S(2)}) collective-permute-start(bf16[128,2048]{1,0:T(8,128)(2,1)} %collective-permute-done.1.refs_1_), channel_id=1, source_target_pairs={{0,4},{2,6},{4,0},{6,2},{8,12},{10,14},{12,8},{14,10},{16,20},{18,... | collective-permute-start | bytes 1572872 | tf_op jit(solution)/shard_map/ppermute | solution.py:264
  61.5 0.7 slice.32
  62.2 0.5 collective-permute-start.10
  62.8 0.9 arrange.1.mine_ref
  63.8 14.4 %collective-permute-done.10.refs_10_ = bf16[64,2048]{1,0:T(8,128)(2,1)S(1)} collective-permute-done((bf16[64,2048]{1,0:T(8,128)(2,1)}, bf16[64,2048]{1,0:T(8,128)(2,1)S(1)}, u32[]{:S(2)}, u32[]{:S(2)}) %collective-permute-start.10) | collective-permute-done | bytes 262176 | tf_op jit(solution)/shard_map/ppermute | solution.py:264
  78.2 0.6 collective-permute-start.8
  78.8 1.7 %collective-permute-start.9 = (bf16[128,2048]{1,0:T(8,128)(2,1)}, bf16[128,2048]{1,0:T(8,128)(2,1)S(1)}, u32[]{:S(2)}, u32[]{:S(2)}) collective-permute-start(bf16[128,2048]{1,0:T(8,128)(2,1)} %collective-permute-done.2.refs_2_), channel_id=1, source_target_pairs={{0,4},{2,6},{4,0},{6,2},{8,12},{10,14},{12,8},{14,10},{16,20},{18,... | collective-permute-start | bytes 1572872 | tf_op jit(solution)/shard_map/ppermute | solution.py:264
  80.5 1.5 %collective-permute-start.12 = (bf16[128,2048]{1,0:T(8,128)(2,1)}, bf16[128,2048]{1,0:T(8,128)(2,1)S(1)}, u32[]{:S(2)}, u32[]{:S(2)}) collective-permute-start(bf16[128,2048]{1,0:T(8,128)(2,1)} %collective-permute-done.3.refs_3_), channel_id=1, source_target_pairs={{0,2},{2,0},{4,6},{6,4},{8,10},{10,8},{12,14},{14,12},{16,18},{18,... | collective-permute-start | bytes 1572872 | tf_op jit(solution)/shard_map/ppermute | solution.py:264
  82.0 0.3 collective-permute-start.13
  82.3 10.9 %collective-permute-done.8.refs_8_ = bf16[128,2048]{1,0:T(8,128)(2,1)S(1)} collective-permute-done((bf16[128,2048]{1,0:T(8,128)(2,1)}, bf16[128,2048]{1,0:T(8,128)(2,1)S(1)}, u32[]{:S(2)}, u32[]{:S(2)}) %collective-permute-start.8) | collective-permute-done | bytes 524320 | tf_op jit(solution)/shard_map/ppermute | solution.py:264
  93.2 0.6 collective-permute-start.11
  93.8 2.5 %collective-permute-start.14 = (bf16[64,2048]{1,0:T(8,128)(2,1)S(1)}, bf16[64,2048]{1,0:T(8,128)(2,1)S(1)}, u32[]{:S(2)}, u32[]{:S(2)}) collective-permute-start(bf16[64,2048]{1,0:T(8,128)(2,1)S(1)} %collective-permute-done.10.refs_10_), channel_id=1, source_target_pairs={{0,8},{2,10},{4,12},{6,14},{8,16},{10,18},{12,20},{14,22},{16,24},... | collective-permute-start | bytes 786440 | tf_op jit(solution)/shard_map/ppermute | solution.py:267
  96.3 7.7 %collective-permute-done.12.refs_12_ = bf16[128,2048]{1,0:T(8,128)(2,1)S(1)} collective-permute-done((bf16[128,2048]{1,0:T(8,128)(2,1)}, bf16[128,2048]{1,0:T(8,128)(2,1)S(1)}, u32[]{:S(2)}, u32[]{:S(2)}) %collective-permute-start.12) | collective-permute-done | bytes 524320 | tf_op jit(solution)/shard_map/ppermute | solution.py:264
  104.0 1.9 %collective-permute-start.15 = (bf16[32,2048]{1,0:T(8,128)(2,1)S(1)}, bf16[32,2048]{1,0:T(8,128)(2,1)S(1)}, u32[]{:S(2)}, u32[]{:S(2)}) collective-permute-start(bf16[32,2048]{1,0:T(8,128)(2,1)S(1)} %slice.34), channel_id=1, source_target_pairs={{0,4},{2,6},{4,0},{6,2},{8,12},{10,14},{12,8},{14,10},{16,20},{18,... | collective-permute-start | bytes 393224 | tf_op jit(solution)/shard_map/ppermute | solution.py:264
  105.9 2.5 %multiply_reduce_fusion.1 = f32[2048]{0:T(1024)S(1)} fusion(f32[512,2048]{1,0:T(8,128)} %weight_ref.1), kind=kLoop, calls=%fused_computation.1 | loop fusion | flops 2095104 | bytes 4202496 | tf_op jit(solution)/shard_map/reduce_sum | solution.py:302
  108.6 0.6 collective-permute-start.16
  109.2 0.4 collective-permute-start.18
  109.6 1.6 %collective-permute-done.17.refs_3_ = bf16[64,2048]{1,0:T(8,128)(2,1)S(1)} collective-permute-done((bf16[64,2048]{1,0:T(8,128)(2,1)S(1)}, bf16[64,2048]{1,0:T(8,128)(2,1)S(1)}, u32[]{:S(2)}, u32[]{:S(2)}) %collective-permute-start.17) | collective-permute-done | bytes 262176 | tf_op jit(solution)/shard_map/ppermute | solution.py:267
  111.3 0.6 collective-permute-start.19
  111.8 1.7 %collective-permute-start.20 = (bf16[64,2048]{1,0:T(8,128)(2,1)S(1)}, bf16[64,2048]{1,0:T(8,128)(2,1)S(1)}, u32[]{:S(2)}, u32[]{:S(2)}) collective-permute-start(bf16[64,2048]{1,0:T(8,128)(2,1)S(1)} %slice.38), channel_id=1, source_target_pairs={{0,4},{2,6},{4,0},{6,2},{8,12},{10,14},{12,8},{14,10},{16,20},{18,... | collective-permute-start | bytes 786440 | tf_op jit(solution)/shard_map/ppermute | solution.py:264
  113.6 1.5 %collective-permute-start.21 = (bf16[64,2048]{1,0:T(8,128)(2,1)S(1)}, bf16[64,2048]{1,0:T(8,128)(2,1)S(1)}, u32[]{:S(2)}, u32[]{:S(2)}) collective-permute-start(bf16[64,2048]{1,0:T(8,128)(2,1)S(1)} %slice.39), channel_id=1, source_target_pairs={{0,2},{2,0},{4,6},{6,4},{8,10},{10,8},{12,14},{14,12},{16,18},{18,... | collective-permute-start | bytes 786440 | tf_op jit(solution)/shard_map/ppermute | solution.py:264
  115.1 6.5 %gemm.1.before_ref = f32[512,2048]{1,0:T(8,128)S(1)} custom-call(s32[1]{0:T(128)} %bitcast.side_ref, bf16[256,2048]{1,0:T(8,128)(2,1)S(1)} %arrange.1.mine_ref, bf16[256,2048]{1,0:T(8,128)(2,1)S(1)} %collective-permute-done.other_ref, bf16[128,2048]{1,0:T(8,128)(2,1)} %refs_0_.1, bf16[128,2048]{1,0:T(8,128)(2,1)} %collective-permute-done.1.refs_1_, ...), custom_call_target="tpu_custom_call" | custom-call | flops 3489660928 | bytes 6815744 | tf_op jit(solution)/shard_map/gemm/pallas_call | solution.py:128
  121.6 1.5 %last_gemm.1 = (f32[512,2048]{1,0:T(8,128)S(1)}, f32[1,512]{1,0:T(1,128)S(1)}) custom-call(s32[1]{0:T(128)} %bitcast.side_ref, bf16[256,2048]{1,0:T(8,128)(2,1)S(1)} %arrange.1.mine_ref, bf16[256,2048]{1,0:T(8,128)(2,1)S(1)} %collective-permute-done.other_ref, f32[512,2048]{1,0:T(8,128)S(1)} %gemm.1.before_ref, ...), custom_call_target="tpu_custom_call" | custom-call | flops 805306368 | bytes 1572864 | tf_op jit(solution)/shard_map/last_gemm/pallas_call | solution.py:170
  123.2 1.1 collective-permute-done.22
  124.4 0.7 add_reduce_fusion
  125.2 0.6 collective-permute-start.23
  125.8 0.3 collective-permute-start.24
  126.1 2.6 %collective-permute-start.25 = (f32[2,2176]{1,0:T(2,128)S(1)}, f32[2,2176]{1,0:T(2,128)S(1)}, u32[]{:S(2)}, u32[]{:S(2)}) collective-permute-start(f32[2,2176]{1,0:T(2,128)S(1)} %pad_maximum_fusion), channel_id=1, source_target_pairs={{0,6},{2,4},{4,2},{6,0},{8,14},{10,12},{12,10},{14,8},{16,22},{18,... | collective-permute-start | bytes 52232 | tf_op jit(solution)/shard_map/ppermute | solution.py:27
  129.0 0.6 collective-permute-done.24
  129.6 1.2 collective-permute-done.25
  130.8 2.3 %collective-permute-start.26 = (f32[2,2176]{1,0:T(2,128)S(1)}, f32[2,2176]{1,0:T(2,128)S(1)}, u32[]{:S(2)}, u32[]{:S(2)}) collective-permute-start(f32[2,2176]{1,0:T(2,128)S(1)} %add_add_fusion.1), channel_id=1, source_target_pairs={{0,8},{2,10},{4,12},{6,14},{8,0},{10,2},{12,4},{14,6},{16,24},{18,... | collective-permute-start | bytes 52232 | tf_op jit(solution)/shard_map/ppermute | solution.py:27
  133.1 1.2 collective-permute-start.27
  134.3 1.4 collective-permute-start.28
  135.7 2.1 %collective-permute-done.27 = f32[2,2176]{1,0:T(2,128)S(1)} collective-permute-done((f32[2,2176]{1,0:T(2,128)S(1)}, f32[2,2176]{1,0:T(2,128)S(1)}, u32[]{:S(2)}, u32[]{:S(2)}) %collective-permute-start.27) | collective-permute-done | bytes 17440 | tf_op jit(solution)/shard_map/ppermute | solution.py:27
  137.8 2.1 %collective-permute-done.28 = f32[2,2176]{1,0:T(2,128)S(1)} collective-permute-done((f32[2,2176]{1,0:T(2,128)S(1)}, f32[2,2176]{1,0:T(2,128)S(1)}, u32[]{:S(2)}, u32[]{:S(2)}) %collective-permute-start.28) | collective-permute-done | bytes 17440 | tf_op jit(solution)/shard_map/ppermute | solution.py:27
  140.2 0.6 copy.11
  140.8 0.6 collective-permute-done.29
  141.3 3.7 %finish.1 = (f32[512,2048]{1,0:T(8,128)}, f32[512,2048]{1,0:T(8,128)}) custom-call(f32[8,128]{1,0:T(8,128)S(1)} %add.74.sums_ref, f32[1,512]{1,0:T(1,128)S(1)} %bitcast.8, f32[1,2048]{1,0:T(1,128)S(1)} %get-tuple-element.13.col_ref, f32[512,2048]{1,0:T(8,128)S(1)} %get-tuple-element.10.gradient_ref, f32[512,2048]{1,0:T(8,128)S(1)} %copy-done), custom_call_target="tpu_custom_call" | custom-call | flops 4194304 | bytes 16777216 | tf_op jit(solution)/shard_map/finish/pallas_call | solution.py:233
  (72 shorter events, 1.0 us)
Async XLA Ops:
  0.6 62.1 %copy-start.13 = (s32[16]{0:T(128)S(1)}, s32[16]{0:T(128)}, u32[]{:S(2)}) copy-start(s32[16]{0:T(128)} %constant.65.clone) | copy-start | bytes 196
  0.6 62.1 %copy-start.14 = (s32[16]{0:T(128)S(1)}, s32[16]{0:T(128)}, u32[]{:S(2)}) copy-start(s32[16]{0:T(128)} %constant.66.clone) | copy-start | bytes 196
  0.7 1.6 %copy-start.1 = (bf16[128,8192]{1,0:T(8,128)(2,1)S(1)}, bf16[128,8192]{1,0:T(8,128)(2,1)}, u32[]{:S(2)}) copy-start(bf16[128,8192]{1,0:T(8,128)(2,1)} %acts_ref.1) | copy-start | bytes 6291460
  3.3 59.4 %all-to-all-start = ((bf16[16,128,256]{2,1,0:T(8,128)(2,1)}), bf16[16,128,256]{2,1,0:T(8,128)(2,1)S(1)}, u32[]{:S(2)}, u32[]{:S(2)}) async-start(bf16[16,128,256]{2,1,0:T(8,128)(2,1)} %pack.1), calls=%async_computation | async-start | bytes 2097152 | tf_op jit(solution)/shard_map/all_to_all | solution.py:287
  11.7 33.7 %collective-permute-start.1 = (bf16[128,2048]{1,0:T(8,128)(2,1)}, bf16[128,2048]{1,0:T(8,128)(2,1)}, u32[]{:S(2)}, u32[]{:S(2)}) collective-permute-start(bf16[128,2048]{1,0:T(8,128)(2,1)} %refs_0_.1), channel_id=1, source_target_pairs={{0,8},{2,10},{4,12},{6,14},{8,16},{10,18},{12,20},{14,22},{16,24},... | collective-permute-start | bytes 1572872 | tf_op jit(solution)/shard_map/ppermute | solution.py:267
  13.6 46.4 %collective-permute-start.4 = (bf16[128,2048]{1,0:T(8,128)(2,1)}, bf16[128,2048]{1,0:T(8,128)(2,1)S(1)}, u32[]{:S(2)}, u32[]{:S(2)}) collective-permute-start(bf16[128,2048]{1,0:T(8,128)(2,1)} %refs_0_.1), channel_id=1, source_target_pairs={{0,2},{2,0},{4,6},{6,4},{8,10},{10,8},{12,14},{14,12},{16,18},{18,... | collective-permute-start | bytes 1572872 | tf_op jit(solution)/shard_map/ppermute | solution.py:264
  15.1 47.2 %collective-permute-start.2 = (bf16[128,2048]{1,0:T(8,128)(2,1)}, bf16[128,2048]{1,0:T(8,128)(2,1)}, u32[]{:S(2)}, u32[]{:S(2)}) collective-permute-start(bf16[128,2048]{1,0:T(8,128)(2,1)} %refs_0_.1), channel_id=1, source_target_pairs={{0,24},{2,26},{4,28},{6,30},{8,0},{10,2},{12,4},{14,6},{16,8},{18,... | collective-permute-start | bytes 1572872 | tf_op jit(solution)/shard_map/ppermute | solution.py:267
  17.4 46.3 %collective-permute-start.5 = (bf16[128,2048]{1,0:T(8,128)(2,1)}, bf16[128,2048]{1,0:T(8,128)(2,1)S(1)}, u32[]{:S(2)}, u32[]{:S(2)}) collective-permute-start(bf16[128,2048]{1,0:T(8,128)(2,1)} %refs_0_.1), channel_id=1, source_target_pairs={{0,4},{2,6},{4,0},{6,2},{8,12},{10,14},{12,8},{14,10},{16,20},{18,... | collective-permute-start | bytes 1572872 | tf_op jit(solution)/shard_map/ppermute | solution.py:264
  45.3 33.4 %collective-permute-start.3 = (bf16[128,2048]{1,0:T(8,128)(2,1)}, bf16[128,2048]{1,0:T(8,128)(2,1)}, u32[]{:S(2)}, u32[]{:S(2)}) collective-permute-start(bf16[128,2048]{1,0:T(8,128)(2,1)} %collective-permute-done.1.refs_1_), channel_id=1, source_target_pairs={{0,8},{2,10},{4,12},{6,14},{8,16},{10,18},{12,20},{14,22},{16,24},... | collective-permute-start | bytes 1572872 | tf_op jit(solution)/shard_map/ppermute | solution.py:267
  58.5 22.0 %collective-permute-start.6 = (bf16[128,2048]{1,0:T(8,128)(2,1)}, bf16[128,2048]{1,0:T(8,128)(2,1)S(1)}, u32[]{:S(2)}, u32[]{:S(2)}) collective-permute-start(bf16[128,2048]{1,0:T(8,128)(2,1)} %collective-permute-done.1.refs_1_), channel_id=1, source_target_pairs={{0,2},{2,0},{4,6},{6,4},{8,10},{10,8},{12,14},{14,12},{16,18},{18,... | collective-permute-start | bytes 1572872 | tf_op jit(solution)/shard_map/ppermute | solution.py:264
  60.0 48.5 %copy-start.4 = (bf16[128,2048]{1,0:T(8,128)(2,1)}, bf16[128,2048]{1,0:T(8,128)(2,1)S(1)}, u32[]{:S(2)}) copy-start(bf16[128,2048]{1,0:T(8,128)(2,1)S(1)} %collective-permute-done.4.refs_4_) | copy-start | bytes 1572868
  60.0 22.0 %collective-permute-start.7 = (bf16[128,2048]{1,0:T(8,128)(2,1)}, bf16[128,2048]{1,0:T(8,128)(2,1)S(1)}, u32[]{:S(2)}, u32[]{:S(2)}) collective-permute-start(bf16[128,2048]{1,0:T(8,128)(2,1)} %collective-permute-done.1.refs_1_), channel_id=1, source_target_pairs={{0,4},{2,6},{4,0},{6,2},{8,12},{10,14},{12,8},{14,10},{16,20},{18,... | collective-permute-start | bytes 1572872 | tf_op jit(solution)/shard_map/ppermute | solution.py:264
  62.2 16.0 %collective-permute-start.10 = (bf16[64,2048]{1,0:T(8,128)(2,1)}, bf16[64,2048]{1,0:T(8,128)(2,1)S(1)}, u32[]{:S(2)}, u32[]{:S(2)}) collective-permute-start(bf16[64,2048]{1,0:T(8,128)(2,1)} %slice.32), channel_id=1, source_target_pairs={{0,4},{2,6},{4,0},{6,2},{8,12},{10,14},{12,8},{14,10},{16,20},{18,... | collective-permute-start | bytes 786440 | tf_op jit(solution)/shard_map/ppermute | solution.py:264
  63.7 51.3 %copy-start.5 = (bf16[128,2048]{1,0:T(8,128)(2,1)}, bf16[128,2048]{1,0:T(8,128)(2,1)S(1)}, u32[]{:S(2)}) copy-start(bf16[128,2048]{1,0:T(8,128)(2,1)S(1)} %collective-permute-done.5.refs_5_) | copy-start | bytes 1572868
  63.7 49.9 %collective-permute-start = (bf16[256,2048]{1,0:T(8,128)(2,1)S(1)}, bf16[256,2048]{1,0:T(8,128)(2,1)S(1)}, u32[]{:S(2)}, u32[]{:S(2)}) collective-permute-start(bf16[256,2048]{1,0:T(8,128)(2,1)S(1)} %arrange.1.mine_ref), channel_id=1, source_target_pairs={{0,1},{1,0},{2,3},{3,2},{4,5},{5,4},{6,7},{7,6},{8,9},{9,8},{10,11... | collective-permute-start | bytes 3145736 | tf_op jit(solution)/shard_map/ppermute | solution.py:294
  78.2 36.8 %copy-start.10 = (bf16[64,2048]{1,0:T(8,128)(2,1)}, bf16[64,2048]{1,0:T(8,128)(2,1)S(1)}, u32[]{:S(2)}) copy-start(bf16[64,2048]{1,0:T(8,128)(2,1)S(1)} %collective-permute-done.10.refs_10_) | copy-start | bytes 786436
  78.2 15.0 %collective-permute-start.8 = (bf16[128,2048]{1,0:T(8,128)(2,1)}, bf16[128,2048]{1,0:T(8,128)(2,1)S(1)}, u32[]{:S(2)}, u32[]{:S(2)}) collective-permute-start(bf16[128,2048]{1,0:T(8,128)(2,1)} %collective-permute-done.2.refs_2_), channel_id=1, source_target_pairs={{0,2},{2,0},{4,6},{6,4},{8,10},{10,8},{12,14},{14,12},{16,18},{18,... | collective-permute-start | bytes 1572872 | tf_op jit(solution)/shard_map/ppermute | solution.py:264
  78.8 15.0 %collective-permute-start.9 = (bf16[128,2048]{1,0:T(8,128)(2,1)}, bf16[128,2048]{1,0:T(8,128)(2,1)S(1)}, u32[]{:S(2)}, u32[]{:S(2)}) collective-permute-start(bf16[128,2048]{1,0:T(8,128)(2,1)} %collective-permute-done.2.refs_2_), channel_id=1, source_target_pairs={{0,4},{2,6},{4,0},{6,2},{8,12},{10,14},{12,8},{14,10},{16,20},{18,... | collective-permute-start | bytes 1572872 | tf_op jit(solution)/shard_map/ppermute | solution.py:264
  80.5 34.5 %copy-start.6 = (bf16[128,2048]{1,0:T(8,128)(2,1)}, bf16[128,2048]{1,0:T(8,128)(2,1)S(1)}, u32[]{:S(2)}) copy-start(bf16[128,2048]{1,0:T(8,128)(2,1)S(1)} %collective-permute-done.6.refs_6_) | copy-start | bytes 1572868
  80.5 23.5 %collective-permute-start.12 = (bf16[128,2048]{1,0:T(8,128)(2,1)}, bf16[128,2048]{1,0:T(8,128)(2,1)S(1)}, u32[]{:S(2)}, u32[]{:S(2)}) collective-permute-start(bf16[128,2048]{1,0:T(8,128)(2,1)} %collective-permute-done.3.refs_3_), channel_id=1, source_target_pairs={{0,2},{2,0},{4,6},{6,4},{8,10},{10,8},{12,14},{14,12},{16,18},{18,... | collective-permute-start | bytes 1572872 | tf_op jit(solution)/shard_map/ppermute | solution.py:264
  82.0 33.1 %copy-start.7 = (bf16[128,2048]{1,0:T(8,128)(2,1)}, bf16[128,2048]{1,0:T(8,128)(2,1)S(1)}, u32[]{:S(2)}) copy-start(bf16[128,2048]{1,0:T(8,128)(2,1)S(1)} %collective-permute-done.7.refs_7_) | copy-start | bytes 1572868
  82.0 22.0 %collective-permute-start.13 = (bf16[128,2048]{1,0:T(8,128)(2,1)}, bf16[128,2048]{1,0:T(8,128)(2,1)S(1)}, u32[]{:S(2)}, u32[]{:S(2)}) collective-permute-start(bf16[128,2048]{1,0:T(8,128)(2,1)} %collective-permute-done.3.refs_3_), channel_id=1, source_target_pairs={{0,4},{2,6},{4,0},{6,2},{8,12},{10,14},{12,8},{14,10},{16,20},{18,... | collective-permute-start | bytes 1572872 | tf_op jit(solution)/shard_map/ppermute | solution.py:264
  93.2 21.8 %copy-start.8 = (bf16[128,2048]{1,0:T(8,128)(2,1)}, bf16[128,2048]{1,0:T(8,128)(2,1)S(1)}, u32[]{:S(2)}) copy-start(bf16[128,2048]{1,0:T(8,128)(2,1)S(1)} %collective-permute-done.8.refs_8_) | copy-start | bytes 1572868
  93.2 15.4 %collective-permute-start.11 = (bf16[64,2048]{1,0:T(8,128)(2,1)S(1)}, bf16[64,2048]{1,0:T(8,128)(2,1)S(1)}, u32[]{:S(2)}, u32[]{:S(2)}) collective-permute-start(bf16[64,2048]{1,0:T(8,128)(2,1)S(1)} %slice.33), channel_id=1, source_target_pairs={{0,2},{2,0},{4,6},{6,4},{8,10},{10,8},{12,14},{14,12},{16,18},{18,... | collective-permute-start | bytes 786440 | tf_op jit(solution)/shard_map/ppermute | solution.py:264
  93.8 21.3 %copy-start.9 = (bf16[128,2048]{1,0:T(8,128)(2,1)}, bf16[128,2048]{1,0:T(8,128)(2,1)S(1)}, u32[]{:S(2)}) copy-start(bf16[128,2048]{1,0:T(8,128)(2,1)S(1)} %collective-permute-done.9.refs_9_) | copy-start | bytes 1572868
  93.8 15.4 %collective-permute-start.14 = (bf16[64,2048]{1,0:T(8,128)(2,1)S(1)}, bf16[64,2048]{1,0:T(8,128)(2,1)S(1)}, u32[]{:S(2)}, u32[]{:S(2)}) collective-permute-start(bf16[64,2048]{1,0:T(8,128)(2,1)S(1)} %collective-permute-done.10.refs_10_), channel_id=1, source_target_pairs={{0,8},{2,10},{4,12},{6,14},{8,16},{10,18},{12,20},{14,22},{16,24},... | collective-permute-start | bytes 786440 | tf_op jit(solution)/shard_map/ppermute | solution.py:267
  104.0 7.3 %collective-permute-start.17 = (bf16[64,2048]{1,0:T(8,128)(2,1)S(1)}, bf16[64,2048]{1,0:T(8,128)(2,1)S(1)}, u32[]{:S(2)}, u32[]{:S(2)}) collective-permute-start(bf16[64,2048]{1,0:T(8,128)(2,1)S(1)} %collective-permute-done.10.refs_10_), channel_id=1, source_target_pairs={{0,24},{2,26},{4,28},{6,30},{8,0},{10,2},{12,4},{14,6},{16,8},{18,... | collective-permute-start | bytes 786440 | tf_op jit(solution)/shard_map/ppermute | solution.py:267
  104.0 7.9 %collective-permute-start.15 = (bf16[32,2048]{1,0:T(8,128)(2,1)S(1)}, bf16[32,2048]{1,0:T(8,128)(2,1)S(1)}, u32[]{:S(2)}, u32[]{:S(2)}) collective-permute-start(bf16[32,2048]{1,0:T(8,128)(2,1)S(1)} %slice.34), channel_id=1, source_target_pairs={{0,4},{2,6},{4,0},{6,2},{8,12},{10,14},{12,8},{14,10},{16,20},{18,... | collective-permute-start | bytes 393224 | tf_op jit(solution)/shard_map/ppermute | solution.py:264
  108.6 6.5 %copy-start.11 = (bf16[64,2048]{1,0:T(8,128)(2,1)}, bf16[64,2048]{1,0:T(8,128)(2,1)S(1)}, u32[]{:S(2)}) copy-start(bf16[64,2048]{1,0:T(8,128)(2,1)S(1)} %collective-permute-done.11.refs_11_) | copy-start | bytes 786436
  108.6 13.0 %collective-permute-start.16 = (bf16[32,2048]{1,0:T(8,128)(2,1)S(1)}, bf16[32,2048]{1,0:T(8,128)(2,1)S(1)}, u32[]{:S(2)}, u32[]{:S(2)}) collective-permute-start(bf16[32,2048]{1,0:T(8,128)(2,1)S(1)} %slice.35), channel_id=1, source_target_pairs={{0,2},{2,0},{4,6},{6,4},{8,10},{10,8},{12,14},{14,12},{16,18},{18,... | collective-permute-start | bytes 393224 | tf_op jit(solution)/shard_map/ppermute | solution.py:264
  109.2 12.4 %collective-permute-start.18 = (bf16[32,2048]{1,0:T(8,128)(2,1)S(1)}, bf16[32,2048]{1,0:T(8,128)(2,1)S(1)}, u32[]{:S(2)}, u32[]{:S(2)}) collective-permute-start(bf16[32,2048]{1,0:T(8,128)(2,1)S(1)} %slice.36), channel_id=1, source_target_pairs={{0,4},{2,6},{4,0},{6,2},{8,12},{10,14},{12,8},{14,10},{16,20},{18,... | collective-permute-start | bytes 393224 | tf_op jit(solution)/shard_map/ppermute | solution.py:264
  111.3 10.3 %collective-permute-start.19 = (bf16[32,2048]{1,0:T(8,128)(2,1)S(1)}, bf16[32,2048]{1,0:T(8,128)(2,1)S(1)}, u32[]{:S(2)}, u32[]{:S(2)}) collective-permute-start(bf16[32,2048]{1,0:T(8,128)(2,1)S(1)} %slice.37), channel_id=1, source_target_pairs={{0,2},{2,0},{4,6},{6,4},{8,10},{10,8},{12,14},{14,12},{16,18},{18,... | collective-permute-start | bytes 393224 | tf_op jit(solution)/shard_map/ppermute | solution.py:264
  111.8 9.8 %collective-permute-start.20 = (bf16[64,2048]{1,0:T(8,128)(2,1)S(1)}, bf16[64,2048]{1,0:T(8,128)(2,1)S(1)}, u32[]{:S(2)}, u32[]{:S(2)}) collective-permute-start(bf16[64,2048]{1,0:T(8,128)(2,1)S(1)} %slice.38), channel_id=1, source_target_pairs={{0,4},{2,6},{4,0},{6,2},{8,12},{10,14},{12,8},{14,10},{16,20},{18,... | collective-permute-start | bytes 786440 | tf_op jit(solution)/shard_map/ppermute | solution.py:264
  113.6 8.1 %collective-permute-start.21 = (bf16[64,2048]{1,0:T(8,128)(2,1)S(1)}, bf16[64,2048]{1,0:T(8,128)(2,1)S(1)}, u32[]{:S(2)}, u32[]{:S(2)}) collective-permute-start(bf16[64,2048]{1,0:T(8,128)(2,1)S(1)} %slice.39), channel_id=1, source_target_pairs={{0,2},{2,0},{4,6},{6,4},{8,10},{10,8},{12,14},{14,12},{16,18},{18,... | collective-permute-start | bytes 786440 | tf_op jit(solution)/shard_map/ppermute | solution.py:264
  121.6 2.8 %copy-start.12 = (f32[512]{0:T(512)S(1)}, f32[512]{0:T(512)}, u32[]{:S(2)}) copy-start(f32[512]{0:T(512)} %param.10) | copy-start | bytes 6148
  123.1 16.8 %copy-start.3 = (f32[2048]{0:T(1024)S(1)}, f32[2048]{0:T(1024)}, u32[]{:S(2)}) copy-start(f32[2048]{0:T(1024)} %param.11) | copy-start | bytes 24580
  123.1 18.2 %copy-start = (f32[512,2048]{1,0:T(8,128)S(1)}, f32[512,2048]{1,0:T(8,128)}, u32[]{:S(2)}) copy-start(f32[512,2048]{1,0:T(8,128)} %weight_ref.1) | copy-start | bytes 12582916
  123.1 1.2 collective-permute-start.22
  124.4 20.6 %copy-start.2 = (f32[512]{0:T(512)}, f32[512]{0:T(512)S(1)}, u32[]{:S(2)}) copy-start(f32[512]{0:T(512)S(1)} %get-tuple-element.22) | copy-start | bytes 6148
  125.2 3.8 %collective-permute-start.23 = (f32[2,2176]{1,0:T(2,128)S(1)}, f32[2,2176]{1,0:T(2,128)S(1)}, u32[]{:S(2)}, u32[]{:S(2)}) collective-permute-start(f32[2,2176]{1,0:T(2,128)S(1)} %pad_maximum_fusion), channel_id=1, source_target_pairs={{0,2},{2,0},{4,6},{6,4},{8,10},{10,8},{12,14},{14,12},{16,18},{18,... | collective-permute-start | bytes 52232 | tf_op jit(solution)/shard_map/ppermute | solution.py:27
  125.8 3.8 %collective-permute-start.24 = (f32[2,2176]{1,0:T(2,128)S(1)}, f32[2,2176]{1,0:T(2,128)S(1)}, u32[]{:S(2)}, u32[]{:S(2)}) collective-permute-start(f32[2,2176]{1,0:T(2,128)S(1)} %pad_maximum_fusion), channel_id=1, source_target_pairs={{0,4},{2,6},{4,0},{6,2},{8,12},{10,14},{12,8},{14,10},{16,20},{18,... | collective-permute-start | bytes 52232 | tf_op jit(solution)/shard_map/ppermute | solution.py:27
  126.1 4.6 %collective-permute-start.25 = (f32[2,2176]{1,0:T(2,128)S(1)}, f32[2,2176]{1,0:T(2,128)S(1)}, u32[]{:S(2)}, u32[]{:S(2)}) collective-permute-start(f32[2,2176]{1,0:T(2,128)S(1)} %pad_maximum_fusion), channel_id=1, source_target_pairs={{0,6},{2,4},{4,2},{6,0},{8,14},{10,12},{12,10},{14,8},{16,22},{18,... | collective-permute-start | bytes 52232 | tf_op jit(solution)/shard_map/ppermute | solution.py:27
  130.8 4.9 %collective-permute-start.26 = (f32[2,2176]{1,0:T(2,128)S(1)}, f32[2,2176]{1,0:T(2,128)S(1)}, u32[]{:S(2)}, u32[]{:S(2)}) collective-permute-start(f32[2,2176]{1,0:T(2,128)S(1)} %add_add_fusion.1), channel_id=1, source_target_pairs={{0,8},{2,10},{4,12},{6,14},{8,0},{10,2},{12,4},{14,6},{16,24},{18,... | collective-permute-start | bytes 52232 | tf_op jit(solution)/shard_map/ppermute | solution.py:27
  133.1 4.7 %collective-permute-start.27 = (f32[2,2176]{1,0:T(2,128)S(1)}, f32[2,2176]{1,0:T(2,128)S(1)}, u32[]{:S(2)}, u32[]{:S(2)}) collective-permute-start(f32[2,2176]{1,0:T(2,128)S(1)} %add_add_fusion.1), channel_id=1, source_target_pairs={{0,16},{2,18},{4,20},{6,22},{8,24},{10,26},{12,28},{14,30},{16,0},... | collective-permute-start | bytes 52232 | tf_op jit(solution)/shard_map/ppermute | solution.py:27
  134.3 5.5 %collective-permute-start.28 = (f32[2,2176]{1,0:T(2,128)S(1)}, f32[2,2176]{1,0:T(2,128)S(1)}, u32[]{:S(2)}, u32[]{:S(2)}) collective-permute-start(f32[2,2176]{1,0:T(2,128)S(1)} %add_add_fusion.1), channel_id=1, source_target_pairs={{0,24},{2,26},{4,28},{6,30},{8,16},{10,18},{12,20},{14,22},{16,8},... | collective-permute-start | bytes 52232 | tf_op jit(solution)/shard_map/ppermute | solution.py:27
  140.1 1.2 collective-permute-start.29

commit v5 on v4

--- a/solution.py
+++ b/solution.py
@@ -210,9 +210,9 @@
     for t in range(0, cols.shape[1], LANES):
         cols[:, t : t + LANES] = lax.rsqrt(col_ref[:, t : t + LANES]) / clip
     height = min(64, rows.shape[0])
+    bounds = [0, height // 4] + list(range(height, rows.shape[0] + 1, height))
     copies = []
-    for i in range(rows.shape[0] // height):
-        here = slice(i * height, (i + 1) * height)
+    for i, here in enumerate(slice(a, b) for a, b in zip(bounds, bounds[1:])):
         scale = rows[here, :]
         for t in range(0, cols.shape[1], LANES):
             lanes = slice(t, t + LANES)
@@ -240,7 +240,7 @@
             pltpu.VMEM((rows, cols), jnp.float32),
             pltpu.VMEM((rows, LANES), jnp.float32),
             pltpu.VMEM((1, cols), jnp.float32),
-            pltpu.SemaphoreType.DMA((2 * pl.cdiv(rows, min(64, rows)),)),
+            pltpu.SemaphoreType.DMA((2 * pl.cdiv(rows, min(64, rows)) + 2,)),
         ],
         compiler_params=pltpu.CompilerParams(vmem_limit_bytes=20 << 20),
         cost_estimate=pl.CostEstimate(flops=4 * rows * cols, bytes_accessed=16 * rows * cols, transcendentals=0),

time: 145 us -> 145 us (level)
  no operation moved by 1% of the time
where the time goes in v5:
time: 145 us
  waiting for transfers between devices  69.1 us (48%)
  starting transfers between devices  54.7 us (38%)
  Pallas kernels  13.7 us (9%)
  other arithmetic  3.38 us (2%)
  local copies, waits for them, and re-layouts  3.1 us (2%)
    ppermute x16, waiting for transfers between devices, swap(): return lax.ppermute(v, 'row', [(i, i ^ bit) for i in range(n_row)])  33.1 us
    ppermute x5, waiting for transfers between devices, along_z(): lax.ppermute(v, 'row', [(i, (i + 4 * by) % n_row) for i in range(n_row)])  28.1 us
    ppermute x5, starting transfers between devices, along_z(): lax.ppermute(v, 'row', [(i, (i + 4 * by) % n_row) for i in range(n_row)])  19.9 us
    ppermute x16, starting transfers between devices, swap(): return lax.ppermute(v, 'row', [(i, i ^ bit) for i in range(n_row)])  17.7 us
    ppermute x8, starting transfers between devices, butterfly(): terms.append(lax.ppermute(value, axis, [(i, i ^ s) for i in range(n)]))  8.59 us
    all_to_all x1, starting transfers between devices, per_device(): blocks = lax.all_to_all(blocks, 'row', 0, 0, tiled=True)  8.34 us
    ppermute x8, waiting for transfers between devices, butterfly(): terms.append(lax.ppermute(value, axis, [(i, i ^ s) for i in range(n)]))  7.89 us
    pallas_call x1, Pallas kernels, gemm(): pl.pallas_call(gemm_kernel, out_shape=pltpu.VMEM((rows, cols), jnp.float3...  6.48 us
  transfers between devices with their start and end apart: 31, of which 12 were waited for; matrix products, arithmetic and copies ran while one was open for 3% of the time, Pallas kernels for 5%

profile of v5, /device:TPU:0, one launch (start us, length us, event | category | flops | bytes accessed | tf_op | source)
XLA Modules:
  0.0 144.9 jit_solution(16762088727893556687)
XLA Ops:
  0.7 1.6 %copy-done.1 = bf16[128,8192]{1,0:T(8,128)(2,1)S(1)} copy-done((bf16[128,8192]{1,0:T(8,128)(2,1)S(1)}, bf16[128,8192]{1,0:T(8,128)(2,1)}, u32[]{:S(2)}) %copy-start.1) | copy-done | bytes 2097176
  2.3 1.1 pack.1
  3.3 8.3 %all-to-all-start = ((bf16[16,128,256]{2,1,0:T(8,128)(2,1)}), bf16[16,128,256]{2,1,0:T(8,128)(2,1)S(1)}, u32[]{:S(2)}, u32[]{:S(2)}) async-start(bf16[16,128,256]{2,1,0:T(8,128)(2,1)} %pack.1), calls=%async_computation | async-start | bytes 2097152 | tf_op jit(solution)/shard_map/all_to_all | solution.py:287
  11.7 1.9 %collective-permute-start.1 = (bf16[128,2048]{1,0:T(8,128)(2,1)}, bf16[128,2048]{1,0:T(8,128)(2,1)}, u32[]{:S(2)}, u32[]{:S(2)}) collective-permute-start(bf16[128,2048]{1,0:T(8,128)(2,1)} %refs_0_.1), channel_id=1, source_target_pairs={{0,8},{2,10},{4,12},{6,14},{8,16},{10,18},{12,20},{14,22},{16,24},... | collective-permute-start | bytes 1572872 | tf_op jit(solution)/shard_map/ppermute | solution.py:267
  13.6 1.5 %collective-permute-start.4 = (bf16[128,2048]{1,0:T(8,128)(2,1)}, bf16[128,2048]{1,0:T(8,128)(2,1)S(1)}, u32[]{:S(2)}, u32[]{:S(2)}) collective-permute-start(bf16[128,2048]{1,0:T(8,128)(2,1)} %refs_0_.1), channel_id=1, source_target_pairs={{0,2},{2,0},{4,6},{6,4},{8,10},{10,8},{12,14},{14,12},{16,18},{18,... | collective-permute-start | bytes 1572872 | tf_op jit(solution)/shard_map/ppermute | solution.py:264
  15.1 2.4 %collective-permute-start.2 = (bf16[128,2048]{1,0:T(8,128)(2,1)}, bf16[128,2048]{1,0:T(8,128)(2,1)}, u32[]{:S(2)}, u32[]{:S(2)}) collective-permute-start(bf16[128,2048]{1,0:T(8,128)(2,1)} %refs_0_.1), channel_id=1, source_target_pairs={{0,24},{2,26},{4,28},{6,30},{8,0},{10,2},{12,4},{14,6},{16,8},{18,... | collective-permute-start | bytes 1572872 | tf_op jit(solution)/shard_map/ppermute | solution.py:267
  17.4 1.5 %collective-permute-start.5 = (bf16[128,2048]{1,0:T(8,128)(2,1)}, bf16[128,2048]{1,0:T(8,128)(2,1)S(1)}, u32[]{:S(2)}, u32[]{:S(2)}) collective-permute-start(bf16[128,2048]{1,0:T(8,128)(2,1)} %refs_0_.1), channel_id=1, source_target_pairs={{0,4},{2,6},{4,0},{6,2},{8,12},{10,14},{12,8},{14,10},{16,20},{18,... | collective-permute-start | bytes 1572872 | tf_op jit(solution)/shard_map/ppermute | solution.py:264
  18.9 26.4 %collective-permute-done.1.refs_1_ = bf16[128,2048]{1,0:T(8,128)(2,1)} collective-permute-done((bf16[128,2048]{1,0:T(8,128)(2,1)}, bf16[128,2048]{1,0:T(8,128)(2,1)}, u32[]{:S(2)}, u32[]{:S(2)}) %collective-permute-start.1) | collective-permute-done | bytes 524320 | tf_op jit(solution)/shard_map/ppermute | solution.py:267
  45.3 13.2 %collective-permute-start.3 = (bf16[128,2048]{1,0:T(8,128)(2,1)}, bf16[128,2048]{1,0:T(8,128)(2,1)}, u32[]{:S(2)}, u32[]{:S(2)}) collective-permute-start(bf16[128,2048]{1,0:T(8,128)(2,1)} %collective-permute-done.1.refs_1_), channel_id=1, source_target_pairs={{0,8},{2,10},{4,12},{6,14},{8,16},{10,18},{12,20},{14,22},{16,24},... | collective-permute-start | bytes 1572872 | tf_op jit(solution)/shard_map/ppermute | solution.py:267
  58.5 1.5 %collective-permute-start.6 = (bf16[128,2048]{1,0:T(8,128)(2,1)}, bf16[128,2048]{1,0:T(8,128)(2,1)S(1)}, u32[]{:S(2)}, u32[]{:S(2)}) collective-permute-start(bf16[128,2048]{1,0:T(8,128)(2,1)} %collective-permute-done.1.refs_1_), channel_id=1, source_target_pairs={{0,2},{2,0},{4,6},{6,4},{8,10},{10,8},{12,14},{14,12},{16,18},{18,... | collective-permute-start | bytes 1572872 | tf_op jit(solution)/shard_map/ppermute | solution.py:264
  60.0 1.5 %collective-permute-start.7 = (bf16[128,2048]{1,0:T(8,128)(2,1)}, bf16[128,2048]{1,0:T(8,128)(2,1)S(1)}, u32[]{:S(2)}, u32[]{:S(2)}) collective-permute-start(bf16[128,2048]{1,0:T(8,128)(2,1)} %collective-permute-done.1.refs_1_), channel_id=1, source_target_pairs={{0,4},{2,6},{4,0},{6,2},{8,12},{10,14},{12,8},{14,10},{16,20},{18,... | collective-permute-start | bytes 1572872 | tf_op jit(solution)/shard_map/ppermute | solution.py:264
  61.5 0.7 slice.32
  62.2 0.5 collective-permute-start.10
  62.8 0.9 arrange.1.mine_ref
  63.8 14.4 %collective-permute-done.10.refs_10_ = bf16[64,2048]{1,0:T(8,128)(2,1)S(1)} collective-permute-done((bf16[64,2048]{1,0:T(8,128)(2,1)}, bf16[64,2048]{1,0:T(8,128)(2,1)S(1)}, u32[]{:S(2)}, u32[]{:S(2)}) %collective-permute-start.10) | collective-permute-done | bytes 262176 | tf_op jit(solution)/shard_map/ppermute | solution.py:264
  78.2 0.6 collective-permute-start.8
  78.8 1.7 %collective-permute-start.9 = (bf16[128,2048]{1,0:T(8,128)(2,1)}, bf16[128,2048]{1,0:T(8,128)(2,1)S(1)}, u32[]{:S(2)}, u32[]{:S(2)}) collective-permute-start(bf16[128,2048]{1,0:T(8,128)(2,1)} %collective-permute-done.2.refs_2_), channel_id=1, source_target_pairs={{0,4},{2,6},{4,0},{6,2},{8,12},{10,14},{12,8},{14,10},{16,20},{18,... | collective-permute-start | bytes 1572872 | tf_op jit(solution)/shard_map/ppermute | solution.py:264
  80.5 1.5 %collective-permute-start.12 = (bf16[128,2048]{1,0:T(8,128)(2,1)}, bf16[128,2048]{1,0:T(8,128)(2,1)S(1)}, u32[]{:S(2)}, u32[]{:S(2)}) collective-permute-start(bf16[128,2048]{1,0:T(8,128)(2,1)} %collective-permute-done.3.refs_3_), channel_id=1, source_target_pairs={{0,2},{2,0},{4,6},{6,4},{8,10},{10,8},{12,14},{14,12},{16,18},{18,... | collective-permute-start | bytes 1572872 | tf_op jit(solution)/shard_map/ppermute | solution.py:264
  82.0 0.3 collective-permute-start.13
  82.3 10.9 %collective-permute-done.8.refs_8_ = bf16[128,2048]{1,0:T(8,128)(2,1)S(1)} collective-permute-done((bf16[128,2048]{1,0:T(8,128)(2,1)}, bf16[128,2048]{1,0:T(8,128)(2,1)S(1)}, u32[]{:S(2)}, u32[]{:S(2)}) %collective-permute-start.8) | collective-permute-done | bytes 524320 | tf_op jit(solution)/shard_map/ppermute | solution.py:264
  93.2 0.6 collective-permute-start.11
  93.8 2.5 %collective-permute-start.14 = (bf16[64,2048]{1,0:T(8,128)(2,1)S(1)}, bf16[64,2048]{1,0:T(8,128)(2,1)S(1)}, u32[]{:S(2)}, u32[]{:S(2)}) collective-permute-start(bf16[64,2048]{1,0:T(8,128)(2,1)S(1)} %collective-permute-done.10.refs_10_), channel_id=1, source_target_pairs={{0,8},{2,10},{4,12},{6,14},{8,16},{10,18},{12,20},{14,22},{16,24},... | collective-permute-start | bytes 786440 | tf_op jit(solution)/shard_map/ppermute | solution.py:267
  96.3 7.7 %collective-permute-done.12.refs_12_ = bf16[128,2048]{1,0:T(8,128)(2,1)S(1)} collective-permute-done((bf16[128,2048]{1,0:T(8,128)(2,1)}, bf16[128,2048]{1,0:T(8,128)(2,1)S(1)}, u32[]{:S(2)}, u32[]{:S(2)}) %collective-permute-start.12) | collective-permute-done | bytes 524320 | tf_op jit(solution)/shard_map/ppermute | solution.py:264
  104.0 1.9 %collective-permute-start.15 = (bf16[32,2048]{1,0:T(8,128)(2,1)S(1)}, bf16[32,2048]{1,0:T(8,128)(2,1)S(1)}, u32[]{:S(2)}, u32[]{:S(2)}) collective-permute-start(bf16[32,2048]{1,0:T(8,128)(2,1)S(1)} %slice.34), channel_id=1, source_target_pairs={{0,4},{2,6},{4,0},{6,2},{8,12},{10,14},{12,8},{14,10},{16,20},{18,... | collective-permute-start | bytes 393224 | tf_op jit(solution)/shard_map/ppermute | solution.py:264
  105.9 2.5 %multiply_reduce_fusion.1 = f32[2048]{0:T(1024)S(1)} fusion(f32[512,2048]{1,0:T(8,128)} %weight_ref.1), kind=kLoop, calls=%fused_computation.1 | loop fusion | flops 2095104 | bytes 4202496 | tf_op jit(solution)/shard_map/reduce_sum | solution.py:302
  108.6 0.6 collective-permute-start.16
  109.2 0.4 collective-permute-start.18
  109.6 1.6 %collective-permute-done.17.refs_3_ = bf16[64,2048]{1,0:T(8,128)(2,1)S(1)} collective-permute-done((bf16[64,2048]{1,0:T(8,128)(2,1)S(1)}, bf16[64,2048]{1,0:T(8,128)(2,1)S(1)}, u32[]{:S(2)}, u32[]{:S(2)}) %collective-permute-start.17) | collective-permute-done | bytes 262176 | tf_op jit(solution)/shard_map/ppermute | solution.py:267
  111.3 0.6 collective-permute-start.19
  111.8 1.7 %collective-permute-start.20 = (bf16[64,2048]{1,0:T(8,128)(2,1)S(1)}, bf16[64,2048]{1,0:T(8,128)(2,1)S(1)}, u32[]{:S(2)}, u32[]{:S(2)}) collective-permute-start(bf16[64,2048]{1,0:T(8,128)(2,1)S(1)} %slice.38), channel_id=1, source_target_pairs={{0,4},{2,6},{4,0},{6,2},{8,12},{10,14},{12,8},{14,10},{16,20},{18,... | collective-permute-start | bytes 786440 | tf_op jit(solution)/shard_map/ppermute | solution.py:264
  113.6 1.5 %collective-permute-start.21 = (bf16[64,2048]{1,0:T(8,128)(2,1)S(1)}, bf16[64,2048]{1,0:T(8,128)(2,1)S(1)}, u32[]{:S(2)}, u32[]{:S(2)}) collective-permute-start(bf16[64,2048]{1,0:T(8,128)(2,1)S(1)} %slice.39), channel_id=1, source_target_pairs={{0,2},{2,0},{4,6},{6,4},{8,10},{10,8},{12,14},{14,12},{16,18},{18,... | collective-permute-start | bytes 786440 | tf_op jit(solution)/shard_map/ppermute | solution.py:264
  115.1 6.5 %gemm.1.before_ref = f32[512,2048]{1,0:T(8,128)S(1)} custom-call(s32[1]{0:T(128)} %bitcast.side_ref, bf16[256,2048]{1,0:T(8,128)(2,1)S(1)} %arrange.1.mine_ref, bf16[256,2048]{1,0:T(8,128)(2,1)S(1)} %collective-permute-done.other_ref, bf16[128,2048]{1,0:T(8,128)(2,1)} %refs_0_.1, bf16[128,2048]{1,0:T(8,128)(2,1)} %collective-permute-done.1.refs_1_, ...), custom_call_target="tpu_custom_call" | custom-call | flops 3489660928 | bytes 6815744 | tf_op jit(solution)/shard_map/gemm/pallas_call | solution.py:128
  121.6 1.5 %last_gemm.1 = (f32[512,2048]{1,0:T(8,128)S(1)}, f32[1,512]{1,0:T(1,128)S(1)}) custom-call(s32[1]{0:T(128)} %bitcast.side_ref, bf16[256,2048]{1,0:T(8,128)(2,1)S(1)} %arrange.1.mine_ref, bf16[256,2048]{1,0:T(8,128)(2,1)S(1)} %collective-permute-done.other_ref, f32[512,2048]{1,0:T(8,128)S(1)} %gemm.1.before_ref, ...), custom_call_target="tpu_custom_call" | custom-call | flops 805306368 | bytes 1572864 | tf_op jit(solution)/shard_map/last_gemm/pallas_call | solution.py:170
  123.2 1.1 collective-permute-done.22
  124.4 0.7 add_reduce_fusion
  125.2 0.6 collective-permute-start.23
  125.8 0.3 collective-permute-start.24
  126.1 2.6 %collective-permute-start.25 = (f32[2,2176]{1,0:T(2,128)S(1)}, f32[2,2176]{1,0:T(2,128)S(1)}, u32[]{:S(2)}, u32[]{:S(2)}) collective-permute-start(f32[2,2176]{1,0:T(2,128)S(1)} %pad_maximum_fusion), channel_id=1, source_target_pairs={{0,6},{2,4},{4,2},{6,0},{8,14},{10,12},{12,10},{14,8},{16,22},{18,... | collective-permute-start | bytes 52232 | tf_op jit(solution)/shard_map/ppermute | solution.py:27
  129.0 0.6 collective-permute-done.24
  129.6 1.2 collective-permute-done.25
  130.8 2.3 %collective-permute-start.26 = (f32[2,2176]{1,0:T(2,128)S(1)}, f32[2,2176]{1,0:T(2,128)S(1)}, u32[]{:S(2)}, u32[]{:S(2)}) collective-permute-start(f32[2,2176]{1,0:T(2,128)S(1)} %add_add_fusion.1), channel_id=1, source_target_pairs={{0,8},{2,10},{4,12},{6,14},{8,0},{10,2},{12,4},{14,6},{16,24},{18,... | collective-permute-start | bytes 52232 | tf_op jit(solution)/shard_map/ppermute | solution.py:27
  133.1 1.2 collective-permute-start.27
  134.3 1.4 collective-permute-start.28
  135.7 2.1 %collective-permute-done.27 = f32[2,2176]{1,0:T(2,128)S(1)} collective-permute-done((f32[2,2176]{1,0:T(2,128)S(1)}, f32[2,2176]{1,0:T(2,128)S(1)}, u32[]{:S(2)}, u32[]{:S(2)}) %collective-permute-start.27) | collective-permute-done | bytes 17440 | tf_op jit(solution)/shard_map/ppermute | solution.py:27
  137.8 2.1 %collective-permute-done.28 = f32[2,2176]{1,0:T(2,128)S(1)} collective-permute-done((f32[2,2176]{1,0:T(2,128)S(1)}, f32[2,2176]{1,0:T(2,128)S(1)}, u32[]{:S(2)}, u32[]{:S(2)}) %collective-permute-start.28) | collective-permute-done | bytes 17440 | tf_op jit(solution)/shard_map/ppermute | solution.py:27
  140.2 0.6 copy.11
  140.8 0.6 collective-permute-done.29
  141.3 3.6 %finish.1 = (f32[512,2048]{1,0:T(8,128)}, f32[512,2048]{1,0:T(8,128)}) custom-call(f32[8,128]{1,0:T(8,128)S(1)} %add.74.sums_ref, f32[1,512]{1,0:T(1,128)S(1)} %bitcast.8, f32[1,2048]{1,0:T(1,128)S(1)} %get-tuple-element.13.col_ref, f32[512,2048]{1,0:T(8,128)S(1)} %get-tuple-element.10.gradient_ref, f32[512,2048]{1,0:T(8,128)S(1)} %copy-done), custom_call_target="tpu_custom_call" | custom-call | flops 4194304 | bytes 16777216 | tf_op jit(solution)/shard_map/finish/pallas_call | solution.py:233
  (72 shorter events, 1.0 us)
Async XLA Ops:
  0.6 62.1 %copy-start.13 = (s32[16]{0:T(128)S(1)}, s32[16]{0:T(128)}, u32[]{:S(2)}) copy-start(s32[16]{0:T(128)} %constant.65.clone) | copy-start | bytes 196
  0.6 62.1 %copy-start.14 = (s32[16]{0:T(128)S(1)}, s32[16]{0:T(128)}, u32[]{:S(2)}) copy-start(s32[16]{0:T(128)} %constant.66.clone) | copy-start | bytes 196
  0.7 1.6 %copy-start.1 = (bf16[128,8192]{1,0:T(8,128)(2,1)S(1)}, bf16[128,8192]{1,0:T(8,128)(2,1)}, u32[]{:S(2)}) copy-start(bf16[128,8192]{1,0:T(8,128)(2,1)} %acts_ref.1) | copy-start | bytes 6291460
  3.3 59.4 %all-to-all-start = ((bf16[16,128,256]{2,1,0:T(8,128)(2,1)}), bf16[16,128,256]{2,1,0:T(8,128)(2,1)S(1)}, u32[]{:S(2)}, u32[]{:S(2)}) async-start(bf16[16,128,256]{2,1,0:T(8,128)(2,1)} %pack.1), calls=%async_computation | async-start | bytes 2097152 | tf_op jit(solution)/shard_map/all_to_all | solution.py:287
  11.7 33.7 %collective-permute-start.1 = (bf16[128,2048]{1,0:T(8,128)(2,1)}, bf16[128,2048]{1,0:T(8,128)(2,1)}, u32[]{:S(2)}, u32[]{:S(2)}) collective-permute-start(bf16[128,2048]{1,0:T(8,128)(2,1)} %refs_0_.1), channel_id=1, source_target_pairs={{0,8},{2,10},{4,12},{6,14},{8,16},{10,18},{12,20},{14,22},{16,24},... | collective-permute-start | bytes 1572872 | tf_op jit(solution)/shard_map/ppermute | solution.py:267
  13.6 46.4 %collective-permute-start.4 = (bf16[128,2048]{1,0:T(8,128)(2,1)}, bf16[128,2048]{1,0:T(8,128)(2,1)S(1)}, u32[]{:S(2)}, u32[]{:S(2)}) collective-permute-start(bf16[128,2048]{1,0:T(8,128)(2,1)} %refs_0_.1), channel_id=1, source_target_pairs={{0,2},{2,0},{4,6},{6,4},{8,10},{10,8},{12,14},{14,12},{16,18},{18,... | collective-permute-start | bytes 1572872 | tf_op jit(solution)/shard_map/ppermute | solution.py:264
  15.1 47.2 %collective-permute-start.2 = (bf16[128,2048]{1,0:T(8,128)(2,1)}, bf16[128,2048]{1,0:T(8,128)(2,1)}, u32[]{:S(2)}, u32[]{:S(2)}) collective-permute-start(bf16[128,2048]{1,0:T(8,128)(2,1)} %refs_0_.1), channel_id=1, source_target_pairs={{0,24},{2,26},{4,28},{6,30},{8,0},{10,2},{12,4},{14,6},{16,8},{18,... | collective-permute-start | bytes 1572872 | tf_op jit(solution)/shard_map/ppermute | solution.py:267
  17.4 46.3 %collective-permute-start.5 = (bf16[128,2048]{1,0:T(8,128)(2,1)}, bf16[128,2048]{1,0:T(8,128)(2,1)S(1)}, u32[]{:S(2)}, u32[]{:S(2)}) collective-permute-start(bf16[128,2048]{1,0:T(8,128)(2,1)} %refs_0_.1), channel_id=1, source_target_pairs={{0,4},{2,6},{4,0},{6,2},{8,12},{10,14},{12,8},{14,10},{16,20},{18,... | collective-permute-start | bytes 1572872 | tf_op jit(solution)/shard_map/ppermute | solution.py:264
  45.3 33.4 %collective-permute-start.3 = (bf16[128,2048]{1,0:T(8,128)(2,1)}, bf16[128,2048]{1,0:T(8,128)(2,1)}, u32[]{:S(2)}, u32[]{:S(2)}) collective-permute-start(bf16[128,2048]{1,0:T(8,128)(2,1)} %collective-permute-done.1.refs_1_), channel_id=1, source_target_pairs={{0,8},{2,10},{4,12},{6,14},{8,16},{10,18},{12,20},{14,22},{16,24},... | collective-permute-start | bytes 1572872 | tf_op jit(solution)/shard_map/ppermute | solution.py:267
  58.5 22.0 %collective-permute-start.6 = (bf16[128,2048]{1,0:T(8,128)(2,1)}, bf16[128,2048]{1,0:T(8,128)(2,1)S(1)}, u32[]{:S(2)}, u32[]{:S(2)}) collective-permute-start(bf16[128,2048]{1,0:T(8,128)(2,1)} %collective-permute-done.1.refs_1_), channel_id=1, source_target_pairs={{0,2},{2,0},{4,6},{6,4},{8,10},{10,8},{12,14},{14,12},{16,18},{18,... | collective-permute-start | bytes 1572872 | tf_op jit(solution)/shard_map/ppermute | solution.py:264
  60.0 48.5 %copy-start.4 = (bf16[128,2048]{1,0:T(8,128)(2,1)}, bf16[128,2048]{1,0:T(8,128)(2,1)S(1)}, u32[]{:S(2)}) copy-start(bf16[128,2048]{1,0:T(8,128)(2,1)S(1)} %collective-permute-done.4.refs_4_) | copy-start | bytes 1572868
  60.0 22.0 %collective-permute-start.7 = (bf16[128,2048]{1,0:T(8,128)(2,1)}, bf16[128,2048]{1,0:T(8,128)(2,1)S(1)}, u32[]{:S(2)}, u32[]{:S(2)}) collective-permute-start(bf16[128,2048]{1,0:T(8,128)(2,1)} %collective-permute-done.1.refs_1_), channel_id=1, source_target_pairs={{0,4},{2,6},{4,0},{6,2},{8,12},{10,14},{12,8},{14,10},{16,20},{18,... | collective-permute-start | bytes 1572872 | tf_op jit(solution)/shard_map/ppermute | solution.py:264
  62.2 16.0 %collective-permute-start.10 = (bf16[64,2048]{1,0:T(8,128)(2,1)}, bf16[64,2048]{1,0:T(8,128)(2,1)S(1)}, u32[]{:S(2)}, u32[]{:S(2)}) collective-permute-start(bf16[64,2048]{1,0:T(8,128)(2,1)} %slice.32), channel_id=1, source_target_pairs={{0,4},{2,6},{4,0},{6,2},{8,12},{10,14},{12,8},{14,10},{16,20},{18,... | collective-permute-start | bytes 786440 | tf_op jit(solution)/shard_map/ppermute | solution.py:264
  63.7 51.3 %copy-start.5 = (bf16[128,2048]{1,0:T(8,128)(2,1)}, bf16[128,2048]{1,0:T(8,128)(2,1)S(1)}, u32[]{:S(2)}) copy-start(bf16[128,2048]{1,0:T(8,128)(2,1)S(1)} %collective-permute-done.5.refs_5_) | copy-start | bytes 1572868
  63.7 49.9 %collective-permute-start = (bf16[256,2048]{1,0:T(8,128)(2,1)S(1)}, bf16[256,2048]{1,0:T(8,128)(2,1)S(1)}, u32[]{:S(2)}, u32[]{:S(2)}) collective-permute-start(bf16[256,2048]{1,0:T(8,128)(2,1)S(1)} %arrange.1.mine_ref), channel_id=1, source_target_pairs={{0,1},{1,0},{2,3},{3,2},{4,5},{5,4},{6,7},{7,6},{8,9},{9,8},{10,11... | collective-permute-start | bytes 3145736 | tf_op jit(solution)/shard_map/ppermute | solution.py:294
  78.2 36.8 %copy-start.10 = (bf16[64,2048]{1,0:T(8,128)(2,1)}, bf16[64,2048]{1,0:T(8,128)(2,1)S(1)}, u32[]{:S(2)}) copy-start(bf16[64,2048]{1,0:T(8,128)(2,1)S(1)} %collective-permute-done.10.refs_10_) | copy-start | bytes 786436
  78.2 15.0 %collective-permute-start.8 = (bf16[128,2048]{1,0:T(8,128)(2,1)}, bf16[128,2048]{1,0:T(8,128)(2,1)S(1)}, u32[]{:S(2)}, u32[]{:S(2)}) collective-permute-start(bf16[128,2048]{1,0:T(8,128)(2,1)} %collective-permute-done.2.refs_2_), channel_id=1, source_target_pairs={{0,2},{2,0},{4,6},{6,4},{8,10},{10,8},{12,14},{14,12},{16,18},{18,... | collective-permute-start | bytes 1572872 | tf_op jit(solution)/shard_map/ppermute | solution.py:264
  78.8 15.0 %collective-permute-start.9 = (bf16[128,2048]{1,0:T(8,128)(2,1)}, bf16[128,2048]{1,0:T(8,128)(2,1)S(1)}, u32[]{:S(2)}, u32[]{:S(2)}) collective-permute-start(bf16[128,2048]{1,0:T(8,128)(2,1)} %collective-permute-done.2.refs_2_), channel_id=1, source_target_pairs={{0,4},{2,6},{4,0},{6,2},{8,12},{10,14},{12,8},{14,10},{16,20},{18,... | collective-permute-start | bytes 1572872 | tf_op jit(solution)/shard_map/ppermute | solution.py:264
  80.5 34.5 %copy-start.6 = (bf16[128,2048]{1,0:T(8,128)(2,1)}, bf16[128,2048]{1,0:T(8,128)(2,1)S(1)}, u32[]{:S(2)}) copy-start(bf16[128,2048]{1,0:T(8,128)(2,1)S(1)} %collective-permute-done.6.refs_6_) | copy-start | bytes 1572868
  80.5 23.5 %collective-permute-start.12 = (bf16[128,2048]{1,0:T(8,128)(2,1)}, bf16[128,2048]{1,0:T(8,128)(2,1)S(1)}, u32[]{:S(2)}, u32[]{:S(2)}) collective-permute-start(bf16[128,2048]{1,0:T(8,128)(2,1)} %collective-permute-done.3.refs_3_), channel_id=1, source_target_pairs={{0,2},{2,0},{4,6},{6,4},{8,10},{10,8},{12,14},{14,12},{16,18},{18,... | collective-permute-start | bytes 1572872 | tf_op jit(solution)/shard_map/ppermute | solution.py:264
  82.0 33.1 %copy-start.7 = (bf16[128,2048]{1,0:T(8,128)(2,1)}, bf16[128,2048]{1,0:T(8,128)(2,1)S(1)}, u32[]{:S(2)}) copy-start(bf16[128,2048]{1,0:T(8,128)(2,1)S(1)} %collective-permute-done.7.refs_7_) | copy-start | bytes 1572868
  82.0 22.0 %collective-permute-start.13 = (bf16[128,2048]{1,0:T(8,128)(2,1)}, bf16[128,2048]{1,0:T(8,128)(2,1)S(1)}, u32[]{:S(2)}, u32[]{:S(2)}) collective-permute-start(bf16[128,2048]{1,0:T(8,128)(2,1)} %collective-permute-done.3.refs_3_), channel_id=1, source_target_pairs={{0,4},{2,6},{4,0},{6,2},{8,12},{10,14},{12,8},{14,10},{16,20},{18,... | collective-permute-start | bytes 1572872 | tf_op jit(solution)/shard_map/ppermute | solution.py:264
  93.2 21.8 %copy-start.8 = (bf16[128,2048]{1,0:T(8,128)(2,1)}, bf16[128,2048]{1,0:T(8,128)(2,1)S(1)}, u32[]{:S(2)}) copy-start(bf16[128,2048]{1,0:T(8,128)(2,1)S(1)} %collective-permute-done.8.refs_8_) | copy-start | bytes 1572868
  93.2 15.4 %collective-permute-start.11 = (bf16[64,2048]{1,0:T(8,128)(2,1)S(1)}, bf16[64,2048]{1,0:T(8,128)(2,1)S(1)}, u32[]{:S(2)}, u32[]{:S(2)}) collective-permute-start(bf16[64,2048]{1,0:T(8,128)(2,1)S(1)} %slice.33), channel_id=1, source_target_pairs={{0,2},{2,0},{4,6},{6,4},{8,10},{10,8},{12,14},{14,12},{16,18},{18,... | collective-permute-start | bytes 786440 | tf_op jit(solution)/shard_map/ppermute | solution.py:264
  93.8 21.3 %copy-start.9 = (bf16[128,2048]{1,0:T(8,128)(2,1)}, bf16[128,2048]{1,0:T(8,128)(2,1)S(1)}, u32[]{:S(2)}) copy-start(bf16[128,2048]{1,0:T(8,128)(2,1)S(1)} %collective-permute-done.9.refs_9_) | copy-start | bytes 1572868
  93.8 15.4 %collective-permute-start.14 = (bf16[64,2048]{1,0:T(8,128)(2,1)S(1)}, bf16[64,2048]{1,0:T(8,128)(2,1)S(1)}, u32[]{:S(2)}, u32[]{:S(2)}) collective-permute-start(bf16[64,2048]{1,0:T(8,128)(2,1)S(1)} %collective-permute-done.10.refs_10_), channel_id=1, source_target_pairs={{0,8},{2,10},{4,12},{6,14},{8,16},{10,18},{12,20},{14,22},{16,24},... | collective-permute-start | bytes 786440 | tf_op jit(solution)/shard_map/ppermute | solution.py:267
  104.0 7.3 %collective-permute-start.17 = (bf16[64,2048]{1,0:T(8,128)(2,1)S(1)}, bf16[64,2048]{1,0:T(8,128)(2,1)S(1)}, u32[]{:S(2)}, u32[]{:S(2)}) collective-permute-start(bf16[64,2048]{1,0:T(8,128)(2,1)S(1)} %collective-permute-done.10.refs_10_), channel_id=1, source_target_pairs={{0,24},{2,26},{4,28},{6,30},{8,0},{10,2},{12,4},{14,6},{16,8},{18,... | collective-permute-start | bytes 786440 | tf_op jit(solution)/shard_map/ppermute | solution.py:267
  104.0 7.9 %collective-permute-start.15 = (bf16[32,2048]{1,0:T(8,128)(2,1)S(1)}, bf16[32,2048]{1,0:T(8,128)(2,1)S(1)}, u32[]{:S(2)}, u32[]{:S(2)}) collective-permute-start(bf16[32,2048]{1,0:T(8,128)(2,1)S(1)} %slice.34), channel_id=1, source_target_pairs={{0,4},{2,6},{4,0},{6,2},{8,12},{10,14},{12,8},{14,10},{16,20},{18,... | collective-permute-start | bytes 393224 | tf_op jit(solution)/shard_map/ppermute | solution.py:264
  108.6 6.5 %copy-start.11 = (bf16[64,2048]{1,0:T(8,128)(2,1)}, bf16[64,2048]{1,0:T(8,128)(2,1)S(1)}, u32[]{:S(2)}) copy-start(bf16[64,2048]{1,0:T(8,128)(2,1)S(1)} %collective-permute-done.11.refs_11_) | copy-start | bytes 786436
  108.6 13.0 %collective-permute-start.16 = (bf16[32,2048]{1,0:T(8,128)(2,1)S(1)}, bf16[32,2048]{1,0:T(8,128)(2,1)S(1)}, u32[]{:S(2)}, u32[]{:S(2)}) collective-permute-start(bf16[32,2048]{1,0:T(8,128)(2,1)S(1)} %slice.35), channel_id=1, source_target_pairs={{0,2},{2,0},{4,6},{6,4},{8,10},{10,8},{12,14},{14,12},{16,18},{18,... | collective-permute-start | bytes 393224 | tf_op jit(solution)/shard_map/ppermute | solution.py:264
  109.2 12.4 %collective-permute-start.18 = (bf16[32,2048]{1,0:T(8,128)(2,1)S(1)}, bf16[32,2048]{1,0:T(8,128)(2,1)S(1)}, u32[]{:S(2)}, u32[]{:S(2)}) collective-permute-start(bf16[32,2048]{1,0:T(8,128)(2,1)S(1)} %slice.36), channel_id=1, source_target_pairs={{0,4},{2,6},{4,0},{6,2},{8,12},{10,14},{12,8},{14,10},{16,20},{18,... | collective-permute-start | bytes 393224 | tf_op jit(solution)/shard_map/ppermute | solution.py:264
  111.3 10.3 %collective-permute-start.19 = (bf16[32,2048]{1,0:T(8,128)(2,1)S(1)}, bf16[32,2048]{1,0:T(8,128)(2,1)S(1)}, u32[]{:S(2)}, u32[]{:S(2)}) collective-permute-start(bf16[32,2048]{1,0:T(8,128)(2,1)S(1)} %slice.37), channel_id=1, source_target_pairs={{0,2},{2,0},{4,6},{6,4},{8,10},{10,8},{12,14},{14,12},{16,18},{18,... | collective-permute-start | bytes 393224 | tf_op jit(solution)/shard_map/ppermute | solution.py:264
  111.8 9.8 %collective-permute-start.20 = (bf16[64,2048]{1,0:T(8,128)(2,1)S(1)}, bf16[64,2048]{1,0:T(8,128)(2,1)S(1)}, u32[]{:S(2)}, u32[]{:S(2)}) collective-permute-start(bf16[64,2048]{1,0:T(8,128)(2,1)S(1)} %slice.38), channel_id=1, source_target_pairs={{0,4},{2,6},{4,0},{6,2},{8,12},{10,14},{12,8},{14,10},{16,20},{18,... | collective-permute-start | bytes 786440 | tf_op jit(solution)/shard_map/ppermute | solution.py:264
  113.6 8.1 %collective-permute-start.21 = (bf16[64,2048]{1,0:T(8,128)(2,1)S(1)}, bf16[64,2048]{1,0:T(8,128)(2,1)S(1)}, u32[]{:S(2)}, u32[]{:S(2)}) collective-permute-start(bf16[64,2048]{1,0:T(8,128)(2,1)S(1)} %slice.39), channel_id=1, source_target_pairs={{0,2},{2,0},{4,6},{6,4},{8,10},{10,8},{12,14},{14,12},{16,18},{18,... | collective-permute-start | bytes 786440 | tf_op jit(solution)/shard_map/ppermute | solution.py:264
  121.6 2.8 %copy-start.12 = (f32[512]{0:T(512)S(1)}, f32[512]{0:T(512)}, u32[]{:S(2)}) copy-start(f32[512]{0:T(512)} %param.10) | copy-start | bytes 6148
  123.1 16.8 %copy-start.3 = (f32[2048]{0:T(1024)S(1)}, f32[2048]{0:T(1024)}, u32[]{:S(2)}) copy-start(f32[2048]{0:T(1024)} %param.11) | copy-start | bytes 24580
  123.1 18.2 %copy-start = (f32[512,2048]{1,0:T(8,128)S(1)}, f32[512,2048]{1,0:T(8,128)}, u32[]{:S(2)}) copy-start(f32[512,2048]{1,0:T(8,128)} %weight_ref.1) | copy-start | bytes 12582916
  123.1 1.2 collective-permute-start.22
  124.4 20.6 %copy-start.2 = (f32[512]{0:T(512)}, f32[512]{0:T(512)S(1)}, u32[]{:S(2)}) copy-start(f32[512]{0:T(512)S(1)} %get-tuple-element.22) | copy-start | bytes 6148
  125.2 3.8 %collective-permute-start.23 = (f32[2,2176]{1,0:T(2,128)S(1)}, f32[2,2176]{1,0:T(2,128)S(1)}, u32[]{:S(2)}, u32[]{:S(2)}) collective-permute-start(f32[2,2176]{1,0:T(2,128)S(1)} %pad_maximum_fusion), channel_id=1, source_target_pairs={{0,2},{2,0},{4,6},{6,4},{8,10},{10,8},{12,14},{14,12},{16,18},{18,... | collective-permute-start | bytes 52232 | tf_op jit(solution)/shard_map/ppermute | solution.py:27
  125.8 3.8 %collective-permute-start.24 = (f32[2,2176]{1,0:T(2,128)S(1)}, f32[2,2176]{1,0:T(2,128)S(1)}, u32[]{:S(2)}, u32[]{:S(2)}) collective-permute-start(f32[2,2176]{1,0:T(2,128)S(1)} %pad_maximum_fusion), channel_id=1, source_target_pairs={{0,4},{2,6},{4,0},{6,2},{8,12},{10,14},{12,8},{14,10},{16,20},{18,... | collective-permute-start | bytes 52232 | tf_op jit(solution)/shard_map/ppermute | solution.py:27
  126.1 4.6 %collective-permute-start.25 = (f32[2,2176]{1,0:T(2,128)S(1)}, f32[2,2176]{1,0:T(2,128)S(1)}, u32[]{:S(2)}, u32[]{:S(2)}) collective-permute-start(f32[2,2176]{1,0:T(2,128)S(1)} %pad_maximum_fusion), channel_id=1, source_target_pairs={{0,6},{2,4},{4,2},{6,0},{8,14},{10,12},{12,10},{14,8},{16,22},{18,... | collective-permute-start | bytes 52232 | tf_op jit(solution)/shard_map/ppermute | solution.py:27
  130.8 4.9 %collective-permute-start.26 = (f32[2,2176]{1,0:T(2,128)S(1)}, f32[2,2176]{1,0:T(2,128)S(1)}, u32[]{:S(2)}, u32[]{:S(2)}) collective-permute-start(f32[2,2176]{1,0:T(2,128)S(1)} %add_add_fusion.1), channel_id=1, source_target_pairs={{0,8},{2,10},{4,12},{6,14},{8,0},{10,2},{12,4},{14,6},{16,24},{18,... | collective-permute-start | bytes 52232 | tf_op jit(solution)/shard_map/ppermute | solution.py:27
  133.1 4.7 %collective-permute-start.27 = (f32[2,2176]{1,0:T(2,128)S(1)}, f32[2,2176]{1,0:T(2,128)S(1)}, u32[]{:S(2)}, u32[]{:S(2)}) collective-permute-start(f32[2,2176]{1,0:T(2,128)S(1)} %add_add_fusion.1), channel_id=1, source_target_pairs={{0,16},{2,18},{4,20},{6,22},{8,24},{10,26},{12,28},{14,30},{16,0},... | collective-permute-start | bytes 52232 | tf_op jit(solution)/shard_map/ppermute | solution.py:27
  134.3 5.5 %collective-permute-start.28 = (f32[2,2176]{1,0:T(2,128)S(1)}, f32[2,2176]{1,0:T(2,128)S(1)}, u32[]{:S(2)}, u32[]{:S(2)}) collective-permute-start(f32[2,2176]{1,0:T(2,128)S(1)} %add_add_fusion.1), channel_id=1, source_target_pairs={{0,24},{2,26},{4,28},{6,30},{8,16},{10,18},{12,20},{14,22},{16,8},... | collective-permute-start | bytes 52232 | tf_op jit(solution)/shard_map/ppermute | solution.py:27
  140.1 1.2 collective-permute-start.29
